TPU v7x, 1024 devices: a whole 4x8x16 slice. The times are simulated.
1024 devices in a mesh: section: 8 (over y), dp: 32 (over z, core), tensor: 4 (over x).
Axes of the slice: x: 4, y: 8, z: 16, core: 2. Of those that a mesh axis runs over, the one named last changes fastest.
Arguments:
- out_grad: bfloat16 [4096, 4096], P('dp', 'tensor'), may hold values from -6 to 6
- section_out: bfloat16 [8, 4096, 4096], P('section', 'dp', 'tensor'), may hold values from -6 to 6
- context: bfloat16 [8, 4096, 2048], P('section', 'dp', 'tensor'), may hold values from -6 to 6
- queries: bfloat16 [8, 4096, 2048], P('section', 'dp', 'tensor')
- key_heads: bfloat16 [8, 4096, 2048], P('section', 'dp', 'tensor')
- values: bfloat16 [8, 4096, 2048], P('section', 'dp', 'tensor'), may hold values from -6 to 6
- o_weight: bfloat16 [8, 4096, 2048], P('section', None, 'tensor'), may hold values from -0.125 to 0.125
- doc_lengths: int32 [32], replicated, may hold values from 1 to 256, 4096 in all
Outputs:
- query_grad: bfloat16 [8, 4096, 2048], P('section', 'dp', 'tensor')
- key_grad: bfloat16 [8, 4096, 2048], P('section', 'dp', 'tensor')
- value_grad: bfloat16 [8, 4096, 2048], P('section', 'dp', 'tensor')
- o_weight_grad: float32 [8, 4096, 2048], P('section', 'dp', 'tensor')
Inputs may be any that keep to these rules, and one draw needn't show every extreme that they name: `doc_lengths`: the lengths sum to 4096, and the longest document has exactly 256 patches.
All inputs are finite; a program needn't handle non-finite values.
Results may differ from a plain program's by a relative error of at most 0.023.
Values may be sent and summed in bfloat16 or wider, within the bound.
No kernel may reach another device: no remote copies, remote signals or barrier semaphores. Data moves between devices by JAX's collectives and lax.ppermute only.
A program may use at most 32 MiB of HBM per device.

v0:
```python
import jax
import jax.numpy as jnp
from jax import lax
from jax.sharding import PartitionSpec as P

HD = 128
REACH = 2


def entering(value, axis, combine, identity):
    count, position = (lax.axis_size(axis), lax.axis_index(axis))
    everything = lax.all_gather(value.astype(jnp.bfloat16), axis)
    start = jnp.broadcast_to(jnp.asarray(identity, value.dtype), value.shape)

    def hop(k, before):
        at = count - 1 - k
        reached = at > position
        new = combine(before, everything[at].astype(value.dtype))
        return jnp.where(reached, new, before)

    return lax.fori_loop(0, count, hop, start)


def passed_along(value, axis, steps):
    count = lax.axis_size(axis)
    leading, last = (max(0, -steps), min(count, count - steps))
    return lax.ppermute(value, axis, [(source, source + steps) for source in range(leading, last)])


def add_pair(earlier, later):
    return earlier + later


def document_of(positions, ends):
    return jnp.sum((positions[:, None] >= ends[None, :]).astype(jnp.int32), axis=-1)


def on_device(out_grad, section_out, context, queries, key_heads, values, o_weight, doc_lengths):
    rows, width = (queries.shape[1], queries.shape[2])
    head_count = width // HD
    scaling = HD ** (-0.5)
    own_out = section_out[0].astype(jnp.float32)
    above = entering(own_out, "section", add_pair, jnp.zeros_like(own_out))
    grad_local = (out_grad.astype(jnp.float32) + 0.25 * (above + own_out)).astype(jnp.bfloat16)
    grad_full = lax.all_gather(grad_local, "tensor", axis=1, tiled=True)
    d_context = jnp.dot(grad_full, o_weight[0], preferred_element_type=jnp.float32).astype(
        jnp.bfloat16
    )
    three = (rows, head_count, HD)
    query_b = queries[0].reshape(three)
    dctx_b = d_context.reshape(three)
    ctx_flat = context[0]
    ends = jnp.cumsum(doc_lengths)
    first = lax.axis_index("dp") * rows
    own_place = first + jnp.arange(rows, dtype=jnp.int32)
    own_docs = document_of(own_place, ends)
    key_list = []
    value_list = []
    for step in range(REACH, 0, -1):
        moved = passed_along((key_heads[0], values[0]), "dp", step)
        key_list.append(moved[0])
        value_list.append(moved[1])
    window = (REACH + 1) * rows
    key_win = jnp.concatenate(key_list + [key_heads[0]], 0).reshape(window, head_count, HD)
    value_win = jnp.concatenate(value_list + [values[0]], 0).reshape(window, head_count, HD)
    window_place = first - REACH * rows + jnp.arange(window, dtype=jnp.int32)
    window_docs = document_of(window_place, ends)
    allowed = (
        (own_docs[:, None] == window_docs[None, :])
        & (window_place[None, :] <= own_place[:, None])
        & (window_place[None, :] >= 0)
    )
    scores = (
        jnp.einsum("ihd,jhd->hij", query_b, key_win, preferred_element_type=jnp.float32) * scaling
    )
    scores = jnp.where(allowed[None], scores, -jnp.inf)
    prob = jax.nn.softmax(scores, axis=-1)
    prob_b = prob.astype(jnp.bfloat16)
    d_prob = jnp.einsum("ihd,jhd->hij", dctx_b, value_win, preferred_element_type=jnp.float32)
    delta = jnp.transpose(
        jnp.sum(dctx_b.astype(jnp.float32) * ctx_flat.reshape(three).astype(jnp.float32), axis=-1)
    )
    d_score = (prob * (d_prob - delta[..., None]) * scaling).astype(jnp.bfloat16)
    query_grad = jnp.einsum(
        "hij,jhd->ihd", d_score, key_win, preferred_element_type=jnp.float32
    ).astype(jnp.bfloat16)
    key_part = jnp.einsum("hij,ihd->jhd", d_score, query_b, preferred_element_type=jnp.float32)
    value_part = jnp.einsum("hij,ihd->jhd", prob_b, dctx_b, preferred_element_type=jnp.float32)
    key_sum = key_part[REACH * rows :]
    value_sum = value_part[REACH * rows :]
    for step in range(1, REACH + 1):
        lower = (REACH - step) * rows
        returned = (
            passed_along(key_part[lower : lower + rows].astype(jnp.bfloat16), "dp", -step).astype(
                jnp.float32
            ),
            passed_along(value_part[lower : lower + rows].astype(jnp.bfloat16), "dp", -step).astype(
                jnp.float32
            ),
        )
        key_sum = key_sum + returned[0]
        value_sum = value_sum + returned[1]
    weight_grad = lax.psum_scatter(
        lax.dot_general(
            grad_full, ctx_flat, (((0,), (0,)), ((), ())), preferred_element_type=jnp.float32
        ).astype(jnp.bfloat16),
        "dp",
        scatter_dimension=0,
        tiled=True,
    ).astype(jnp.float32)
    shape_out = (1, rows, width)
    return (
        query_grad.reshape(shape_out),
        key_sum.astype(jnp.bfloat16).reshape(shape_out),
        value_sum.astype(jnp.bfloat16).reshape(shape_out),
        weight_grad[None],
    )


def solution(mesh):
    placed = (
        P("dp", "tensor"),
        P("section", "dp", "tensor"),
        P("section", "dp", "tensor"),
        P("section", "dp", "tensor"),
        P("section", "dp", "tensor"),
        P("section", "dp", "tensor"),
        P("section", None, "tensor"),
        P(),
    )
    return jax.shard_map(
        on_device,
        mesh=mesh,
        in_specs=placed,
        out_specs=(
            P("section", "dp", "tensor"),
            P("section", "dp", "tensor"),
            P("section", "dp", "tensor"),
            P("section", "dp", "tensor"),
        ),
        check_vma=False,
    )
```

profile of v0, /device:TPU:1, one launch (start us, length us, event | category | flops | bytes accessed | tf_op | source)
XLA Modules:
  0.0 242.8 jit_solution(11140570486631791185)
XLA Ops:
  8.0 55.8 %all-gather.3.cloned.1.call-done = bf16[8,128,1024]{2,1,0:T(8,128)(2,1)} async-done(((bf16[1,128,1024]{2,1,0:T(8,128)(2,1)}), bf16[8,128,1024]{2,1,0:T(8,128)(2,1)}) %all-gather.3.cloned.1.call-update) | async-done | bytes 2097168 | tf_op jit(solution)/shard_map/all_gather | solution.py:12
  63.8 10.1 %while.16 = (s32[]{:T(128)}, f32[128,1024]{1,0:T(8,128)S(1)}, s32[]{:T(128)}, bf16[8,128,1024]{2,1,0:T(8,128)(2,1)}, s32[]{:T(128)}, /*index=5*/s32[]{:T(128)}, s32[]{:T(128)}, s32[]{:T(128)}) while((s32[]{:T(128)}, f32[128,1024]{1,0:T(8,128)S(1)}, s32[]{:T(128)}, bf16[8,128,1024]{2,1,0:T(8,128)(2,1)}, s32[]{:T(128)}, ...), condition=%wide.region_6.7_spmd.clone, body=%wide.region_5.6_spmd.clone.sunk | while | flops 524296 | bytes 1310883 | solution.py:21
  63.8 1.2 add_select_fusion.2
  65.0 1.2 add_select_fusion.2
  66.3 1.2 add_select_fusion.2
  67.5 1.2 add_select_fusion.2
  68.8 1.2 add_select_fusion.2
  70.1 1.2 add_select_fusion.2
  71.3 1.2 add_select_fusion.2
  72.6 1.2 add_select_fusion.2
  73.8 0.8 fusion.15
  74.7 35.9 %all-gather.5.cloned.1.call-done = bf16[128,4096]{1,0:T(8,128)(2,1)} async-done(((bf16[128,1024]{1,0:T(8,128)(2,1)}), bf16[128,4096]{1,0:T(8,128)(2,1)}) %all-gather.5.cloned.1.call-update) | async-done | bytes 1048592 | tf_op jit(solution)/shard_map/all_gather | solution.py:45
  110.7 4.4 %convolution_convert_fusion = bf16[4096,512]{1,0:T(8,128)(2,1)} fusion(bf16[128,4096]{1,0:T(8,128)(2,1)} %all-gather.5.cloned.1.call-done, bf16[1,128,512]{2,1,0:T(8,128)(2,1)S(1)} %copy-done.2), kind=kOutput, calls=%fused_computation.2 | convolution fusion | flops 538968064 | bytes 5373952 | tf_op jit(solution)/shard_map/dot_general | solution.py:104
  115.1 0.9 copy-done.4
  116.1 6.0 %collective-permute-start.3 = (bf16[128,512]{0,1:T(8,128)(2,1)S(1)}, bf16[128,512]{0,1:T(8,128)(2,1)S(1)}, u32[]{:S(2)}, u32[]{:S(2)}) collective-permute-start(bf16[128,512]{0,1:T(8,128)(2,1)S(1)} %bitcast.62), channel_id=1, source_target_pairs={{0,4},{4,8},{8,12},{12,16},{16,20},{20,24},{24,28},{28,32},{32,36}... | collective-permute-start | bytes 393224 | tf_op jit(solution)/shard_map/ppermute | solution.py:27
  122.2 3.3 %collective-permute-start.2 = (bf16[128,512]{0,1:T(8,128)(2,1)S(1)}, bf16[128,512]{0,1:T(8,128)(2,1)S(1)}, u32[]{:S(2)}, u32[]{:S(2)}) collective-permute-start(bf16[128,512]{0,1:T(8,128)(2,1)S(1)} %bitcast.63), channel_id=1, source_target_pairs={{0,8},{4,12},{8,16},{12,20},{16,24},{20,28},{24,32},{28,36},{32,40... | collective-permute-start | bytes 393224 | tf_op jit(solution)/shard_map/ppermute | solution.py:27
  125.6 2.2 collective-permute-start.1
  127.8 3.3 %collective-permute-start = (bf16[128,512]{0,1:T(8,128)(2,1)S(1)}, bf16[128,512]{0,1:T(8,128)(2,1)S(1)}, u32[]{:S(2)}, u32[]{:S(2)}) collective-permute-start(bf16[128,512]{0,1:T(8,128)(2,1)S(1)} %bitcast.60), channel_id=1, source_target_pairs={{0,8},{4,12},{8,16},{12,20},{16,24},{20,28},{24,32},{28,36},{32,40... | collective-permute-start | bytes 393224 | tf_op jit(solution)/shard_map/ppermute | solution.py:27
  132.8 0.9 collective-permute-done
  134.1 1.3 fusion.37
  135.4 2.9 %fusion.10 = bf16[128,512]{1,0:T(8,128)(2,1)S(1)} fusion(bf16[128,4096]{1,0:T(8,128)(2,1)S(1)} %copy-done, bf16[1,4096,512]{2,1,0:T(8,128)(2,1)} %param.16), kind=kOutput, calls=%fused_computation.16 | convolution fusion | flops 536936448 | bytes 5373952 | tf_op jit(solution)/shard_map/dot_general | solution.py:46
  138.8 1.4 fusion.9
  141.8 3.0 %collective-permute-start.6 = (bf16[128,4,128]{0,2,1:T(8,128)(2,1)S(1)}, bf16[128,4,128]{0,2,1:T(8,128)(2,1)S(1)}, u32[]{:S(2)}, u32[]{:S(2)}) collective-permute-start(bf16[128,4,128]{0,2,1:T(8,128)(2,1)S(1)} %get-tuple-element.154), channel_id=1, source_target_pairs={{4,0},{8,4},{12,8},{16,12},{20,16},{24,20},{28,24},{32,28},{36,32}... | collective-permute-start | bytes 393224 | tf_op jit(solution)/shard_map/ppermute | solution.py:27
  144.8 1.3 collective-permute-start.7
  146.4 1.9 collective-permute-start.4
  148.4 1.3 collective-permute-start.5
  149.7 0.9 collective-permute-done.6
  150.6 3.7 %collective-permute-done.7 = bf16[128,4,128]{0,2,1:T(8,128)(2,1)S(1)} collective-permute-done((bf16[128,4,128]{0,2,1:T(8,128)(2,1)S(1)}, bf16[128,4,128]{0,2,1:T(8,128)(2,1)S(1)}, u32[]{:S(2)}, u32[]{:S(2)}) %collective-permute-start.7) | collective-permute-done | bytes 131104 | tf_op jit(solution)/shard_map/ppermute | solution.py:27
  155.1 2.3 collective-permute-done.4
  157.4 1.0 collective-permute-done.5
  159.2 75.4 %reduce-scatter.2.cloned.1.call-done = bf16[128,512]{1,0:T(8,128)(2,1)} async-done(((bf16[4096,512]{1,0:T(8,128)(2,1)}), bf16[128,512]{1,0:T(8,128)(2,1)}) %reduce-scatter.2.cloned.1.call-update) | async-done | bytes 131088 | tf_op jit(solution)/shard_map/reduce_scatter | solution.py:103
  234.7 1.6 bitcast_convert_fusion
  (59 shorter events, 7.0 us)
Async XLA Ops:
  7.2 66.7 %copy-start.1 = (bf16[1,128,1024]{2,1,0:T(8,128)(2,1)S(1)}, bf16[1,128,1024]{2,1,0:T(8,128)(2,1)}, u32[]{:S(2)}) copy-start(bf16[1,128,1024]{2,1,0:T(8,128)(2,1)} %param.11) | copy-start | bytes 786436
  7.2 66.7 %copy-start.3 = (bf16[128,1024]{1,0:T(8,128)(2,1)S(1)}, bf16[128,1024]{1,0:T(8,128)(2,1)}, u32[]{:S(2)}) copy-start(bf16[128,1024]{1,0:T(8,128)(2,1)} %param.10) | copy-start | bytes 786436
  7.2 56.6 %all-gather.3.cloned.1.call-start = ((), (), s32[]{:S(2)}) async-start(), calls=%async_computation.1 | async-start | bytes 2359296 | tf_op jit(solution)/shard_map/all_gather | solution.py:12
  7.9 102.8 %copy-start.2 = (bf16[1,128,512]{2,1,0:T(8,128)(2,1)S(1)}, bf16[1,128,512]{2,1,0:T(8,128)(2,1)}, u32[]{:S(2)}) copy-start(bf16[1,128,512]{2,1,0:T(8,128)(2,1)} %param.12) | copy-start | bytes 393220
  7.9 102.7 %all-gather.5.cloned.1.call-start = ((), (), s32[]{:S(2)}) async-start(), calls=%async_computation.2 | async-start | bytes 1310720 | tf_op jit(solution)/shard_map/all_gather | solution.py:45
  74.7 160.0 %reduce-scatter.2.cloned.1.call-start = ((), (), s32[]{:S(2)}) async-start(), calls=%async_computation.3 | async-start | bytes 4325376 | tf_op jit(solution)/shard_map/reduce_scatter | solution.py:103
  115.1 0.9 copy-start.4
  115.1 10.4 %copy-start.5 = (bf16[1,128,512]{2,1,0:T(8,128)(2,1)S(1)}, bf16[1,128,512]{2,1,0:T(8,128)(2,1)}, u32[]{:S(2)}) copy-start(bf16[1,128,512]{2,1,0:T(8,128)(2,1)} %param.14) | copy-start | bytes 393220
  115.1 16.1 %copy-start.7 = (s32[32]{0:T(128)S(1)}, s32[32]{0:T(128)}, u32[]{:S(2)}) copy-start(s32[32]{0:T(128)} %param.17) | copy-start | bytes 388
  115.1 16.6 %copy-start.6 = (bf16[1,128,512]{2,1,0:T(8,128)(2,1)S(1)}, bf16[1,128,512]{2,1,0:T(8,128)(2,1)}, u32[]{:S(2)}) copy-start(bf16[1,128,512]{2,1,0:T(8,128)(2,1)} %param.13) | copy-start | bytes 393220
  116.0 19.4 %copy-start = (bf16[128,4096]{1,0:T(8,128)(2,1)S(1)}, bf16[128,4096]{1,0:T(8,128)(2,1)}, u32[]{:S(2)}) copy-start(bf16[128,4096]{1,0:T(8,128)(2,1)} %all-gather.5.cloned.1.call-done) | copy-start | bytes 3145732
  116.1 16.2 %collective-permute-start.3 = (bf16[128,512]{0,1:T(8,128)(2,1)S(1)}, bf16[128,512]{0,1:T(8,128)(2,1)S(1)}, u32[]{:S(2)}, u32[]{:S(2)}) collective-permute-start(bf16[128,512]{0,1:T(8,128)(2,1)S(1)} %bitcast.62), channel_id=1, source_target_pairs={{0,4},{4,8},{8,12},{12,16},{16,20},{20,24},{24,28},{28,32},{32,36}... | collective-permute-start | bytes 393224 | tf_op jit(solution)/shard_map/ppermute | solution.py:27
  122.2 10.3 %collective-permute-start.2 = (bf16[128,512]{0,1:T(8,128)(2,1)S(1)}, bf16[128,512]{0,1:T(8,128)(2,1)S(1)}, u32[]{:S(2)}, u32[]{:S(2)}) collective-permute-start(bf16[128,512]{0,1:T(8,128)(2,1)S(1)} %bitcast.63), channel_id=1, source_target_pairs={{0,8},{4,12},{8,16},{12,20},{16,24},{20,28},{24,32},{28,36},{32,40... | collective-permute-start | bytes 393224 | tf_op jit(solution)/shard_map/ppermute | solution.py:27
  125.6 7.0 %collective-permute-start.1 = (bf16[128,512]{0,1:T(8,128)(2,1)S(1)}, bf16[128,512]{0,1:T(8,128)(2,1)S(1)}, u32[]{:S(2)}, u32[]{:S(2)}) collective-permute-start(bf16[128,512]{0,1:T(8,128)(2,1)S(1)} %bitcast.59), channel_id=1, source_target_pairs={{0,4},{4,8},{8,12},{12,16},{16,20},{20,24},{24,28},{28,32},{32,36}... | collective-permute-start | bytes 393224 | tf_op jit(solution)/shard_map/ppermute | solution.py:27
  127.8 5.9 %collective-permute-start = (bf16[128,512]{0,1:T(8,128)(2,1)S(1)}, bf16[128,512]{0,1:T(8,128)(2,1)S(1)}, u32[]{:S(2)}, u32[]{:S(2)}) collective-permute-start(bf16[128,512]{0,1:T(8,128)(2,1)S(1)} %bitcast.60), channel_id=1, source_target_pairs={{0,8},{4,12},{8,16},{12,20},{16,24},{20,28},{24,32},{28,36},{32,40... | collective-permute-start | bytes 393224 | tf_op jit(solution)/shard_map/ppermute | solution.py:27
  141.8 8.8 %collective-permute-start.6 = (bf16[128,4,128]{0,2,1:T(8,128)(2,1)S(1)}, bf16[128,4,128]{0,2,1:T(8,128)(2,1)S(1)}, u32[]{:S(2)}, u32[]{:S(2)}) collective-permute-start(bf16[128,4,128]{0,2,1:T(8,128)(2,1)S(1)} %get-tuple-element.154), channel_id=1, source_target_pairs={{4,0},{8,4},{12,8},{16,12},{20,16},{24,20},{28,24},{32,28},{36,32}... | collective-permute-start | bytes 393224 | tf_op jit(solution)/shard_map/ppermute | solution.py:27
  144.8 9.5 %collective-permute-start.7 = (bf16[128,4,128]{0,2,1:T(8,128)(2,1)S(1)}, bf16[128,4,128]{0,2,1:T(8,128)(2,1)S(1)}, u32[]{:S(2)}, u32[]{:S(2)}) collective-permute-start(bf16[128,4,128]{0,2,1:T(8,128)(2,1)S(1)} %get-tuple-element.155), channel_id=1, source_target_pairs={{8,0},{12,4},{16,8},{20,12},{24,16},{28,20},{32,24},{36,28},{40,32... | collective-permute-start | bytes 393224 | tf_op jit(solution)/shard_map/ppermute | solution.py:27
  146.4 10.9 %collective-permute-start.4 = (bf16[128,4,128]{0,2,1:T(8,128)(2,1)S(1)}, bf16[128,4,128]{0,2,1:T(8,128)(2,1)S(1)}, u32[]{:S(2)}, u32[]{:S(2)}) collective-permute-start(bf16[128,4,128]{0,2,1:T(8,128)(2,1)S(1)} %get-tuple-element.156), channel_id=1, source_target_pairs={{4,0},{8,4},{12,8},{16,12},{20,16},{24,20},{28,24},{32,28},{36,32}... | collective-permute-start | bytes 393224 | tf_op jit(solution)/shard_map/ppermute | solution.py:27
  148.4 10.0 %collective-permute-start.5 = (bf16[128,4,128]{0,2,1:T(8,128)(2,1)S(1)}, bf16[128,4,128]{0,2,1:T(8,128)(2,1)S(1)}, u32[]{:S(2)}, u32[]{:S(2)}) collective-permute-start(bf16[128,4,128]{0,2,1:T(8,128)(2,1)S(1)} %get-tuple-element.157), channel_id=1, source_target_pairs={{8,0},{12,4},{16,8},{20,12},{24,16},{28,20},{32,24},{36,28},{40,32... | collective-permute-start | bytes 393224 | tf_op jit(solution)/shard_map/ppermute | solution.py:27
Sparse Core Ops, SparseCore 0:
  10.7 53.0 all-gather.2
  74.8 35.8 all-gather.4
  115.3 119.3 reduce-scatter.1
where the time goes:
time: 246 us; the launch traced here: 243 us
  waiting for transfers between devices  177 us (72%)
  starting transfers between devices  22.4 us (9%)
  between operations  14.1 us (6%)
  other arithmetic  13.2 us (5%)
  matrix products  11.3 us (5%)
  local copies, waits for them, and re-layouts  4.86 us (2%)
    reduce_scatter x1, waiting for transfers between devices, on_device(): lax.psum_scatter(lax.dot_general(grad_full, ctx_flat, (((0,), (0,)), ((),...  75.4 us
    all_gather x1, waiting for transfers between devices, entering(): everything = lax.all_gather(value.astype(jnp.bfloat16), axis)  55.8 us
    all_gather x1, waiting for transfers between devices, on_device(): grad_full = lax.all_gather(grad_local, 'tensor', axis=1, tiled=True)  35.9 us
    ppermute x8, starting transfers between devices, passed_along(): lax.ppermute(value, axis, [(source, source + steps) for source in range(l...  22.3 us
    select_n x8, other arithmetic, hop(): return jnp.where(reached, new, before)  9.85 us
    ppermute x8, waiting for transfers between devices, passed_along(): lax.ppermute(value, axis, [(source, source + steps) for source in range(l...  8.84 us
  transfers between devices with their start and end apart: 11, of which 8 were waited for; matrix products, arithmetic and copies ran while one was open for 5% of the time, Pallas kernels for 0%

commit v1 on v0

v1 whole, which is shorter than its diff:
```python
import functools

import jax
import jax.numpy as jnp
from jax import lax
from jax.experimental import pallas as pl
from jax.experimental.pallas import tpu as pltpu
from jax.sharding import Mesh, PartitionSpec as P

HD = 128
REACH = 2
CORES = 2
F32 = jnp.float32
BF16 = jnp.bfloat16
WHOLE = pl.BlockSpec(memory_space=pltpu.VMEM)
SCALARS = pl.BlockSpec(memory_space=pltpu.SMEM)
DP = ("z", "core")


def contract(a, b, left, right):
    return lax.dot_general(
        a, b, (((left,), (right,)), ((), ())), preferred_element_type=F32
    )


def shifted(value, steps):
    count = lax.axis_size("z") * lax.axis_size("core")
    return lax.ppermute(value, DP, [(i, (i + steps) % count) for i in range(count)])


def exchanged(value, axis):
    return lax.all_to_all(value, axis, 0, 0, tiled=True)


def spread(value, axis):
    copies = lax.axis_size(axis)
    return exchanged(jnp.broadcast_to(value[None], (copies, *value.shape)), axis)


def suffix_kernel(out_grad_ref, layers_ref, grads_ref):
    count, rows, _ = layers_ref.shape
    at = pl.multiple_of(lax.axis_index("section") * rows, rows)
    base = out_grad_ref[pl.ds(at, rows), :].astype(F32)
    upper = None
    for layer in range(count - 1, -1, -1):
        own = layers_ref[layer].astype(F32)
        upper = own if upper is None else upper + own
        grads_ref[layer] = (base + 0.25 * upper).astype(BF16)


def prob_kernel(lengths_ref, query_ref, own_ref, near_ref, far_ref, prob_ref):
    rows, width = query_ref.shape
    window = (REACH + 1) * rows
    block = lax.axis_index("z") * CORES + lax.axis_index("core")
    first = block * rows
    place = first + lax.broadcasted_iota(jnp.int32, (rows, window), 0)
    keys = first - REACH * rows + lax.broadcasted_iota(jnp.int32, (rows, window), 1)
    narrow = first + lax.broadcasted_iota(jnp.int32, (rows, HD), 0)

    def advance(k, carry):
        end, start = carry
        end = end + lengths_ref[k]
        return end, jnp.where(narrow >= end, end, start)

    start = lax.fori_loop(
        0, lengths_ref.shape[0], advance, (jnp.int32(0), jnp.zeros((rows, HD), jnp.int32))
    )[1]
    start = jnp.concatenate([start] * (window // HD), axis=1)
    allowed = (keys <= place) & (keys >= start)
    for head in range(width // HD):
        cols = slice(head * HD, (head + 1) * HD)
        query = query_ref[:, cols]
        scores = jnp.concatenate(
            [contract(query, ref[0, :, cols], 1, 1) for ref in (far_ref, near_ref, own_ref)],
            axis=1,
        )
        scores = jnp.where(allowed, scores * HD ** (-0.5), -jnp.inf)
        top = jnp.max(scores, axis=-1, keepdims=True)
        weight = jnp.exp(scores - top)
        prob_ref[head] = weight / jnp.sum(weight, axis=-1, keepdims=True)


def grads_kernel(
    grad_ref, weight_ref, prob_ref, query_ref, own_ref, near_ref, far_ref, context_ref,
    query_grad_ref, own_part_ref, near_part_ref, far_part_ref,
):
    parts, rows, width = grad_ref.shape
    total = None
    for part in range(parts):
        term = jnp.dot(
            grad_ref[part],
            weight_ref[part * width : (part + 1) * width, :],
            preferred_element_type=F32,
        )
        total = term if total is None else total + term
    d_context = total.astype(BF16)
    blocks = ((far_ref, far_part_ref), (near_ref, near_part_ref), (own_ref, own_part_ref))
    for head in range(query_ref.shape[1] // HD):
        cols = slice(head * HD, (head + 1) * HD)
        query = query_ref[:, cols]
        dctx = d_context[:, cols]
        delta = jnp.sum(
            dctx.astype(F32) * context_ref[:, cols].astype(F32), axis=-1, keepdims=True
        )
        query_grad = None
        for index, (held, part_ref) in enumerate(blocks):
            prob = prob_ref[head, :, index * rows : (index + 1) * rows]
            d_prob = contract(dctx, held[1, :, cols], 1, 1)
            d_score = (prob * (d_prob - delta) * HD ** (-0.5)).astype(BF16)
            term = jnp.dot(d_score, held[0, :, cols], preferred_element_type=F32)
            query_grad = term if query_grad is None else query_grad + term
            part_ref[0, :, cols] = contract(d_score, query, 0, 0).astype(part_ref.dtype)
            part_ref[1, :, cols] = contract(prob.astype(BF16), dctx, 0, 0).astype(part_ref.dtype)
        query_grad_ref[:, cols] = query_grad.astype(BF16)


def weight_kernel(grad_ref, context_ref, keep_ref, send_ref):
    quarters, blocks, rows, features = grad_ref.shape
    total = None
    for quarter in range(quarters):
        grad = grad_ref[quarter].reshape(blocks * rows, features)
        context = context_ref[:, quarter * rows : (quarter + 1) * rows, :]
        term = contract(grad, context.reshape(blocks * rows, context.shape[-1]), 0, 0)
        total = term if total is None else total + term
    half = features // CORES
    first, second = total[:half], total[half:]
    is_first = lax.axis_index("core") == 0
    keep_ref[...] = jnp.where(is_first, first, second)
    send_ref[...] = jnp.where(is_first, second, first).astype(BF16)


def call(kernel, outs, inputs, specs, flops, nbytes):
    return pl.pallas_call(
        kernel,
        out_shape=outs,
        in_specs=specs,
        out_specs=[WHOLE] * len(outs),
        cost_estimate=pl.CostEstimate(flops=flops, bytes_accessed=nbytes, transcendentals=0),
        compiler_params=pltpu.CompilerParams(vmem_limit_bytes=28 * 2**20),
    )(*inputs)


def on_device(out_grad, section_out, context, queries, key_heads, values, o_weight, doc_lengths):
    rows, width = queries.shape[1:]
    features = out_grad.shape[1]
    sections, tensors, chips = (lax.axis_size(a) for a in ("section", "tensor", "z"))
    heads = width // HD
    window = (REACH + 1) * rows
    shape = jax.ShapeDtypeStruct

    context_all = lax.all_gather(context[0], "z")

    layers = exchanged(section_out.reshape(sections, rows // sections, features), "section")
    held = jnp.concatenate([key_heads, values], 0)
    near = shifted(held, 1)
    far = shifted(held, 2)
    (grads,) = call(
        suffix_kernel,
        [shape(layers.shape, BF16)],
        (out_grad, layers),
        [WHOLE] * 2,
        layers.size * 3,
        layers.size * 4,
    )
    grad_local = exchanged(grads, "section").reshape(rows, features)
    (prob,) = call(
        prob_kernel,
        [shape((heads, rows, window), F32)],
        (doc_lengths, queries[0], held, near, far),
        [SCALARS] + [WHOLE] * 4,
        heads * rows * window * (2 * HD + 10),
        heads * rows * window * 8,
    )
    grad_full = spread(grad_local, "tensor")

    quarter = rows // tensors
    mine = lax.dynamic_slice_in_dim(grad_full, lax.axis_index("tensor") * quarter, quarter, 1)
    pieces = chips // tensors
    mine = jnp.transpose(
        mine.reshape(tensors, quarter, pieces, features // pieces), (0, 2, 1, 3)
    ).reshape(chips, quarter, features // pieces)
    columns = exchanged(mine, "z")

    query_grad, own_part, near_part, far_part = call(
        grads_kernel,
        [
            shape((rows, width), BF16),
            shape((2, rows, width), F32),
            shape((2, rows, width), BF16),
            shape((2, rows, width), BF16),
        ],
        (grad_full, o_weight[0], prob, queries[0], held, near, far, context[0]),
        [WHOLE] * 8,
        2 * rows * features * tensors * width + 8 * rows * window * width,
        2 * features * tensors * width,
    )
    near_back = shifted(near_part, -1)
    far_back = shifted(far_part, -2)
    sums = (own_part + near_back.astype(F32) + far_back.astype(F32)).astype(BF16)

    columns_all = spread(columns, "tensor")
    keep, send = call(
        weight_kernel,
        [shape((rows, width), F32), shape((rows, width), BF16)],
        (columns_all, context_all),
        [WHOLE] * 2,
        2 * columns_all.size * width,
        2 * (columns_all.size + context_all.size),
    )
    other = lax.ppermute(send, "core", [(i, CORES - 1 - i) for i in range(CORES)])
    weight_grad = keep + other.astype(F32)
    return query_grad[None], sums[:1], sums[1:], weight_grad[None]


def solution(mesh):
    sections, shards, tensors = mesh.devices.shape
    split = Mesh(
        mesh.devices.reshape(sections, shards // CORES, CORES, tensors),
        ("section", "z", "core", "tensor"),
    )
    placed = P("section", DP, "tensor")
    return jax.shard_map(
        on_device,
        mesh=split,
        in_specs=(
            P(DP, "tensor"), placed, placed, placed, placed, placed,
            P("section", None, "tensor"), P(),
        ),
        out_specs=(placed,) * 4,
        check_vma=False,
    )
```

time: 246 us -> 138 us (0.56)
  waiting for transfers between devices: 177 us -> 33.9 us
  blocking collectives: 0 us -> 29 us
  starting transfers between devices: 22.4 us -> 44.7 us
  other arithmetic: 13.2 us -> 1.57 us
  matrix products: 11.3 us -> 0 us
  Pallas kernels: 0 us -> 5.79 us
  local copies, waits for them, and re-layouts: 4.86 us -> 7.75 us
    all_gather x2 -> x1, waiting for transfers between devices: 91.7 us -> 0.02 us  [on_device(): context_all = lax.all_gather(context[0], 'z')]
    reduce_scatter x1 -> x0, waiting for transfers between devices: 75.4 us -> none  [on_device(): lax.psum_scatter(lax.dot_general(grad_full, ctx_flat, (((0,), (0,)), ((),...]
    all_to_all x0 -> x3, starting transfers between devices: none -> 29 us  [exchanged(): return lax.all_to_all(value, axis, 0, 0, tiled=True)]
    all_to_all x0 -> x2, blocking collectives: none -> 29 us  [exchanged(): return lax.all_to_all(value, axis, 0, 0, tiled=True)]
    all_to_all x0 -> x3, waiting for transfers between devices: none -> 13.9 us  [exchanged(): return lax.all_to_all(value, axis, 0, 0, tiled=True)]
    ppermute x8 -> x5, waiting for transfers between devices: 8.84 us -> 19.4 us  [the longest x4 18.8 us: shifted(): lax.ppermute(value, DP, [(i, (i + steps) % count) for i in range(count)])]
    dot_general x7 -> x0, matrix products: 10 us -> none  [the longest x1 4.44 us: on_device(): lax.dot_general(grad_full, ctx_flat, (((0,), (0,)), ((), ())), preferred_...]
    select_n x8 -> x0, other arithmetic: 9.85 us -> none  [hop(): return jnp.where(reached, new, before)]
  transfers between devices with their start and end apart: 11 -> 9, of which waited for: 8 -> 7; matrix products, arithmetic and copies ran while one was open for 5% -> 3% of each run, Pallas kernels for 0% -> 4%
where the time goes in v1:
time: 138 us; the launch traced here: 137 us
  starting transfers between devices  44.7 us (32%)
  waiting for transfers between devices  33.9 us (25%)
  blocking collectives  29 us (21%)
  between operations  14.2 us (10%)
  local copies, waits for them, and re-layouts  7.75 us (6%)
  Pallas kernels  5.79 us (4%)
  other arithmetic  1.57 us (1%)
    all_to_all x3, starting transfers between devices, exchanged(): return lax.all_to_all(value, axis, 0, 0, tiled=True)  29 us
    all_to_all x2, blocking collectives, exchanged(): return lax.all_to_all(value, axis, 0, 0, tiled=True)  29 us
    ppermute x4, waiting for transfers between devices, shifted(): lax.ppermute(value, DP, [(i, (i + steps) % count) for i in range(count)])  18.8 us
    all_to_all x3, waiting for transfers between devices, exchanged(): return lax.all_to_all(value, axis, 0, 0, tiled=True)  13.9 us
    ppermute x4, starting transfers between devices, shifted(): lax.ppermute(value, DP, [(i, (i + steps) % count) for i in range(count)])  13.7 us
    pallas_call x4, Pallas kernels, call(): pl.pallas_call(kernel, out_shape=outs, in_specs=specs, out_specs=[WHOLE]...  5.79 us
    unnamed x17, local copies, waits for them, and re-layouts  4.75 us
  transfers between devices with their start and end apart: 9, of which 7 were waited for; matrix products, arithmetic and copies ran while one was open for 3% of the time, Pallas kernels for 4%

profile of v1, /device:TPU:1, one launch (start us, length us, event | category | flops | bytes accessed | tf_op | source)
XLA Modules:
  0.0 136.9 jit_solution(764255589784220611)
XLA Ops:
  7.2 0.0 all-gather.2.cloned.1.call-start
  7.2 0.7 all-gather.2.cloned.1.call-update
  7.9 17.0 %all_to_all.25.layers_ref = bf16[8,16,1024]{2,1,0:T(8,128)(2,1)S(1)} all-to-all(bf16[8,16,1024]{2,1,0:T(8,128)(2,1)} %bitcast.14), channel_id=1, replica_groups=mesh['section'=8,'z'=16,'core'=2,'tensor'=4] {'section'}, dimensions={0} | all-to-all | bytes 524288 | tf_op jit(solution)/shard_map/all_to_all | solution.py:32
  24.9 0.9 copy-done.4
  25.9 0.1 shard_map.111
  25.9 12.0 %all_to_all.26 = bf16[8,16,1024]{2,1,0:T(8,128)(2,1)S(1)} all-to-all(bf16[8,16,1024]{2,1,0:T(8,128)(2,1)S(1)} %shard_map.111), channel_id=1, replica_groups=mesh['section'=8,'z'=16,'core'=2,'tensor'=4] {'section'}, dimensions={0} | all-to-all | bytes 524288 | tf_op jit(solution)/shard_map/all_to_all | solution.py:32
  38.0 1.1 broadcast_in_dim.20
  39.1 5.3 %all-to-all-start.2 = ((bf16[4,128,1024]{2,1,0:T(8,128)(2,1)}), bf16[4,128,1024]{2,1,0:T(8,128)(2,1)S(1)}, u32[]{:S(2)}, u32[]{:S(2)}) async-start(bf16[4,128,1024]{2,1,0:T(8,128)(2,1)} %broadcast_in_dim.20), calls=%async_computation.2 | async-start | bytes 2097152 | tf_op jit(solution)/shard_map/all_to_all | solution.py:32
  44.4 9.7 %all-to-all-done.2.grad_ref = bf16[4,128,1024]{2,1,0:T(8,128)(2,1)S(1)} async-done(((bf16[4,128,1024]{2,1,0:T(8,128)(2,1)}), bf16[4,128,1024]{2,1,0:T(8,128)(2,1)S(1)}, u32[]{:S(2)}, u32[]{:S(2)}) %all-to-all-start.2) | async-done | bytes 1048608 | tf_op jit(solution)/shard_map/all_to_all | solution.py:32
  54.2 0.7 pad_maximum_fusion
  54.9 20.2 %all-to-all-start.3 = ((bf16[16,32,256]{2,1,0:T(8,128)(2,1)}), bf16[16,32,256]{2,1,0:T(8,128)(2,1)S(1)}, u32[]{:S(2)}, u32[]{:S(2)}) async-start(bf16[16,32,256]{2,1,0:T(8,128)(2,1)} %bitcast.6), calls=%async_computation.3 | async-start | bytes 524288 | tf_op jit(solution)/shard_map/all_to_all | solution.py:32
  75.2 6.5 %collective-permute-start = (bf16[2,128,512]{2,1,0:T(8,128)(2,1)S(1)}, bf16[2,128,512]{2,1,0:T(8,128)(2,1)S(1)}, u32[]{:S(2)}, u32[]{:S(2)}) collective-permute-start(bf16[2,128,512]{2,1,0:T(8,128)(2,1)S(1)} %constant_dynamic-update-slice_fusion.own_ref), channel_id=1, source_target_pairs={{0,4},{4,8},{8,12},{12,16},{16,20},{20,24},{24,28},{28,32},{32,36}... | collective-permute-start | bytes 786440 | tf_op jit(solution)/shard_map/ppermute | solution.py:28
  81.7 3.1 %collective-permute-start.1 = (bf16[2,128,512]{2,1,0:T(8,128)(2,1)S(1)}, bf16[2,128,512]{2,1,0:T(8,128)(2,1)S(1)}, u32[]{:S(2)}, u32[]{:S(2)}) collective-permute-start(bf16[2,128,512]{2,1,0:T(8,128)(2,1)S(1)} %constant_dynamic-update-slice_fusion.own_ref), channel_id=1, source_target_pairs={{0,8},{4,12},{8,16},{12,20},{16,24},{20,28},{24,32},{28,36},{32,40... | collective-permute-start | bytes 786440 | tf_op jit(solution)/shard_map/ppermute | solution.py:28
  84.8 4.1 %all-to-all-done.3 = bf16[16,32,256]{2,1,0:T(8,128)(2,1)S(1)} async-done(((bf16[16,32,256]{2,1,0:T(8,128)(2,1)}), bf16[16,32,256]{2,1,0:T(8,128)(2,1)S(1)}, u32[]{:S(2)}, u32[]{:S(2)}) %all-to-all-start.3) | async-done | bytes 262176 | tf_op jit(solution)/shard_map/all_to_all | solution.py:32
  88.9 1.1 broadcast_in_dim.22
  90.0 3.5 %all-to-all-start.4 = ((bf16[4,16,32,256]{3,2,1,0:T(8,128)(2,1)}), bf16[4,16,32,256]{3,2,1,0:T(8,128)(2,1)S(1)}, u32[]{:S(2)}, u32[]{:S(2)}) async-start(bf16[4,16,32,256]{3,2,1,0:T(8,128)(2,1)} %broadcast_in_dim.22), calls=%async_computation.4 | async-start | bytes 2097152 | tf_op jit(solution)/shard_map/all_to_all | solution.py:32
  93.5 3.1 %collective-permute-done.near_ref = bf16[2,128,512]{2,1,0:T(8,128)(2,1)S(1)} collective-permute-done((bf16[2,128,512]{2,1,0:T(8,128)(2,1)S(1)}, bf16[2,128,512]{2,1,0:T(8,128)(2,1)S(1)}, u32[]{:S(2)}, u32[]{:S(2)}) %collective-permute-start) | collective-permute-done | bytes 262176 | tf_op jit(solution)/shard_map/ppermute | solution.py:28
  96.7 7.0 %collective-permute-done.1.far_ref = bf16[2,128,512]{2,1,0:T(8,128)(2,1)S(1)} collective-permute-done((bf16[2,128,512]{2,1,0:T(8,128)(2,1)S(1)}, bf16[2,128,512]{2,1,0:T(8,128)(2,1)S(1)}, u32[]{:S(2)}, u32[]{:S(2)}) %collective-permute-start.1) | collective-permute-done | bytes 262176 | tf_op jit(solution)/shard_map/ppermute | solution.py:28
  103.7 1.5 %shard_map.112.prob_ref = f32[4,128,384]{2,1,0:T(8,128)S(1)} custom-call(s32[32]{0:T(128)S(1)} %copy-done.5, bf16[128,512]{1,0:T(8,128)(2,1)S(1)} %bitcast.10, bf16[2,128,512]{2,1,0:T(8,128)(2,1)S(1)} %constant_dynamic-update-slice_fusion.own_ref, bf16[2,128,512]{2,1,0:T(8,128)(2,1)S(1)} %collective-permute-done.near_ref, ...), custom_call_target="tpu_custom_call" | custom-call | flops 52297728 | bytes 1572864 | tf_op jit(solution)/shard_map/pallas_call | solution.py:133
  105.2 2.2 %copy-done = bf16[1,4096,512]{2,1,0:T(8,128)(2,1)S(1)} copy-done((bf16[1,4096,512]{2,1,0:T(8,128)(2,1)S(1)}, bf16[1,4096,512]{2,1,0:T(8,128)(2,1)}, u32[]{:S(2)}) %copy-start) | copy-done | bytes 4194328
  107.4 3.4 %shard_map.113 = (bf16[128,512]{1,0:T(8,128)(2,1)}, f32[2,128,512]{2,1,0:T(8,128)S(1)}, bf16[2,128,512]{2,1,0:T(8,128)(2,1)S(1)}, bf16[2,128,512]{2,1,0:T(8,128)(2,1)S(1)}) custom-call(bf16[4,128,1024]{2,1,0:T(8,128)(2,1)S(1)} %all-to-all-done.2.grad_ref, bf16[4096,512]{1,0:T(8,128)(2,1)S(1)} %bitcast.9, f32[4,128,384]{2,1,0:T(8,128)S(1)} %shard_map.112.prob_ref, ...), custom_call_target="tpu_custom_call" | custom-call | flops 738197504 | bytes 4194304 | tf_op jit(solution)/shard_map/pallas_call | solution.py:133
  110.8 3.1 %collective-permute-start.3 = (bf16[2,128,512]{2,1,0:T(8,128)(2,1)S(1)}, bf16[2,128,512]{2,1,0:T(8,128)(2,1)S(1)}, u32[]{:S(2)}, u32[]{:S(2)}) collective-permute-start(bf16[2,128,512]{2,1,0:T(8,128)(2,1)S(1)} %get-tuple-element.13), channel_id=1, source_target_pairs={{0,120},{4,124},{8,0},{12,4},{16,8},{20,12},{24,16},{28,20},{32,24... | collective-permute-start | bytes 786440 | tf_op jit(solution)/shard_map/ppermute | solution.py:28
  114.0 0.9 collective-permute-start.2
  114.9 4.9 %collective-permute-done.3 = bf16[2,128,512]{2,1,0:T(8,128)(2,1)S(1)} collective-permute-done((bf16[2,128,512]{2,1,0:T(8,128)(2,1)S(1)}, bf16[2,128,512]{2,1,0:T(8,128)(2,1)S(1)}, u32[]{:S(2)}, u32[]{:S(2)}) %collective-permute-start.3) | collective-permute-done | bytes 262176 | tf_op jit(solution)/shard_map/ppermute | solution.py:28
  119.8 3.7 %collective-permute-done.2 = bf16[2,128,512]{2,1,0:T(8,128)(2,1)S(1)} collective-permute-done((bf16[2,128,512]{2,1,0:T(8,128)(2,1)S(1)}, bf16[2,128,512]{2,1,0:T(8,128)(2,1)S(1)}, u32[]{:S(2)}, u32[]{:S(2)}) %collective-permute-start.2) | collective-permute-done | bytes 262176 | tf_op jit(solution)/shard_map/ppermute | solution.py:28
  123.6 0.1 add_convert_fusion
  123.7 1.6 %copy-done.1 = bf16[16,128,512]{2,1,0:T(8,128)(2,1)S(1)} copy-done((bf16[16,128,512]{2,1,0:T(8,128)(2,1)S(1)}, bf16[16,128,512]{2,1,0:T(8,128)(2,1)}, u32[]{:S(2)}) %copy-start.1) | copy-done | bytes 2097176
  125.3 0.7 shard_map.114
  126.0 1.9 %collective-permute-start.4 = (bf16[128,512]{1,0:T(8,128)(2,1)S(1)}, bf16[128,512]{1,0:T(8,128)(2,1)S(1)}, u32[]{:S(2)}, u32[]{:S(2)}) collective-permute-start(bf16[128,512]{1,0:T(8,128)(2,1)S(1)} %get-tuple-element.15), channel_id=1, source_target_pairs={{0,4},{4,0},{1,5},{5,1},{2,6},{6,2},{3,7},{7,3},{8,12},{12,8},{9,1... | collective-permute-start | bytes 393224 | tf_op jit(solution)/shard_map/ppermute | solution.py:210
  128.0 0.7 fusion
  128.7 0.6 collective-permute-done.4
  129.3 0.7 add_bitcast_fusion
  (18 shorter events, 0.1 us)
Async XLA Ops:
  7.2 68.0 %copy-start.6 = (bf16[1,128,512]{2,1,0:T(8,128)(2,1)S(1)}, bf16[1,128,512]{2,1,0:T(8,128)(2,1)}, u32[]{:S(2)}) copy-start(bf16[1,128,512]{2,1,0:T(8,128)(2,1)} %param.12) | copy-start | bytes 393220
  7.2 68.0 %copy-start.7 = (bf16[1,128,512]{2,1,0:T(8,128)(2,1)S(1)}, bf16[1,128,512]{2,1,0:T(8,128)(2,1)}, u32[]{:S(2)}) copy-start(bf16[1,128,512]{2,1,0:T(8,128)(2,1)} %param.13) | copy-start | bytes 393220
  7.2 116.5 %all-gather.2.cloned.1.call-start = ((), (), s32[]{:S(2)}) async-start(), calls=%async_computation.5 | async-start | bytes 2228224 | tf_op jit(solution)/shard_map/all_gather | solution.py:151
  24.9 1.0 copy-start.4
  38.0 65.7 %copy-start.2 = (bf16[1,128,512]{2,1,0:T(8,128)(2,1)S(1)}, bf16[1,128,512]{2,1,0:T(8,128)(2,1)}, u32[]{:S(2)}) copy-start(bf16[1,128,512]{2,1,0:T(8,128)(2,1)} %param.11) | copy-start | bytes 393220
  38.0 65.7 %copy-start.5 = (s32[32]{0:T(128)S(1)}, s32[32]{0:T(128)}, u32[]{:S(2)}) copy-start(s32[32]{0:T(128)} %lengths_ref.1) | copy-start | bytes 388
  39.1 66.1 %copy-start.3 = (bf16[1,128,512]{2,1,0:T(8,128)(2,1)S(1)}, bf16[1,128,512]{2,1,0:T(8,128)(2,1)}, u32[]{:S(2)}) copy-start(bf16[1,128,512]{2,1,0:T(8,128)(2,1)} %param.10) | copy-start | bytes 393220
  39.1 15.1 %all-to-all-start.2 = ((bf16[4,128,1024]{2,1,0:T(8,128)(2,1)}), bf16[4,128,1024]{2,1,0:T(8,128)(2,1)S(1)}, u32[]{:S(2)}, u32[]{:S(2)}) async-start(bf16[4,128,1024]{2,1,0:T(8,128)(2,1)} %broadcast_in_dim.20), calls=%async_computation.2 | async-start | bytes 2097152 | tf_op jit(solution)/shard_map/all_to_all | solution.py:32
  54.9 34.0 %all-to-all-start.3 = ((bf16[16,32,256]{2,1,0:T(8,128)(2,1)}), bf16[16,32,256]{2,1,0:T(8,128)(2,1)S(1)}, u32[]{:S(2)}, u32[]{:S(2)}) async-start(bf16[16,32,256]{2,1,0:T(8,128)(2,1)} %bitcast.6), calls=%async_computation.3 | async-start | bytes 524288 | tf_op jit(solution)/shard_map/all_to_all | solution.py:32
  75.2 21.5 %collective-permute-start = (bf16[2,128,512]{2,1,0:T(8,128)(2,1)S(1)}, bf16[2,128,512]{2,1,0:T(8,128)(2,1)S(1)}, u32[]{:S(2)}, u32[]{:S(2)}) collective-permute-start(bf16[2,128,512]{2,1,0:T(8,128)(2,1)S(1)} %constant_dynamic-update-slice_fusion.own_ref), channel_id=1, source_target_pairs={{0,4},{4,8},{8,12},{12,16},{16,20},{20,24},{24,28},{28,32},{32,36}... | collective-permute-start | bytes 786440 | tf_op jit(solution)/shard_map/ppermute | solution.py:28
  81.7 22.0 %collective-permute-start.1 = (bf16[2,128,512]{2,1,0:T(8,128)(2,1)S(1)}, bf16[2,128,512]{2,1,0:T(8,128)(2,1)S(1)}, u32[]{:S(2)}, u32[]{:S(2)}) collective-permute-start(bf16[2,128,512]{2,1,0:T(8,128)(2,1)S(1)} %constant_dynamic-update-slice_fusion.own_ref), channel_id=1, source_target_pairs={{0,8},{4,12},{8,16},{12,20},{16,24},{20,28},{24,32},{28,36},{32,40... | collective-permute-start | bytes 786440 | tf_op jit(solution)/shard_map/ppermute | solution.py:28
  90.0 33.7 %all-to-all-start.4 = ((bf16[4,16,32,256]{3,2,1,0:T(8,128)(2,1)}), bf16[4,16,32,256]{3,2,1,0:T(8,128)(2,1)S(1)}, u32[]{:S(2)}, u32[]{:S(2)}) async-start(bf16[4,16,32,256]{3,2,1,0:T(8,128)(2,1)} %broadcast_in_dim.22), calls=%async_computation.4 | async-start | bytes 2097152 | tf_op jit(solution)/shard_map/all_to_all | solution.py:32
  105.2 2.2 %copy-start = (bf16[1,4096,512]{2,1,0:T(8,128)(2,1)S(1)}, bf16[1,4096,512]{2,1,0:T(8,128)(2,1)}, u32[]{:S(2)}) copy-start(bf16[1,4096,512]{2,1,0:T(8,128)(2,1)} %param.14) | copy-start | bytes 12582916
  110.8 9.0 %collective-permute-start.3 = (bf16[2,128,512]{2,1,0:T(8,128)(2,1)S(1)}, bf16[2,128,512]{2,1,0:T(8,128)(2,1)S(1)}, u32[]{:S(2)}, u32[]{:S(2)}) collective-permute-start(bf16[2,128,512]{2,1,0:T(8,128)(2,1)S(1)} %get-tuple-element.13), channel_id=1, source_target_pairs={{0,120},{4,124},{8,0},{12,4},{16,8},{20,12},{24,16},{28,20},{32,24... | collective-permute-start | bytes 786440 | tf_op jit(solution)/shard_map/ppermute | solution.py:28
  114.0 9.6 %collective-permute-start.2 = (bf16[2,128,512]{2,1,0:T(8,128)(2,1)S(1)}, bf16[2,128,512]{2,1,0:T(8,128)(2,1)S(1)}, u32[]{:S(2)}, u32[]{:S(2)}) collective-permute-start(bf16[2,128,512]{2,1,0:T(8,128)(2,1)S(1)} %get-tuple-element.12), channel_id=1, source_target_pairs={{0,124},{4,0},{8,4},{12,8},{16,12},{20,16},{24,20},{28,24},{32,28}... | collective-permute-start | bytes 786440 | tf_op jit(solution)/shard_map/ppermute | solution.py:28
  123.7 1.6 %copy-start.1 = (bf16[16,128,512]{2,1,0:T(8,128)(2,1)S(1)}, bf16[16,128,512]{2,1,0:T(8,128)(2,1)}, u32[]{:S(2)}) copy-start(bf16[16,128,512]{2,1,0:T(8,128)(2,1)} %all-gather.2.cloned.1.call-done.context_ref) | copy-start | bytes 6291460
  126.0 3.2 %collective-permute-start.4 = (bf16[128,512]{1,0:T(8,128)(2,1)S(1)}, bf16[128,512]{1,0:T(8,128)(2,1)S(1)}, u32[]{:S(2)}, u32[]{:S(2)}) collective-permute-start(bf16[128,512]{1,0:T(8,128)(2,1)S(1)} %get-tuple-element.15), channel_id=1, source_target_pairs={{0,4},{4,0},{1,5},{5,1},{2,6},{6,2},{3,7},{7,3},{8,12},{12,8},{9,1... | collective-permute-start | bytes 393224 | tf_op jit(solution)/shard_map/ppermute | solution.py:210
Sparse Core Ops, SparseCore 0:
  10.7 83.7 all-gather.1

commit v2 on v1

v2 whole, which is shorter than its diff:
```python
import jax
import jax.numpy as jnp
from jax import lax
from jax.experimental import pallas as pl
from jax.experimental.pallas import tpu as pltpu
from jax.sharding import Mesh, PartitionSpec as P


HD = 128
REACH = 2
CORES = 2
NEAR = 2
F32 = jnp.float32
BF16 = jnp.bfloat16
WHOLE = pl.BlockSpec(memory_space=pltpu.VMEM)
SCALARS = pl.BlockSpec(memory_space=pltpu.SMEM)
DP = ("zh", "zl", "core")
GROUP = ("zl", "core")


def contract(a, b, left, right):
    return lax.dot_general(
        a, b, (((left,), (right,)), ((), ())), preferred_element_type=F32
    )


def shifted(value, steps):
    count = lax.axis_size(DP)
    return lax.ppermute(value, DP, [(i, (i + steps) % count) for i in range(count)])


def turned(value, steps):
    count = lax.axis_size("tensor")
    return lax.ppermute(value, "tensor", [(i, (i + steps) % count) for i in range(count)])


def exchanged(value, axis):
    return lax.all_to_all(value, axis, 0, 0, tiled=True)


def spread(value, axis):
    copies = lax.axis_size(axis)
    return exchanged(jnp.broadcast_to(value[None], (copies, *value.shape)), axis)


def slice_kernel(own_ref, sliced_ref):
    lanes = sliced_ref.shape[-1]
    for at in range(sliced_ref.shape[0]):
        sliced_ref[at] = own_ref[:, at * lanes : (at + 1) * lanes]


def suffix_kernel(out_grad_ref, layers_ref, grads_ref):
    count, _, lanes = layers_ref.shape
    quarters, _, rows, _ = grads_ref.shape
    at = pl.multiple_of(lax.axis_index("section") * lanes, lanes)
    base = out_grad_ref[:, pl.ds(at, lanes)].astype(F32)
    upper = None
    for layer in range(count - 1, -1, -1):
        own = layers_ref[layer].astype(F32)
        upper = own if upper is None else upper + own
        grads = (base + 0.25 * upper).astype(BF16)
        for quarter in range(quarters):
            grads_ref[quarter, layer] = grads[quarter * rows : (quarter + 1) * rows]


def prob_kernel(lengths_ref, query_ref, own_ref, near_ref, far_ref, prob_ref):
    rows, width = query_ref.shape
    window = (REACH + 1) * rows
    block = lax.axis_index(DP)
    first = block * rows
    place = first + lax.broadcasted_iota(jnp.int32, (rows, window), 0)
    keys = first - REACH * rows + lax.broadcasted_iota(jnp.int32, (rows, window), 1)
    narrow = first + lax.broadcasted_iota(jnp.int32, (rows, HD), 0)

    def advance(k, carry):
        end, start = carry
        end = end + lengths_ref[k]
        return end, jnp.where(narrow >= end, end, start)

    start = lax.fori_loop(
        0, lengths_ref.shape[0], advance, (jnp.int32(0), jnp.zeros((rows, HD), jnp.int32))
    )[1]
    start = jnp.concatenate([start] * (window // HD), axis=1)
    allowed = (keys <= place) & (keys >= start)
    for head in range(width // HD):
        cols = slice(head * HD, (head + 1) * HD)
        query = query_ref[:, cols]
        scores = jnp.concatenate(
            [contract(query, ref[0, :, cols], 1, 1) for ref in (far_ref, near_ref, own_ref)],
            axis=1,
        )
        scores = jnp.where(allowed, scores * HD ** (-0.5), -jnp.inf)
        top = jnp.max(scores, axis=-1, keepdims=True)
        weight = jnp.exp(scores - top)
        prob_ref[head] = weight / jnp.sum(weight, axis=-1, keepdims=True)


def grads_kernel(
    mine_ref, left_ref, right_ref, first_ref, second_ref,
    weight_ref, prob_ref, query_ref, own_ref, near_ref, far_ref, context_ref,
    query_grad_ref, own_part_ref, near_part_ref, far_part_ref, d_context_ref,
):
    quarter = mine_ref.shape[1]
    rows = query_ref.shape[0]
    count = rows // quarter
    held_rows = (
        (0, (mine_ref,)), (1, (right_ref,)), (count - 1, (left_ref,)),
        (2, (first_ref, second_ref)),
    )[: min(count, 4)]
    grad = jnp.concatenate(
        [
            jnp.concatenate([ref[at] for ref in refs for at in range(ref.shape[0])], axis=1)
            for _, refs in held_rows
        ],
        axis=0,
    )
    total = jnp.dot(grad, weight_ref[...], preferred_element_type=F32).astype(BF16)
    for index, (steps, _) in enumerate(held_rows):
        at = lax.rem(lax.axis_index("tensor") + steps, count) * quarter
        d_context_ref[pl.ds(pl.multiple_of(at, quarter), quarter), :] = total[
            index * quarter : (index + 1) * quarter
        ]
    d_context = d_context_ref[...]
    blocks = ((far_ref, far_part_ref), (near_ref, near_part_ref), (own_ref, own_part_ref))
    for head in range(query_ref.shape[1] // HD):
        cols = slice(head * HD, (head + 1) * HD)
        query = query_ref[:, cols]
        dctx = d_context[:, cols]
        delta = jnp.sum(
            dctx.astype(F32) * context_ref[:, cols].astype(F32), axis=-1, keepdims=True
        )
        query_grad = None
        for index, (held, part_ref) in enumerate(blocks):
            prob = prob_ref[head, :, index * rows : (index + 1) * rows]
            d_prob = contract(dctx, held[1, :, cols], 1, 1)
            d_score = (prob * (d_prob - delta) * HD ** (-0.5)).astype(BF16)
            term = jnp.dot(d_score, held[0, :, cols], preferred_element_type=F32)
            query_grad = term if query_grad is None else query_grad + term
            part_ref[0, :, cols] = contract(d_score, query, 0, 0).astype(part_ref.dtype)
            part_ref[1, :, cols] = contract(prob.astype(BF16), dctx, 0, 0).astype(part_ref.dtype)
        query_grad_ref[:, cols] = query_grad.astype(BF16)


def weight_kernel(grad_ref, context_ref, terms_ref):
    quarters, blocks, owners, rows, lanes = grad_ref.shape
    for owner in range(owners):
        total = None
        for quarter in range(quarters):
            grad = grad_ref[quarter, :, owner].reshape(blocks * rows, lanes)
            context = context_ref[:, quarter * rows : (quarter + 1) * rows, :]
            term = contract(grad, context.reshape(blocks * rows, context.shape[-1]), 0, 0)
            total = term if total is None else total + term
        terms_ref[owner] = total.astype(BF16)


def call(kernel, outs, inputs, specs, flops, nbytes, scratch=()):
    return pl.pallas_call(
        kernel,
        out_shape=outs,
        in_specs=specs,
        out_specs=[WHOLE] * len(outs),
        scratch_shapes=list(scratch),
        cost_estimate=pl.CostEstimate(flops=flops, bytes_accessed=nbytes, transcendentals=0),
        compiler_params=pltpu.CompilerParams(vmem_limit_bytes=28 * 2**20),
    )(*inputs)


def on_device(out_grad, section_out, context, queries, key_heads, values, o_weight, doc_lengths):
    rows, width = queries.shape[1:]
    features = out_grad.shape[1]
    sections, tensors, chips = (lax.axis_size(a) for a in ("section", "tensor", "zh"))
    owners = lax.axis_size(GROUP)
    heads = width // HD
    window = (REACH + 1) * rows
    lanes = features // sections
    quarter = rows // tensors
    pieces = sections * tensors
    shape = jax.ShapeDtypeStruct

    context_all = lax.all_gather(context[0], "zh")

    (sliced,) = call(
        slice_kernel,
        [shape((sections, rows, lanes), BF16)],
        (section_out[0],),
        [WHOLE],
        0,
        4 * rows * features,
    )
    layers = exchanged(sliced, "section")
    held = jnp.concatenate([key_heads, values], 0)
    near = shifted(held, 1)
    far = shifted(held, 2)
    (grads,) = call(
        suffix_kernel,
        [shape((tensors, sections, quarter, lanes), BF16)],
        (out_grad, layers),
        [WHOLE] * 2,
        layers.size * 3,
        layers.size * 4,
    )
    (prob,) = call(
        prob_kernel,
        [shape((heads, rows, window), F32)],
        (doc_lengths, queries[0], held, near, far),
        [SCALARS] + [WHOLE] * 4,
        heads * rows * window * (2 * HD + 10),
        heads * rows * window * 8,
    )
    mine = exchanged(grads.reshape(pieces, quarter, lanes), ("tensor", "section"))
    columns = exchanged(mine.reshape(chips, owners, quarter, lanes), "zh")
    half = pieces // 2
    from_left = turned(mine, 1)
    from_right = turned(mine, -1)
    far_first = turned(from_left[:half], 1)
    far_second = turned(from_right[half:], -1)
    columns_all = spread(columns, "tensor")

    query_grad, own_part, near_part, far_part = call(
        grads_kernel,
        [
            shape((rows, width), BF16),
            shape((2, rows, width), F32),
            shape((2, rows, width), BF16),
            shape((2, rows, width), BF16),
        ],
        (
            mine, from_left, from_right, far_first, far_second,
            o_weight[0], prob, queries[0], held, near, far, context[0],
        ),
        [WHOLE] * 12,
        2 * rows * features * tensors * width + 8 * rows * window * width,
        2 * features * tensors * width,
        [pltpu.VMEM((rows, width), BF16)],
    )
    near_back = shifted(near_part, -1)
    far_back = shifted(far_part, -2)
    sums = (own_part + near_back.astype(F32) + far_back.astype(F32)).astype(BF16)

    (terms,) = call(
        weight_kernel,
        [shape((owners, lanes, width), BF16)],
        (columns_all, context_all),
        [WHOLE] * 2,
        2 * columns_all.size * width,
        2 * (columns_all.size + context_all.size),
    )
    gathered = exchanged(terms, GROUP)
    weight_grad = jnp.sum(gathered.astype(F32), axis=0)
    return query_grad[None], sums[:1], sums[1:], weight_grad[None]


def solution(mesh):
    sections, shards, tensors = mesh.devices.shape
    split = Mesh(
        mesh.devices.reshape(sections, shards // (CORES * NEAR), NEAR, CORES, tensors),
        ("section", *DP, "tensor"),
    )
    placed = P("section", DP, "tensor")

    return jax.shard_map(
        on_device,
        mesh=split,
        in_specs=(
            P(DP, "tensor"), placed, placed, placed, placed, placed,
            P("section", None, "tensor"), P(),
        ),
        out_specs=(placed,) * 4,
        check_vma=False,
    )
```

time: 138 us -> 162 us (1.17)
  blocking collectives: 29 us -> 50.2 us
  waiting for transfers between devices: 33.9 us -> 38.9 us
  starting transfers between devices: 44.7 us -> 41.3 us
    all_to_all x2, blocking collectives: 29 us -> 50.2 us  [exchanged(): return lax.all_to_all(value, axis, 0, 0, tiled=True)]
    all_gather x1, waiting for transfers between devices: 0.02 us -> 21 us  [on_device(): context_all = lax.all_gather(context[0], 'zh')]
    ppermute x1 -> x4, starting transfers between devices: 1.92 us -> 13 us  [turned(): lax.ppermute(value, 'tensor', [(i, (i + steps) % count) for i in range(co...]
    ppermute x4, waiting for transfers between devices: 18.8 us -> 8.08 us  [shifted(): lax.ppermute(value, DP, [(i, (i + steps) % count) for i in range(count)])]
    all_to_all x3, starting transfers between devices: 29 us -> 19.7 us  [exchanged(): return lax.all_to_all(value, axis, 0, 0, tiled=True)]
    ppermute x4, starting transfers between devices: 13.7 us -> 8.61 us  [shifted(): lax.ppermute(value, DP, [(i, (i + steps) % count) for i in range(count)])]
    all_to_all x3, waiting for transfers between devices: 13.9 us -> 8.92 us  [exchanged(): return lax.all_to_all(value, axis, 0, 0, tiled=True)]
    pallas_call x4 -> x5, Pallas kernels: 5.79 us -> 7.38 us  [call(): pl.pallas_call(kernel, out_shape=outs, in_specs=specs, out_specs=[WHOLE]...]
  transfers between devices with their start and end apart: 9 -> 12, of which waited for: 7 -> 6; matrix products, arithmetic and copies ran while one was open for 3% -> 1% of each run, Pallas kernels for 4% -> 3%
where the time goes in v2:
time: 162 us; the launch traced here: 160 us
  blocking collectives  50.2 us (31%)
  starting transfers between devices  41.3 us (25%)
  waiting for transfers between devices  38.9 us (24%)
  between operations  14.2 us (9%)
  Pallas kernels  7.38 us (5%)
  local copies, waits for them, and re-layouts  7.29 us (4%)
    all_to_all x2, blocking collectives, exchanged(): return lax.all_to_all(value, axis, 0, 0, tiled=True)  50.2 us
    all_gather x1, waiting for transfers between devices, on_device(): context_all = lax.all_gather(context[0], 'zh')  21 us
    all_to_all x3, starting transfers between devices, exchanged(): return lax.all_to_all(value, axis, 0, 0, tiled=True)  19.7 us
    ppermute x4, starting transfers between devices, turned(): lax.ppermute(value, 'tensor', [(i, (i + steps) % count) for i in range(co...  13 us
    all_to_all x3, waiting for transfers between devices, exchanged(): return lax.all_to_all(value, axis, 0, 0, tiled=True)  8.92 us
    ppermute x4, starting transfers between devices, shifted(): lax.ppermute(value, DP, [(i, (i + steps) % count) for i in range(count)])  8.61 us
    ppermute x4, waiting for transfers between devices, shifted(): lax.ppermute(value, DP, [(i, (i + steps) % count) for i in range(count)])  8.08 us
    pallas_call x5, Pallas kernels, call(): pl.pallas_call(kernel, out_shape=outs, in_specs=specs, out_specs=[WHOLE]...  7.38 us
  transfers between devices with their start and end apart: 12, of which 6 were waited for; matrix products, arithmetic and copies ran while one was open for 1% of the time, Pallas kernels for 3%

profile of v2, /device:TPU:1, one launch (start us, length us, event | category | flops | bytes accessed | tf_op | source)
XLA Modules:
  0.0 160.2 jit_solution(18372932866331718205)
XLA Ops:
  7.2 0.9 copy-done.5
  8.2 16.8 %all_to_all.25.layers_ref = bf16[8,128,128]{2,1,0:T(8,128)(2,1)S(1)} all-to-all(bf16[8,128,128]{2,1,0:T(8,128)(2,1)S(1)} %shard_map.111), channel_id=1, replica_groups=mesh['section'=8,'zh'=8,'zl'=2,'core'=2,'tensor'=4] {'section'}, dimensions={0} | all-to-all | bytes 524288 | tf_op jit(solution)/shard_map/all_to_all | solution.py:38
  24.9 0.9 copy-done.4
  25.9 0.8 shard_map.112
  26.7 6.8 %all-to-all-start.1 = ((bf16[32,32,128]{2,1,0:T(8,128)(2,1)}), bf16[32,32,128]{2,1,0:T(8,128)(2,1)S(1)}, u32[]{:S(2)}, u32[]{:S(2)}) async-start(bf16[32,32,128]{2,1,0:T(8,128)(2,1)} %bitcast.1), calls=%async_computation.1 | async-start | bytes 524288 | tf_op jit(solution)/shard_map/all_to_all | solution.py:38
  33.6 0.7 all-gather.2.cloned.1.call-update
  34.3 8.9 %all-to-all-done.1.mine_ref = bf16[32,32,128]{2,1,0:T(8,128)(2,1)S(1)} async-done(((bf16[32,32,128]{2,1,0:T(8,128)(2,1)}), bf16[32,32,128]{2,1,0:T(8,128)(2,1)S(1)}, u32[]{:S(2)}, u32[]{:S(2)}) %all-to-all-start.1) | async-done | bytes 262176 | tf_op jit(solution)/shard_map/all_to_all | solution.py:38
  43.2 33.5 %all_to_all.26 = bf16[8,4,32,128]{3,2,1,0:T(8,128)(2,1)S(1)} all-to-all(bf16[8,4,32,128]{3,2,1,0:T(8,128)(2,1)S(1)} %bitcast.9), channel_id=1, replica_groups=mesh['section'=8,'zh'=8,'zl'=2,'core'=2,'tensor'=4] {'zh'}, dimensions={0} | all-to-all | bytes 524288 | tf_op jit(solution)/shard_map/all_to_all | solution.py:38
  76.6 1.2 broadcast_in_dim.13
  77.8 4.5 %all-to-all-start.3 = ((bf16[4,8,4,32,128]{4,3,2,1,0:T(8,128)(2,1)}), bf16[4,8,4,32,128]{4,3,2,1,0:T(8,128)(2,1)S(1)}, u32[]{:S(2)}, u32[]{:S(2)}) async-start(bf16[4,8,4,32,128]{4,3,2,1,0:T(8,128)(2,1)} %broadcast_in_dim.13), calls=%async_computation.3 | async-start | bytes 2097152 | tf_op jit(solution)/shard_map/all_to_all | solution.py:38
  82.3 21.0 %all-gather.2.cloned.1.call-done.context_ref = bf16[8,128,512]{2,1,0:T(8,128)(2,1)} async-done(((bf16[1,128,512]{2,1,0:T(8,128)(2,1)}), bf16[8,128,512]{2,1,0:T(8,128)(2,1)}) %all-gather.2.cloned.1.call-update) | async-done | bytes 1048592 | tf_op jit(solution)/shard_map/all_gather | solution.py:180
  103.3 1.2 copy-done.1
  104.6 1.5 shard_map.115
  106.1 8.4 %all-to-all-start.4 = ((bf16[4,128,512]{2,1,0:T(8,128)(2,1)}), bf16[4,128,512]{2,1,0:T(8,128)(2,1)S(1)}, u32[]{:S(2)}, u32[]{:S(2)}) async-start(bf16[4,128,512]{2,1,0:T(8,128)(2,1)} %shard_map.115), calls=%async_computation.4 | async-start | bytes 1048576 | tf_op jit(solution)/shard_map/all_to_all | solution.py:38
  114.5 2.8 %collective-permute-start = (bf16[32,32,128]{2,1,0:T(8,128)(2,1)S(1)}, bf16[32,32,128]{2,1,0:T(8,128)(2,1)S(1)}, u32[]{:S(2)}, u32[]{:S(2)}) collective-permute-start(bf16[32,32,128]{2,1,0:T(8,128)(2,1)S(1)} %all-to-all-done.1.mine_ref), channel_id=1, source_target_pairs={{0,1},{1,2},{2,3},{3,0},{4,5},{5,6},{6,7},{7,4},{8,9},{9,10},{10,1... | collective-permute-start | bytes 786440 | tf_op jit(solution)/shard_map/ppermute | solution.py:34
  117.3 3.7 %collective-permute-start.1 = (bf16[32,32,128]{2,1,0:T(8,128)(2,1)S(1)}, bf16[32,32,128]{2,1,0:T(8,128)(2,1)S(1)}, u32[]{:S(2)}, u32[]{:S(2)}) collective-permute-start(bf16[32,32,128]{2,1,0:T(8,128)(2,1)S(1)} %all-to-all-done.1.mine_ref), channel_id=1, source_target_pairs={{0,3},{1,0},{2,1},{3,2},{4,7},{5,4},{6,5},{7,6},{8,11},{9,8},{10,9... | collective-permute-start | bytes 786440 | tf_op jit(solution)/shard_map/ppermute | solution.py:34
  121.0 2.2 %collective-permute-start.4 = (bf16[2,128,512]{2,1,0:T(8,128)(2,1)S(1)}, bf16[2,128,512]{2,1,0:T(8,128)(2,1)S(1)}, u32[]{:S(2)}, u32[]{:S(2)}) collective-permute-start(bf16[2,128,512]{2,1,0:T(8,128)(2,1)S(1)} %constant_dynamic-update-slice_fusion.own_ref), channel_id=1, source_target_pairs={{0,4},{4,8},{8,12},{12,16},{16,20},{20,24},{24,28},{28,32},{32,36}... | collective-permute-start | bytes 786440 | tf_op jit(solution)/shard_map/ppermute | solution.py:29
  123.2 1.9 %collective-permute-start.5 = (bf16[2,128,512]{2,1,0:T(8,128)(2,1)S(1)}, bf16[2,128,512]{2,1,0:T(8,128)(2,1)S(1)}, u32[]{:S(2)}, u32[]{:S(2)}) collective-permute-start(bf16[2,128,512]{2,1,0:T(8,128)(2,1)S(1)} %constant_dynamic-update-slice_fusion.own_ref), channel_id=1, source_target_pairs={{0,8},{4,12},{8,16},{12,20},{16,24},{20,28},{24,32},{28,36},{32,40... | collective-permute-start | bytes 786440 | tf_op jit(solution)/shard_map/ppermute | solution.py:29
  125.2 0.2 collective-permute-done.left_ref
  125.4 1.9 %collective-permute-start.2 = (bf16[16,32,128]{2,1,0:T(8,128)(2,1)S(1)}, bf16[16,32,128]{2,1,0:T(8,128)(2,1)S(1)}, u32[]{:S(2)}, u32[]{:S(2)}) collective-permute-start(bf16[16,32,128]{2,1,0:T(8,128)(2,1)S(1)} %slice.16), channel_id=1, source_target_pairs={{0,1},{1,2},{2,3},{3,0},{4,5},{5,6},{6,7},{7,4},{8,9},{9,10},{10,1... | collective-permute-start | bytes 393224 | tf_op jit(solution)/shard_map/ppermute | solution.py:34
  127.4 4.6 %collective-permute-start.3 = (bf16[16,32,128]{2,1,0:T(8,128)(2,1)S(1)}, bf16[16,32,128]{2,1,0:T(8,128)(2,1)S(1)}, u32[]{:S(2)}, u32[]{:S(2)}) collective-permute-start(bf16[16,32,128]{2,1,0:T(8,128)(2,1)S(1)} %slice.17), channel_id=1, source_target_pairs={{0,3},{1,0},{2,1},{3,2},{4,7},{5,4},{6,5},{7,6},{8,11},{9,8},{10,9... | collective-permute-start | bytes 393224 | tf_op jit(solution)/shard_map/ppermute | solution.py:34
  131.9 1.9 %collective-permute-done.5.far_ref = bf16[2,128,512]{2,1,0:T(8,128)(2,1)S(1)} collective-permute-done((bf16[2,128,512]{2,1,0:T(8,128)(2,1)S(1)}, bf16[2,128,512]{2,1,0:T(8,128)(2,1)S(1)}, u32[]{:S(2)}, u32[]{:S(2)}) %collective-permute-start.5) | collective-permute-done | bytes 262176 | tf_op jit(solution)/shard_map/ppermute | solution.py:29
  133.9 1.5 shard_map.113.prob_ref
  135.5 2.2 %copy-done = bf16[1,4096,512]{2,1,0:T(8,128)(2,1)S(1)} copy-done((bf16[1,4096,512]{2,1,0:T(8,128)(2,1)S(1)}, bf16[1,4096,512]{2,1,0:T(8,128)(2,1)}, u32[]{:S(2)}) %copy-start) | copy-done | bytes 4194328
  137.7 3.5 %shard_map.114 = (bf16[128,512]{1,0:T(8,128)(2,1)}, f32[2,128,512]{2,1,0:T(8,128)S(1)}, bf16[2,128,512]{2,1,0:T(8,128)(2,1)S(1)}, bf16[2,128,512]{2,1,0:T(8,128)(2,1)S(1)}) custom-call(bf16[32,32,128]{2,1,0:T(8,128)(2,1)S(1)} %all-to-all-done.1.mine_ref, bf16[32,32,128]{2,1,0:T(8,128)(2,1)S(1)} %collective-permute-done.left_ref, ...), custom_call_target="tpu_custom_call" | custom-call | flops 738197504 | bytes 4194304 | tf_op jit(solution)/shard_map/pallas_call | solution.py:157
  141.1 0.4 collective-permute-start.6
  141.6 4.1 %collective-permute-start.7 = (bf16[2,128,512]{2,1,0:T(8,128)(2,1)S(1)}, bf16[2,128,512]{2,1,0:T(8,128)(2,1)S(1)}, u32[]{:S(2)}, u32[]{:S(2)}) collective-permute-start(bf16[2,128,512]{2,1,0:T(8,128)(2,1)S(1)} %get-tuple-element.11), channel_id=1, source_target_pairs={{0,120},{4,124},{8,0},{12,4},{16,8},{20,12},{24,16},{28,20},{32,24... | collective-permute-start | bytes 786440 | tf_op jit(solution)/shard_map/ppermute | solution.py:29
  145.6 2.4 %collective-permute-done.6 = bf16[2,128,512]{2,1,0:T(8,128)(2,1)S(1)} collective-permute-done((bf16[2,128,512]{2,1,0:T(8,128)(2,1)S(1)}, bf16[2,128,512]{2,1,0:T(8,128)(2,1)S(1)}, u32[]{:S(2)}, u32[]{:S(2)}) %collective-permute-start.6) | collective-permute-done | bytes 262176 | tf_op jit(solution)/shard_map/ppermute | solution.py:29
  148.0 3.8 %collective-permute-done.7 = bf16[2,128,512]{2,1,0:T(8,128)(2,1)S(1)} collective-permute-done((bf16[2,128,512]{2,1,0:T(8,128)(2,1)S(1)}, bf16[2,128,512]{2,1,0:T(8,128)(2,1)S(1)}, u32[]{:S(2)}, u32[]{:S(2)}) %collective-permute-start.7) | collective-permute-done | bytes 262176 | tf_op jit(solution)/shard_map/ppermute | solution.py:29
  151.8 0.1 add_convert_fusion
  151.9 0.7 fusion
  152.6 0.8 convert_reduce_fusion
  (26 shorter events, 0.2 us)
Async XLA Ops:
  7.2 1.0 copy-start.5
  24.9 1.0 copy-start.4
  26.7 94.3 %copy-start.7 = (bf16[1,128,512]{2,1,0:T(8,128)(2,1)S(1)}, bf16[1,128,512]{2,1,0:T(8,128)(2,1)}, u32[]{:S(2)}) copy-start(bf16[1,128,512]{2,1,0:T(8,128)(2,1)} %param.12) | copy-start | bytes 393220
  26.7 94.3 %copy-start.8 = (bf16[1,128,512]{2,1,0:T(8,128)(2,1)S(1)}, bf16[1,128,512]{2,1,0:T(8,128)(2,1)}, u32[]{:S(2)}) copy-start(bf16[1,128,512]{2,1,0:T(8,128)(2,1)} %param.13) | copy-start | bytes 393220
  26.7 16.5 %all-to-all-start.1 = ((bf16[32,32,128]{2,1,0:T(8,128)(2,1)}), bf16[32,32,128]{2,1,0:T(8,128)(2,1)S(1)}, u32[]{:S(2)}, u32[]{:S(2)}) async-start(bf16[32,32,128]{2,1,0:T(8,128)(2,1)} %bitcast.1), calls=%async_computation.1 | async-start | bytes 524288 | tf_op jit(solution)/shard_map/all_to_all | solution.py:38
  33.5 69.8 %all-gather.2.cloned.1.call-start = ((), (), s32[]{:S(2)}) async-start(), calls=%async_computation.5 | async-start | bytes 1179648 | tf_op jit(solution)/shard_map/all_gather | solution.py:180
  76.6 57.3 %copy-start.2 = (bf16[1,128,512]{2,1,0:T(8,128)(2,1)S(1)}, bf16[1,128,512]{2,1,0:T(8,128)(2,1)}, u32[]{:S(2)}) copy-start(bf16[1,128,512]{2,1,0:T(8,128)(2,1)} %param.11) | copy-start | bytes 393220
  76.6 57.3 %copy-start.6 = (s32[32]{0:T(128)S(1)}, s32[32]{0:T(128)}, u32[]{:S(2)}) copy-start(s32[32]{0:T(128)} %lengths_ref.1) | copy-start | bytes 388
  77.8 57.6 %copy-start.3 = (bf16[1,128,512]{2,1,0:T(8,128)(2,1)S(1)}, bf16[1,128,512]{2,1,0:T(8,128)(2,1)}, u32[]{:S(2)}) copy-start(bf16[1,128,512]{2,1,0:T(8,128)(2,1)} %param.10) | copy-start | bytes 393220
  77.8 25.5 %all-to-all-start.3 = ((bf16[4,8,4,32,128]{4,3,2,1,0:T(8,128)(2,1)}), bf16[4,8,4,32,128]{4,3,2,1,0:T(8,128)(2,1)S(1)}, u32[]{:S(2)}, u32[]{:S(2)}) async-start(bf16[4,8,4,32,128]{4,3,2,1,0:T(8,128)(2,1)} %broadcast_in_dim.13), calls=%async_computation.3 | async-start | bytes 2097152 | tf_op jit(solution)/shard_map/all_to_all | solution.py:38
  103.3 1.2 copy-start.1
  106.1 46.5 %all-to-all-start.4 = ((bf16[4,128,512]{2,1,0:T(8,128)(2,1)}), bf16[4,128,512]{2,1,0:T(8,128)(2,1)S(1)}, u32[]{:S(2)}, u32[]{:S(2)}) async-start(bf16[4,128,512]{2,1,0:T(8,128)(2,1)} %shard_map.115), calls=%async_computation.4 | async-start | bytes 1048576 | tf_op jit(solution)/shard_map/all_to_all | solution.py:38
  114.5 10.9 %collective-permute-start = (bf16[32,32,128]{2,1,0:T(8,128)(2,1)S(1)}, bf16[32,32,128]{2,1,0:T(8,128)(2,1)S(1)}, u32[]{:S(2)}, u32[]{:S(2)}) collective-permute-start(bf16[32,32,128]{2,1,0:T(8,128)(2,1)S(1)} %all-to-all-done.1.mine_ref), channel_id=1, source_target_pairs={{0,1},{1,2},{2,3},{3,0},{4,5},{5,6},{6,7},{7,4},{8,9},{9,10},{10,1... | collective-permute-start | bytes 786440 | tf_op jit(solution)/shard_map/ppermute | solution.py:34
  117.3 10.1 %collective-permute-start.1 = (bf16[32,32,128]{2,1,0:T(8,128)(2,1)S(1)}, bf16[32,32,128]{2,1,0:T(8,128)(2,1)S(1)}, u32[]{:S(2)}, u32[]{:S(2)}) collective-permute-start(bf16[32,32,128]{2,1,0:T(8,128)(2,1)S(1)} %all-to-all-done.1.mine_ref), channel_id=1, source_target_pairs={{0,3},{1,0},{2,1},{3,2},{4,7},{5,4},{6,5},{7,6},{8,11},{9,8},{10,9... | collective-permute-start | bytes 786440 | tf_op jit(solution)/shard_map/ppermute | solution.py:34
  121.0 10.9 %collective-permute-start.4 = (bf16[2,128,512]{2,1,0:T(8,128)(2,1)S(1)}, bf16[2,128,512]{2,1,0:T(8,128)(2,1)S(1)}, u32[]{:S(2)}, u32[]{:S(2)}) collective-permute-start(bf16[2,128,512]{2,1,0:T(8,128)(2,1)S(1)} %constant_dynamic-update-slice_fusion.own_ref), channel_id=1, source_target_pairs={{0,4},{4,8},{8,12},{12,16},{16,20},{20,24},{24,28},{28,32},{32,36}... | collective-permute-start | bytes 786440 | tf_op jit(solution)/shard_map/ppermute | solution.py:29
  123.2 10.6 %collective-permute-start.5 = (bf16[2,128,512]{2,1,0:T(8,128)(2,1)S(1)}, bf16[2,128,512]{2,1,0:T(8,128)(2,1)S(1)}, u32[]{:S(2)}, u32[]{:S(2)}) collective-permute-start(bf16[2,128,512]{2,1,0:T(8,128)(2,1)S(1)} %constant_dynamic-update-slice_fusion.own_ref), channel_id=1, source_target_pairs={{0,8},{4,12},{8,16},{12,20},{16,24},{20,28},{24,32},{28,36},{32,40... | collective-permute-start | bytes 786440 | tf_op jit(solution)/shard_map/ppermute | solution.py:29
  125.4 10.1 %collective-permute-start.2 = (bf16[16,32,128]{2,1,0:T(8,128)(2,1)S(1)}, bf16[16,32,128]{2,1,0:T(8,128)(2,1)S(1)}, u32[]{:S(2)}, u32[]{:S(2)}) collective-permute-start(bf16[16,32,128]{2,1,0:T(8,128)(2,1)S(1)} %slice.16), channel_id=1, source_target_pairs={{0,1},{1,2},{2,3},{3,0},{4,5},{5,6},{6,7},{7,4},{8,9},{9,10},{10,1... | collective-permute-start | bytes 393224 | tf_op jit(solution)/shard_map/ppermute | solution.py:34
  127.4 8.1 %collective-permute-start.3 = (bf16[16,32,128]{2,1,0:T(8,128)(2,1)S(1)}, bf16[16,32,128]{2,1,0:T(8,128)(2,1)S(1)}, u32[]{:S(2)}, u32[]{:S(2)}) collective-permute-start(bf16[16,32,128]{2,1,0:T(8,128)(2,1)S(1)} %slice.17), channel_id=1, source_target_pairs={{0,3},{1,0},{2,1},{3,2},{4,7},{5,4},{6,5},{7,6},{8,11},{9,8},{10,9... | collective-permute-start | bytes 393224 | tf_op jit(solution)/shard_map/ppermute | solution.py:34
  135.5 2.2 %copy-start = (bf16[1,4096,512]{2,1,0:T(8,128)(2,1)S(1)}, bf16[1,4096,512]{2,1,0:T(8,128)(2,1)}, u32[]{:S(2)}) copy-start(bf16[1,4096,512]{2,1,0:T(8,128)(2,1)} %param.14) | copy-start | bytes 12582916
  141.1 6.9 %collective-permute-start.6 = (bf16[2,128,512]{2,1,0:T(8,128)(2,1)S(1)}, bf16[2,128,512]{2,1,0:T(8,128)(2,1)S(1)}, u32[]{:S(2)}, u32[]{:S(2)}) collective-permute-start(bf16[2,128,512]{2,1,0:T(8,128)(2,1)S(1)} %get-tuple-element.10), channel_id=1, source_target_pairs={{0,124},{4,0},{8,4},{12,8},{16,12},{20,16},{24,20},{28,24},{32,28}... | collective-permute-start | bytes 786440 | tf_op jit(solution)/shard_map/ppermute | solution.py:29
  141.6 10.2 %collective-permute-start.7 = (bf16[2,128,512]{2,1,0:T(8,128)(2,1)S(1)}, bf16[2,128,512]{2,1,0:T(8,128)(2,1)S(1)}, u32[]{:S(2)}, u32[]{:S(2)}) collective-permute-start(bf16[2,128,512]{2,1,0:T(8,128)(2,1)S(1)} %get-tuple-element.11), channel_id=1, source_target_pairs={{0,120},{4,124},{8,0},{12,4},{16,8},{20,12},{24,16},{28,20},{32,24... | collective-permute-start | bytes 786440 | tf_op jit(solution)/shard_map/ppermute | solution.py:29
Sparse Core Ops, SparseCore 0:
  37.0 66.2 all-gather.1

commit v3 on v2

--- a/solution.py
+++ b/solution.py
@@ -13,7 +13,7 @@
 F32 = jnp.float32
 BF16 = jnp.bfloat16
 WHOLE = pl.BlockSpec(memory_space=pltpu.VMEM)
-SCALARS = pl.BlockSpec(memory_space=pltpu.SMEM)
+RAW = pl.BlockSpec(memory_space=pltpu.HBM)
 DP = ("zh", "zl", "core")
 GROUP = ("zl", "core")
 
@@ -29,9 +29,14 @@
     return lax.ppermute(value, DP, [(i, (i + steps) % count) for i in range(count)])
 
 
-def turned(value, steps):
-    count = lax.axis_size("tensor")
-    return lax.ppermute(value, "tensor", [(i, (i + steps) % count) for i in range(count)])
+def turned(value, axis, steps):
+    count = lax.axis_size(axis)
+    return lax.ppermute(value, axis, [(i, (i + steps) % count) for i in range(count)])
+
+
+def swapped(value, mask):
+    count = lax.axis_size(GROUP)
+    return lax.ppermute(value, GROUP, [(i, i ^ mask) for i in range(count)])
 
 
 def exchanged(value, axis):
@@ -43,17 +48,41 @@
     return exchanged(jnp.broadcast_to(value[None], (copies, *value.shape)), axis)
 
 
-def slice_kernel(own_ref, sliced_ref):
-    lanes = sliced_ref.shape[-1]
-    for at in range(sliced_ref.shape[0]):
-        sliced_ref[at] = own_ref[:, at * lanes : (at + 1) * lanes]
-
-
-def suffix_kernel(out_grad_ref, layers_ref, grads_ref):
-    count, _, lanes = layers_ref.shape
+def copy_all(copies):
+    for copy in copies:
+        copy.start()
+    for copy in copies:
+        copy.wait()
+
+
+def slice_kernel(own_ref, sliced_ref, sems):
+    count, _, lanes = sliced_ref.shape
+    copy_all(
+        [
+            pltpu.make_async_copy(
+                own_ref.at[:, pl.ds(at * lanes, lanes)], sliced_ref.at[at], sems.at[at]
+            )
+            for at in range(count)
+        ]
+    )
+
+
+def pack_kernel(keys_ref, values_ref, out_grad_ref, held_ref, base_ref, sems):
+    lanes = base_ref.shape[1]
+    at = pl.multiple_of(lax.axis_index("section") * lanes, lanes)
+    copy_all(
+        [
+            pltpu.make_async_copy(keys_ref.at[0], held_ref.at[0], sems.at[0]),
+            pltpu.make_async_copy(values_ref.at[0], held_ref.at[1], sems.at[1]),
+            pltpu.make_async_copy(out_grad_ref.at[:, pl.ds(at, lanes)], base_ref, sems.at[2]),
+        ]
+    )
+
+
+def suffix_kernel(base_ref, layers_ref, grads_ref):
+    count = layers_ref.shape[0]
     quarters, _, rows, _ = grads_ref.shape
-    at = pl.multiple_of(lax.axis_index("section") * lanes, lanes)
-    base = out_grad_ref[:, pl.ds(at, lanes)].astype(F32)
+    base = base_ref[...].astype(F32)
     upper = None
     for layer in range(count - 1, -1, -1):
         own = layers_ref[layer].astype(F32)
@@ -63,7 +92,14 @@
             grads_ref[quarter, layer] = grads[quarter * rows : (quarter + 1) * rows]
 
 
-def prob_kernel(lengths_ref, query_ref, own_ref, near_ref, far_ref, prob_ref):
+def prob_kernel(
+    lengths_hbm, query_hbm, own_ref, near_ref, far_ref,
+    prob_ref, lengths_ref, query_ref, sems,
+):
+    lengths_copy = pltpu.make_async_copy(lengths_hbm, lengths_ref, sems.at[0])
+    query_copy = pltpu.make_async_copy(query_hbm.at[0], query_ref, sems.at[1])
+    lengths_copy.start()
+    query_copy.start()
     rows, width = query_ref.shape
     window = (REACH + 1) * rows
     block = lax.axis_index(DP)
@@ -77,11 +113,13 @@
         end = end + lengths_ref[k]
         return end, jnp.where(narrow >= end, end, start)
 
+    lengths_copy.wait()
     start = lax.fori_loop(
         0, lengths_ref.shape[0], advance, (jnp.int32(0), jnp.zeros((rows, HD), jnp.int32))
     )[1]
     start = jnp.concatenate([start] * (window // HD), axis=1)
     allowed = (keys <= place) & (keys >= start)
+    query_copy.wait()
     for head in range(width // HD):
         cols = slice(head * HD, (head + 1) * HD)
         query = query_ref[:, cols]
@@ -96,25 +134,45 @@
 
 
 def grads_kernel(
-    mine_ref, left_ref, right_ref, first_ref, second_ref,
-    weight_ref, prob_ref, query_ref, own_ref, near_ref, far_ref, context_ref,
-    query_grad_ref, own_part_ref, near_part_ref, far_part_ref, d_context_ref,
+    mine_ref, left_ref, right_ref, across_ref,
+    weight_hbm, prob_ref, query_ref, own_ref, near_ref, far_ref, context_ref,
+    query_grad_ref, own_part_ref, near_part_ref, far_part_ref,
+    d_context_ref, weight_ref, sems,
 ):
-    quarter = mine_ref.shape[1]
+    pieces, quarter, lanes = mine_ref.shape
     rows = query_ref.shape[0]
     count = rows // quarter
-    held_rows = (
-        (0, (mine_ref,)), (1, (right_ref,)), (count - 1, (left_ref,)),
-        (2, (first_ref, second_ref)),
-    )[: min(count, 4)]
-    grad = jnp.concatenate(
-        [
-            jnp.concatenate([ref[at] for ref in refs for at in range(ref.shape[0])], axis=1)
-            for _, refs in held_rows
-        ],
-        axis=0,
-    )
-    total = jnp.dot(grad, weight_ref[...], preferred_element_type=F32).astype(BF16)
+    held_rows = ((0, mine_ref), (1, right_ref), (count - 1, left_ref), (2, across_ref))[:count]
+    chunks = sems.shape[0]
+    step = pieces // chunks
+    depth = step * lanes
+    copies = [
+        pltpu.make_async_copy(
+            weight_hbm.at[0, pl.ds(chunk * depth, depth)],
+            weight_ref.at[pl.ds(chunk * depth, depth)],
+            sems.at[chunk],
+        )
+        for chunk in range(chunks)
+    ]
+    for copy in copies:
+        copy.start()
+    total = None
+    for chunk in range(chunks):
+        grad = jnp.concatenate(
+            [
+                jnp.concatenate(
+                    [ref[at] for at in range(chunk * step, (chunk + 1) * step)], axis=1
+                )
+                for _, ref in held_rows
+            ],
+            axis=0,
+        )
+        copies[chunk].wait()
+        term = jnp.dot(
+            grad, weight_ref[chunk * depth : (chunk + 1) * depth, :], preferred_element_type=F32
+        )
+        total = term if total is None else total + term
+    total = total.astype(BF16)
     for index, (steps, _) in enumerate(held_rows):
         at = lax.rem(lax.axis_index("tensor") + steps, count) * quarter
         d_context_ref[pl.ds(pl.multiple_of(at, quarter), quarter), :] = total[
@@ -141,16 +199,32 @@
         query_grad_ref[:, cols] = query_grad.astype(BF16)
 
 
-def weight_kernel(grad_ref, context_ref, terms_ref):
-    quarters, blocks, owners, rows, lanes = grad_ref.shape
-    for owner in range(owners):
+def weight_kernel(grad_ref, *refs):
+    quarters, blocks, owners, rows, _ = grad_ref.shape
+    context_refs, term_refs = refs[:blocks], refs[blocks:]
+    here, me = lax.axis_index("zh"), lax.axis_index(GROUP)
+    places = [lax.rem(here + steps, blocks) for steps in ring_steps(blocks)]
+    contexts = [
+        jnp.concatenate([ref[quarter * rows : (quarter + 1) * rows] for ref in context_refs], axis=0)
+        for quarter in range(quarters)
+    ]
+    for mask in range(owners):
+        owner = jnp.bitwise_xor(me, mask)
         total = None
         for quarter in range(quarters):
-            grad = grad_ref[quarter, :, owner].reshape(blocks * rows, lanes)
-            context = context_ref[:, quarter * rows : (quarter + 1) * rows, :]
-            term = contract(grad, context.reshape(blocks * rows, context.shape[-1]), 0, 0)
+            grad = jnp.concatenate([grad_ref[quarter, at, owner] for at in places], axis=0)
+            term = contract(grad, contexts[quarter], 0, 0)
             total = term if total is None else total + term
-        terms_ref[owner] = total.astype(BF16)
+        term_refs[mask][...] = total.astype(term_refs[mask].dtype)
+
+
+def ring_steps(count):
+    steps = [0]
+    for hop in range(1, count // 2 + 1):
+        steps.append(count - hop)
+        if hop < count - hop:
+            steps.append(hop)
+    return steps
 
 
 def call(kernel, outs, inputs, specs, flops, nbytes, scratch=()):
@@ -160,9 +234,14 @@
         in_specs=specs,
         out_specs=[WHOLE] * len(outs),
         scratch_shapes=list(scratch),
+        compiler_params=pltpu.CompilerParams(vmem_limit_bytes=24 * 2**20),
         cost_estimate=pl.CostEstimate(flops=flops, bytes_accessed=nbytes, transcendentals=0),
-        compiler_params=pltpu.CompilerParams(vmem_limit_bytes=28 * 2**20),
-    )(*inputs)
+    )(
+        *(
+            pltpu.with_memory_space_constraint(value, pltpu.HBM) if spec is RAW else value
+            for value, spec in zip(inputs, specs)
+        )
+    )
 
 
 def on_device(out_grad, section_out, context, queries, key_heads, values, o_weight, doc_lengths):
@@ -177,43 +256,58 @@
     pieces = sections * tensors
     shape = jax.ShapeDtypeStruct
 
-    context_all = lax.all_gather(context[0], "zh")
-
     (sliced,) = call(
         slice_kernel,
         [shape((sections, rows, lanes), BF16)],
         (section_out[0],),
-        [WHOLE],
+        [RAW],
         0,
         4 * rows * features,
+        [pltpu.SemaphoreType.DMA((sections,))],
     )
     layers = exchanged(sliced, "section")
-    held = jnp.concatenate([key_heads, values], 0)
+    held, base = call(
+        pack_kernel,
+        [shape((2, rows, width), BF16), shape((rows, lanes), BF16)],
+        (key_heads, values, out_grad),
+        [RAW] * 3,
+        0,
+        8 * rows * width,
+        [pltpu.SemaphoreType.DMA((3,))],
+    )
+    blocks = [context[0]]
+    for hop in range(1, chips // 2 + 1):
+        blocks.append(turned(blocks[max(len(blocks) - 2, 0)], "zh", 1))
+        if hop < chips - hop:
+            blocks.append(turned(blocks[max(len(blocks) - 2, 0)], "zh", -1))
     near = shifted(held, 1)
     far = shifted(held, 2)
     (grads,) = call(
         suffix_kernel,
         [shape((tensors, sections, quarter, lanes), BF16)],
-        (out_grad, layers),
+        (base, layers),
         [WHOLE] * 2,
         layers.size * 3,
         layers.size * 4,
     )
+    mine = exchanged(grads.reshape(pieces, quarter, lanes), ("tensor", "section"))
     (prob,) = call(
         prob_kernel,
         [shape((heads, rows, window), F32)],
-        (doc_lengths, queries[0], held, near, far),
-        [SCALARS] + [WHOLE] * 4,
+        (doc_lengths, queries, held, near, far),
+        [RAW] * 2 + [WHOLE] * 3,
         heads * rows * window * (2 * HD + 10),
         heads * rows * window * 8,
-    )
-    mine = exchanged(grads.reshape(pieces, quarter, lanes), ("tensor", "section"))
+        [
+            pltpu.SMEM(doc_lengths.shape, jnp.int32),
+            pltpu.VMEM((rows, width), BF16),
+            pltpu.SemaphoreType.DMA((2,)),
+        ],
+    )
     columns = exchanged(mine.reshape(chips, owners, quarter, lanes), "zh")
-    half = pieces // 2
-    from_left = turned(mine, 1)
-    from_right = turned(mine, -1)
-    far_first = turned(from_left[:half], 1)
-    far_second = turned(from_right[half:], -1)
+    from_left = turned(mine, "tensor", 1)
+    from_right = turned(mine, "tensor", -1)
+    across = turned(from_left, "tensor", 1)
     columns_all = spread(columns, "tensor")
 
     query_grad, own_part, near_part, far_part = call(
@@ -225,28 +319,33 @@
             shape((2, rows, width), BF16),
         ],
         (
-            mine, from_left, from_right, far_first, far_second,
-            o_weight[0], prob, queries[0], held, near, far, context[0],
+            mine, from_left, from_right, across,
+            o_weight, prob, queries[0], held, near, far, context[0],
         ),
-        [WHOLE] * 12,
+        [WHOLE] * 4 + [RAW] + [WHOLE] * 6,
         2 * rows * features * tensors * width + 8 * rows * window * width,
         2 * features * tensors * width,
-        [pltpu.VMEM((rows, width), BF16)],
+        [
+            pltpu.VMEM((rows, width), BF16),
+            pltpu.VMEM(o_weight.shape[1:], BF16),
+            pltpu.SemaphoreType.DMA((4,)),
+        ],
     )
     near_back = shifted(near_part, -1)
     far_back = shifted(far_part, -2)
     sums = (own_part + near_back.astype(F32) + far_back.astype(F32)).astype(BF16)
 
-    (terms,) = call(
+    weight_grad, *terms = call(
         weight_kernel,
-        [shape((owners, lanes, width), BF16)],
-        (columns_all, context_all),
-        [WHOLE] * 2,
+        [shape((lanes, width), F32)] + [shape((lanes, width), BF16)] * (owners - 1),
+        (columns_all, *blocks),
+        [WHOLE] * (1 + chips),
         2 * columns_all.size * width,
-        2 * (columns_all.size + context_all.size),
-    )
-    gathered = exchanged(terms, GROUP)
-    weight_grad = jnp.sum(gathered.astype(F32), axis=0)
+        2 * (columns_all.size + chips * context.size),
+    )
+    for mask in range(1, owners):
+        other = swapped(terms[mask - 1], mask)
+        weight_grad = weight_grad + other.astype(F32)
     return query_grad[None], sums[:1], sums[1:], weight_grad[None]
 
 

time: 162 us -> 150 us (0.926)
  starting transfers between devices: 41.3 us -> 94 us
  blocking collectives: 50.2 us -> 16.3 us
  waiting for transfers between devices: 38.9 us -> 23.1 us
  between operations: 14.2 us -> 0.91 us
  local copies, waits for them, and re-layouts: 7.29 us -> 1.98 us
  Pallas kernels: 7.38 us -> 11.4 us
    ppermute x4 -> x13, starting transfers between devices: 13 us -> 48.4 us  [the longest x10 35 us: turned(): lax.ppermute(value, axis, [(i, (i + steps) % count) for i in range(count)])]
    all_to_all x2 -> x1, blocking collectives: 50.2 us -> 16.3 us  [exchanged(): return lax.all_to_all(value, axis, 0, 0, tiled=True)]
    all_gather x1 -> x0, waiting for transfers between devices: 21 us -> none  [on_device(): context_all = lax.all_gather(context[0], 'zh')]
    ppermute x4 -> x13, waiting for transfers between devices: 0.23 us -> 14.8 us  [the longest x10 13.8 us: turned(): lax.ppermute(value, axis, [(i, (i + steps) % count) for i in range(count)])]
    all_to_all x3, starting transfers between devices: 19.7 us -> 30.1 us  [exchanged(): return lax.all_to_all(value, axis, 0, 0, tiled=True)]
    ppermute x4, waiting for transfers between devices: 8.08 us -> 0.01 us  [shifted(): lax.ppermute(value, DP, [(i, (i + steps) % count) for i in range(count)])]
    ppermute x4, starting transfers between devices: 8.61 us -> 15.6 us  [shifted(): lax.ppermute(value, DP, [(i, (i + steps) % count) for i in range(count)])]
    unnamed x19 -> x4, local copies, waits for them, and re-layouts: 5.33 us -> 0.01 us
  transfers between devices with their start and end apart: 12 -> 20, of which waited for: 6 -> 6; matrix products, arithmetic and copies ran while one was open for 1% -> 1% of each run, Pallas kernels for 3% -> 6%
where the time goes in v3:
time: 150 us; the launch traced here: 149 us
  starting transfers between devices  94 us (63%)
  waiting for transfers between devices  23.1 us (15%)
  blocking collectives  16.3 us (11%)
  Pallas kernels  11.4 us (8%)
  local copies, waits for them, and re-layouts  1.98 us (1%)
    ppermute x10, starting transfers between devices, turned(): lax.ppermute(value, axis, [(i, (i + steps) % count) for i in range(count)])  35 us
    all_to_all x3, starting transfers between devices, exchanged(): return lax.all_to_all(value, axis, 0, 0, tiled=True)  30.1 us
    all_to_all x1, blocking collectives, exchanged(): return lax.all_to_all(value, axis, 0, 0, tiled=True)  16.3 us
    ppermute x4, starting transfers between devices, shifted(): lax.ppermute(value, DP, [(i, (i + steps) % count) for i in range(count)])  15.6 us
    ppermute x10, waiting for transfers between devices, turned(): lax.ppermute(value, axis, [(i, (i + steps) % count) for i in range(count)])  13.8 us
    ppermute x3, starting transfers between devices, swapped(): return lax.ppermute(value, GROUP, [(i, i ^ mask) for i in range(count)])  13.4 us
    pallas_call x6, Pallas kernels, call(): pl.pallas_call(kernel, out_shape=outs, in_specs=specs, out_specs=[WHOLE]...  11.4 us
    all_to_all x3, waiting for transfers between devices, exchanged(): return lax.all_to_all(value, axis, 0, 0, tiled=True)  8.34 us
  transfers between devices with their start and end apart: 20, of which 6 were waited for; matrix products, arithmetic and copies ran while one was open for 1% of the time, Pallas kernels for 6%

profile of v3, /device:TPU:1, one launch (start us, length us, event | category | flops | bytes accessed | tf_op | source)
XLA Modules:
  0.0 148.6 jit_solution(2888950799215646133)
XLA Ops:
  0.7 1.7 %shard_map.112 = bf16[8,128,128]{2,1,0:T(8,128)(2,1)} custom-call(bf16[128,1024]{1,0:T(8,128)(2,1)} %bitcast.14), custom_call_target="tpu_custom_call" | custom-call | bytes 524288 | tf_op jit(solution)/shard_map/pallas_call | solution.py:231
  2.3 7.7 %all-to-all-start = ((bf16[8,128,128]{2,1,0:T(8,128)(2,1)}), bf16[8,128,128]{2,1,0:T(8,128)(2,1)S(1)}, u32[]{:S(2)}, u32[]{:S(2)}) async-start(bf16[8,128,128]{2,1,0:T(8,128)(2,1)} %shard_map.112), calls=%async_computation | async-start | bytes 524288 | tf_op jit(solution)/shard_map/all_to_all | solution.py:43
  10.0 1.0 shard_map.111
  11.0 8.3 %all-to-all-done.layers_ref = bf16[8,128,128]{2,1,0:T(8,128)(2,1)S(1)} async-done(((bf16[8,128,128]{2,1,0:T(8,128)(2,1)}), bf16[8,128,128]{2,1,0:T(8,128)(2,1)S(1)}, u32[]{:S(2)}, u32[]{:S(2)}) %all-to-all-start) | async-done | bytes 262176 | tf_op jit(solution)/shard_map/all_to_all | solution.py:43
  19.4 16.3 %all_to_all.20.mine_ref = bf16[32,32,128]{2,1,0:T(8,128)(2,1)} all-to-all(bf16[32,32,128]{2,1,0:T(8,128)(2,1)S(1)} %bitcast.8), channel_id=1, replica_groups=mesh['section'=8,'zh'=8,'zl'=2,'core'=2,'tensor'=4] {'tensor','section'}, dimensions={0} | all-to-all | bytes 524288 | tf_op jit(solution)/shard_map/all_to_all | solution.py:43
  35.7 18.5 %all-to-all-start.2 = ((bf16[8,4,32,128]{3,2,1,0:T(8,128)(2,1)}), bf16[8,4,32,128]{3,2,1,0:T(8,128)(2,1)S(1)}, u32[]{:S(2)}, u32[]{:S(2)}) async-start(bf16[8,4,32,128]{3,2,1,0:T(8,128)(2,1)} %bitcast.5), calls=%async_computation.2 | async-start | bytes 524288 | tf_op jit(solution)/shard_map/all_to_all | solution.py:43
  54.1 2.5 %collective-permute-start = (bf16[32,32,128]{2,1,0:T(8,128)(2,1)}, bf16[32,32,128]{2,1,0:T(8,128)(2,1)S(1)}, u32[]{:S(2)}, u32[]{:S(2)}) collective-permute-start(bf16[32,32,128]{2,1,0:T(8,128)(2,1)} %all_to_all.20.mine_ref), channel_id=1, source_target_pairs={{0,1},{1,2},{2,3},{3,0},{4,5},{5,6},{6,7},{7,4},{8,9},{9,10},{10,1... | collective-permute-start | bytes 786440 | tf_op jit(solution)/shard_map/ppermute | solution.py:34
  56.7 5.0 %collective-permute-start.3 = (bf16[2,128,512]{2,1,0:T(8,128)(2,1)S(1)}, bf16[2,128,512]{2,1,0:T(8,128)(2,1)S(1)}, u32[]{:S(2)}, u32[]{:S(2)}) collective-permute-start(bf16[2,128,512]{2,1,0:T(8,128)(2,1)S(1)} %get-tuple-element.15.own_ref), channel_id=1, source_target_pairs={{0,4},{4,8},{8,12},{12,16},{16,20},{20,24},{24,28},{28,32},{32,36}... | collective-permute-start | bytes 786440 | tf_op jit(solution)/shard_map/ppermute | solution.py:29
  61.7 3.6 %collective-permute-start.4 = (bf16[2,128,512]{2,1,0:T(8,128)(2,1)S(1)}, bf16[2,128,512]{2,1,0:T(8,128)(2,1)S(1)}, u32[]{:S(2)}, u32[]{:S(2)}) collective-permute-start(bf16[2,128,512]{2,1,0:T(8,128)(2,1)S(1)} %get-tuple-element.15.own_ref), channel_id=1, source_target_pairs={{0,8},{4,12},{8,16},{12,20},{16,24},{20,28},{24,32},{28,36},{32,40... | collective-permute-start | bytes 786440 | tf_op jit(solution)/shard_map/ppermute | solution.py:29
  65.3 4.3 %collective-permute-start.1 = (bf16[32,32,128]{2,1,0:T(8,128)(2,1)}, bf16[32,32,128]{2,1,0:T(8,128)(2,1)S(1)}, u32[]{:S(2)}, u32[]{:S(2)}) collective-permute-start(bf16[32,32,128]{2,1,0:T(8,128)(2,1)} %all_to_all.20.mine_ref), channel_id=1, source_target_pairs={{0,3},{1,0},{2,1},{3,2},{4,7},{5,4},{6,5},{7,6},{8,11},{9,8},{10,9... | collective-permute-start | bytes 786440 | tf_op jit(solution)/shard_map/ppermute | solution.py:34
  69.6 1.9 %collective-permute-start.2 = (bf16[32,32,128]{2,1,0:T(8,128)(2,1)S(1)}, bf16[32,32,128]{2,1,0:T(8,128)(2,1)S(1)}, u32[]{:S(2)}, u32[]{:S(2)}) collective-permute-start(bf16[32,32,128]{2,1,0:T(8,128)(2,1)S(1)} %collective-permute-done.left_ref), channel_id=1, source_target_pairs={{0,1},{1,2},{2,3},{3,0},{4,5},{5,6},{6,7},{7,4},{8,9},{9,10},{10,1... | collective-permute-start | bytes 786440 | tf_op jit(solution)/shard_map/ppermute | solution.py:34
  71.5 1.3 broadcast_in_dim.13
  72.8 3.9 %all-to-all-start.3 = ((bf16[4,8,4,32,128]{4,3,2,1,0:T(8,128)(2,1)}), bf16[4,8,4,32,128]{4,3,2,1,0:T(8,128)(2,1)S(1)}, u32[]{:S(2)}, u32[]{:S(2)}) async-start(bf16[4,8,4,32,128]{4,3,2,1,0:T(8,128)(2,1)} %broadcast_in_dim.13), calls=%async_computation.3 | async-start | bytes 2097152 | tf_op jit(solution)/shard_map/all_to_all | solution.py:43
  76.7 5.2 %collective-permute-start.7 = (bf16[128,512]{1,0:T(8,128)(2,1)S(1)}, bf16[128,512]{1,0:T(8,128)(2,1)S(1)}, u32[]{:S(2)}, u32[]{:S(2)}) collective-permute-start(bf16[128,512]{1,0:T(8,128)(2,1)S(1)} %bitcast.10), channel_id=1, source_target_pairs={{0,16},{16,32},{32,48},{48,64},{64,80},{80,96},{96,112},{112,0},{1... | collective-permute-start | bytes 393224 | tf_op jit(solution)/shard_map/ppermute | solution.py:34
  81.9 3.9 %collective-permute-done.7.refs_1_ = bf16[128,512]{1,0:T(8,128)(2,1)S(1)} collective-permute-done((bf16[128,512]{1,0:T(8,128)(2,1)S(1)}, bf16[128,512]{1,0:T(8,128)(2,1)S(1)}, u32[]{:S(2)}, u32[]{:S(2)}) %collective-permute-start.7) | collective-permute-done | bytes 131104 | tf_op jit(solution)/shard_map/ppermute | solution.py:34
  85.8 2.1 %collective-permute-start.8 = (bf16[128,512]{1,0:T(8,128)(2,1)S(1)}, bf16[128,512]{1,0:T(8,128)(2,1)S(1)}, u32[]{:S(2)}, u32[]{:S(2)}) collective-permute-start(bf16[128,512]{1,0:T(8,128)(2,1)S(1)} %bitcast.11), channel_id=1, source_target_pairs={{0,112},{16,0},{32,16},{48,32},{64,48},{80,64},{96,80},{112,96},{1... | collective-permute-start | bytes 393224 | tf_op jit(solution)/shard_map/ppermute | solution.py:34
  87.9 5.9 %collective-permute-start.9 = (bf16[128,512]{1,0:T(8,128)(2,1)S(1)}, bf16[128,512]{1,0:T(8,128)(2,1)S(1)}, u32[]{:S(2)}, u32[]{:S(2)}) collective-permute-start(bf16[128,512]{1,0:T(8,128)(2,1)S(1)} %collective-permute-done.7.refs_1_), channel_id=1, source_target_pairs={{0,16},{16,32},{32,48},{48,64},{64,80},{80,96},{96,112},{112,0},{1... | collective-permute-start | bytes 393224 | tf_op jit(solution)/shard_map/ppermute | solution.py:34
  93.8 1.7 %shard_map.114.prob_ref = f32[4,128,384]{2,1,0:T(8,128)S(1)} custom-call(s32[32]{0:T(128)} %lengths_hbm.1, bf16[1,128,512]{2,1,0:T(8,128)(2,1)} %query_hbm.1, bf16[2,128,512]{2,1,0:T(8,128)(2,1)S(1)} %get-tuple-element.15.own_ref, bf16[2,128,512]{2,1,0:T(8,128)(2,1)S(1)} %collective-permute-done.3.near_ref, ...), custom_call_target="tpu_custom_call" | custom-call | flops 52297728 | bytes 1572864 | tf_op jit(solution)/shard_map/pallas_call | solution.py:231
  95.6 6.2 %shard_map.115 = (bf16[128,512]{1,0:T(8,128)(2,1)}, f32[2,128,512]{2,1,0:T(8,128)S(1)}, bf16[2,128,512]{2,1,0:T(8,128)(2,1)S(1)}, bf16[2,128,512]{2,1,0:T(8,128)(2,1)S(1)}) custom-call(bf16[32,32,128]{2,1,0:T(8,128)(2,1)} %all_to_all.20.mine_ref, bf16[32,32,128]{2,1,0:T(8,128)(2,1)S(1)} %collective-permute-done.left_ref, ...), custom_call_target="tpu_custom_call" | custom-call | flops 738197504 | bytes 4194304 | tf_op jit(solution)/shard_map/pallas_call | solution.py:231
  101.8 2.4 %collective-permute-start.6 = (bf16[2,128,512]{2,1,0:T(8,128)(2,1)S(1)}, bf16[2,128,512]{2,1,0:T(8,128)(2,1)S(1)}, u32[]{:S(2)}, u32[]{:S(2)}) collective-permute-start(bf16[2,128,512]{2,1,0:T(8,128)(2,1)S(1)} %get-tuple-element.19), channel_id=1, source_target_pairs={{0,120},{4,124},{8,0},{12,4},{16,8},{20,12},{24,16},{28,20},{32,24... | collective-permute-start | bytes 786440 | tf_op jit(solution)/shard_map/ppermute | solution.py:29
  104.2 4.6 %collective-permute-start.5 = (bf16[2,128,512]{2,1,0:T(8,128)(2,1)S(1)}, bf16[2,128,512]{2,1,0:T(8,128)(2,1)S(1)}, u32[]{:S(2)}, u32[]{:S(2)}) collective-permute-start(bf16[2,128,512]{2,1,0:T(8,128)(2,1)S(1)} %get-tuple-element.18), channel_id=1, source_target_pairs={{0,124},{4,0},{8,4},{12,8},{16,12},{20,16},{24,20},{28,24},{32,28}... | collective-permute-start | bytes 786440 | tf_op jit(solution)/shard_map/ppermute | solution.py:29
  108.8 3.7 %collective-permute-start.10 = (bf16[128,512]{1,0:T(8,128)(2,1)S(1)}, bf16[128,512]{1,0:T(8,128)(2,1)S(1)}, u32[]{:S(2)}, u32[]{:S(2)}) collective-permute-start(bf16[128,512]{1,0:T(8,128)(2,1)S(1)} %collective-permute-done.8.refs_2_), channel_id=1, source_target_pairs={{0,112},{16,0},{32,16},{48,32},{64,48},{80,64},{96,80},{112,96},{1... | collective-permute-start | bytes 393224 | tf_op jit(solution)/shard_map/ppermute | solution.py:34
  112.5 2.4 %collective-permute-start.11 = (bf16[128,512]{1,0:T(8,128)(2,1)S(1)}, bf16[128,512]{1,0:T(8,128)(2,1)S(1)}, u32[]{:S(2)}, u32[]{:S(2)}) collective-permute-start(bf16[128,512]{1,0:T(8,128)(2,1)S(1)} %collective-permute-done.9.refs_3_), channel_id=1, source_target_pairs={{0,16},{16,32},{32,48},{48,64},{64,80},{80,96},{96,112},{112,0},{1... | collective-permute-start | bytes 393224 | tf_op jit(solution)/shard_map/ppermute | solution.py:34
  115.0 2.4 %collective-permute-done.10.refs_4_ = bf16[128,512]{1,0:T(8,128)(2,1)S(1)} collective-permute-done((bf16[128,512]{1,0:T(8,128)(2,1)S(1)}, bf16[128,512]{1,0:T(8,128)(2,1)S(1)}, u32[]{:S(2)}, u32[]{:S(2)}) %collective-permute-start.10) | collective-permute-done | bytes 131104 | tf_op jit(solution)/shard_map/ppermute | solution.py:34
  117.4 5.0 %collective-permute-start.12 = (bf16[128,512]{1,0:T(8,128)(2,1)S(1)}, bf16[128,512]{1,0:T(8,128)(2,1)S(1)}, u32[]{:S(2)}, u32[]{:S(2)}) collective-permute-start(bf16[128,512]{1,0:T(8,128)(2,1)S(1)} %collective-permute-done.10.refs_4_), channel_id=1, source_target_pairs={{0,112},{16,0},{32,16},{48,32},{64,48},{80,64},{96,80},{112,96},{1... | collective-permute-start | bytes 393224 | tf_op jit(solution)/shard_map/ppermute | solution.py:34
  122.3 1.7 %collective-permute-done.11.refs_5_ = bf16[128,512]{1,0:T(8,128)(2,1)S(1)} collective-permute-done((bf16[128,512]{1,0:T(8,128)(2,1)S(1)}, bf16[128,512]{1,0:T(8,128)(2,1)S(1)}, u32[]{:S(2)}, u32[]{:S(2)}) %collective-permute-start.11) | collective-permute-done | bytes 131104 | tf_op jit(solution)/shard_map/ppermute | solution.py:34
  124.0 1.9 %collective-permute-start.13 = (bf16[128,512]{1,0:T(8,128)(2,1)S(1)}, bf16[128,512]{1,0:T(8,128)(2,1)S(1)}, u32[]{:S(2)}, u32[]{:S(2)}) collective-permute-start(bf16[128,512]{1,0:T(8,128)(2,1)S(1)} %collective-permute-done.11.refs_5_), channel_id=1, source_target_pairs={{0,16},{16,32},{32,48},{48,64},{64,80},{80,96},{96,112},{112,0},{1... | collective-permute-start | bytes 393224 | tf_op jit(solution)/shard_map/ppermute | solution.py:34
  126.1 5.8 %collective-permute-done.13.refs_7_ = bf16[128,512]{1,0:T(8,128)(2,1)S(1)} collective-permute-done((bf16[128,512]{1,0:T(8,128)(2,1)S(1)}, bf16[128,512]{1,0:T(8,128)(2,1)S(1)}, u32[]{:S(2)}, u32[]{:S(2)}) %collective-permute-start.13) | collective-permute-done | bytes 131104 | tf_op jit(solution)/shard_map/ppermute | solution.py:34
  132.7 9.2 %collective-permute-start.16 = (bf16[128,512]{1,0:T(8,128)(2,1)S(1)}, bf16[128,512]{1,0:T(8,128)(2,1)S(1)}, u32[]{:S(2)}, u32[]{:S(2)}) collective-permute-start(bf16[128,512]{1,0:T(8,128)(2,1)S(1)} %get-tuple-element.23), channel_id=1, source_target_pairs={{0,12},{4,8},{8,4},{12,0},{1,13},{5,9},{9,5},{13,1},{2,14},{6,10},... | collective-permute-start | bytes 393224 | tf_op jit(solution)/shard_map/ppermute | solution.py:39
  141.8 1.9 %collective-permute-start.15 = (bf16[128,512]{1,0:T(8,128)(2,1)S(1)}, bf16[128,512]{1,0:T(8,128)(2,1)S(1)}, u32[]{:S(2)}, u32[]{:S(2)}) collective-permute-start(bf16[128,512]{1,0:T(8,128)(2,1)S(1)} %get-tuple-element.22), channel_id=1, source_target_pairs={{0,8},{4,12},{8,0},{12,4},{1,9},{5,13},{9,1},{13,5},{2,10},{6,14},... | collective-permute-start | bytes 393224 | tf_op jit(solution)/shard_map/ppermute | solution.py:39
  143.8 2.3 %collective-permute-start.14 = (bf16[128,512]{1,0:T(8,128)(2,1)S(1)}, bf16[128,512]{1,0:T(8,128)(2,1)S(1)}, u32[]{:S(2)}, u32[]{:S(2)}) collective-permute-start(bf16[128,512]{1,0:T(8,128)(2,1)S(1)} %get-tuple-element.21), channel_id=1, source_target_pairs={{0,4},{4,0},{8,12},{12,8},{1,5},{5,1},{9,13},{13,9},{2,6},{6,2},{1... | collective-permute-start | bytes 393224 | tf_op jit(solution)/shard_map/ppermute | solution.py:39
  146.8 1.0 collective-permute-done.15
  (23 shorter events, 2.5 us)
Async XLA Ops:
  0.6 76.1 %copy-start.1 = (bf16[1,128,512]{2,1,0:T(8,128)(2,1)S(1)}, bf16[1,128,512]{2,1,0:T(8,128)(2,1)}, u32[]{:S(2)}) copy-start(bf16[1,128,512]{2,1,0:T(8,128)(2,1)} %param.10) | copy-start | bytes 393220
  0.6 94.9 %copy-start = (bf16[1,128,512]{2,1,0:T(8,128)(2,1)S(1)}, bf16[1,128,512]{2,1,0:T(8,128)(2,1)}, u32[]{:S(2)}) copy-start(bf16[1,128,512]{2,1,0:T(8,128)(2,1)} %query_hbm.1) | copy-start | bytes 393220
  2.3 17.0 %all-to-all-start = ((bf16[8,128,128]{2,1,0:T(8,128)(2,1)}), bf16[8,128,128]{2,1,0:T(8,128)(2,1)S(1)}, u32[]{:S(2)}, u32[]{:S(2)}) async-start(bf16[8,128,128]{2,1,0:T(8,128)(2,1)} %shard_map.112), calls=%async_computation | async-start | bytes 524288 | tf_op jit(solution)/shard_map/all_to_all | solution.py:43
  35.7 35.8 %all-to-all-start.2 = ((bf16[8,4,32,128]{3,2,1,0:T(8,128)(2,1)}), bf16[8,4,32,128]{3,2,1,0:T(8,128)(2,1)S(1)}, u32[]{:S(2)}, u32[]{:S(2)}) async-start(bf16[8,4,32,128]{3,2,1,0:T(8,128)(2,1)} %bitcast.5), calls=%async_computation.2 | async-start | bytes 524288 | tf_op jit(solution)/shard_map/all_to_all | solution.py:43
  54.1 15.4 %collective-permute-start = (bf16[32,32,128]{2,1,0:T(8,128)(2,1)}, bf16[32,32,128]{2,1,0:T(8,128)(2,1)S(1)}, u32[]{:S(2)}, u32[]{:S(2)}) collective-permute-start(bf16[32,32,128]{2,1,0:T(8,128)(2,1)} %all_to_all.20.mine_ref), channel_id=1, source_target_pairs={{0,1},{1,2},{2,3},{3,0},{4,5},{5,6},{6,7},{7,4},{8,9},{9,10},{10,1... | collective-permute-start | bytes 786440 | tf_op jit(solution)/shard_map/ppermute | solution.py:34
  56.7 31.2 %collective-permute-start.3 = (bf16[2,128,512]{2,1,0:T(8,128)(2,1)S(1)}, bf16[2,128,512]{2,1,0:T(8,128)(2,1)S(1)}, u32[]{:S(2)}, u32[]{:S(2)}) collective-permute-start(bf16[2,128,512]{2,1,0:T(8,128)(2,1)S(1)} %get-tuple-element.15.own_ref), channel_id=1, source_target_pairs={{0,4},{4,8},{8,12},{12,16},{16,20},{20,24},{24,28},{28,32},{32,36}... | collective-permute-start | bytes 786440 | tf_op jit(solution)/shard_map/ppermute | solution.py:29
  61.7 32.2 %collective-permute-start.4 = (bf16[2,128,512]{2,1,0:T(8,128)(2,1)S(1)}, bf16[2,128,512]{2,1,0:T(8,128)(2,1)S(1)}, u32[]{:S(2)}, u32[]{:S(2)}) collective-permute-start(bf16[2,128,512]{2,1,0:T(8,128)(2,1)S(1)} %get-tuple-element.15.own_ref), channel_id=1, source_target_pairs={{0,8},{4,12},{8,16},{12,20},{16,24},{20,28},{24,32},{28,36},{32,40... | collective-permute-start | bytes 786440 | tf_op jit(solution)/shard_map/ppermute | solution.py:29
  65.3 30.2 %collective-permute-start.1 = (bf16[32,32,128]{2,1,0:T(8,128)(2,1)}, bf16[32,32,128]{2,1,0:T(8,128)(2,1)S(1)}, u32[]{:S(2)}, u32[]{:S(2)}) collective-permute-start(bf16[32,32,128]{2,1,0:T(8,128)(2,1)} %all_to_all.20.mine_ref), channel_id=1, source_target_pairs={{0,3},{1,0},{2,1},{3,2},{4,7},{5,4},{6,5},{7,6},{8,11},{9,8},{10,9... | collective-permute-start | bytes 786440 | tf_op jit(solution)/shard_map/ppermute | solution.py:34
  69.6 26.0 %collective-permute-start.2 = (bf16[32,32,128]{2,1,0:T(8,128)(2,1)S(1)}, bf16[32,32,128]{2,1,0:T(8,128)(2,1)S(1)}, u32[]{:S(2)}, u32[]{:S(2)}) collective-permute-start(bf16[32,32,128]{2,1,0:T(8,128)(2,1)S(1)} %collective-permute-done.left_ref), channel_id=1, source_target_pairs={{0,1},{1,2},{2,3},{3,0},{4,5},{5,6},{6,7},{7,4},{8,9},{9,10},{10,1... | collective-permute-start | bytes 786440 | tf_op jit(solution)/shard_map/ppermute | solution.py:34
  72.8 59.1 %all-to-all-start.3 = ((bf16[4,8,4,32,128]{4,3,2,1,0:T(8,128)(2,1)}), bf16[4,8,4,32,128]{4,3,2,1,0:T(8,128)(2,1)S(1)}, u32[]{:S(2)}, u32[]{:S(2)}) async-start(bf16[4,8,4,32,128]{4,3,2,1,0:T(8,128)(2,1)} %broadcast_in_dim.13), calls=%async_computation.3 | async-start | bytes 2097152 | tf_op jit(solution)/shard_map/all_to_all | solution.py:43
  76.7 9.1 %collective-permute-start.7 = (bf16[128,512]{1,0:T(8,128)(2,1)S(1)}, bf16[128,512]{1,0:T(8,128)(2,1)S(1)}, u32[]{:S(2)}, u32[]{:S(2)}) collective-permute-start(bf16[128,512]{1,0:T(8,128)(2,1)S(1)} %bitcast.10), channel_id=1, source_target_pairs={{0,16},{16,32},{32,48},{48,64},{64,80},{80,96},{96,112},{112,0},{1... | collective-permute-start | bytes 393224 | tf_op jit(solution)/shard_map/ppermute | solution.py:34
  85.8 23.0 %collective-permute-start.8 = (bf16[128,512]{1,0:T(8,128)(2,1)S(1)}, bf16[128,512]{1,0:T(8,128)(2,1)S(1)}, u32[]{:S(2)}, u32[]{:S(2)}) collective-permute-start(bf16[128,512]{1,0:T(8,128)(2,1)S(1)} %bitcast.11), channel_id=1, source_target_pairs={{0,112},{16,0},{32,16},{48,32},{64,48},{80,64},{96,80},{112,96},{1... | collective-permute-start | bytes 393224 | tf_op jit(solution)/shard_map/ppermute | solution.py:34
  87.9 24.6 %collective-permute-start.9 = (bf16[128,512]{1,0:T(8,128)(2,1)S(1)}, bf16[128,512]{1,0:T(8,128)(2,1)S(1)}, u32[]{:S(2)}, u32[]{:S(2)}) collective-permute-start(bf16[128,512]{1,0:T(8,128)(2,1)S(1)} %collective-permute-done.7.refs_1_), channel_id=1, source_target_pairs={{0,16},{16,32},{32,48},{48,64},{64,80},{80,96},{96,112},{112,0},{1... | collective-permute-start | bytes 393224 | tf_op jit(solution)/shard_map/ppermute | solution.py:34
  101.8 24.1 %collective-permute-start.6 = (bf16[2,128,512]{2,1,0:T(8,128)(2,1)S(1)}, bf16[2,128,512]{2,1,0:T(8,128)(2,1)S(1)}, u32[]{:S(2)}, u32[]{:S(2)}) collective-permute-start(bf16[2,128,512]{2,1,0:T(8,128)(2,1)S(1)} %get-tuple-element.19), channel_id=1, source_target_pairs={{0,120},{4,124},{8,0},{12,4},{16,8},{20,12},{24,16},{28,20},{32,24... | collective-permute-start | bytes 786440 | tf_op jit(solution)/shard_map/ppermute | solution.py:29
  104.2 21.7 %collective-permute-start.5 = (bf16[2,128,512]{2,1,0:T(8,128)(2,1)S(1)}, bf16[2,128,512]{2,1,0:T(8,128)(2,1)S(1)}, u32[]{:S(2)}, u32[]{:S(2)}) collective-permute-start(bf16[2,128,512]{2,1,0:T(8,128)(2,1)S(1)} %get-tuple-element.18), channel_id=1, source_target_pairs={{0,124},{4,0},{8,4},{12,8},{16,12},{20,16},{24,20},{28,24},{32,28}... | collective-permute-start | bytes 786440 | tf_op jit(solution)/shard_map/ppermute | solution.py:29
  108.8 8.6 %collective-permute-start.10 = (bf16[128,512]{1,0:T(8,128)(2,1)S(1)}, bf16[128,512]{1,0:T(8,128)(2,1)S(1)}, u32[]{:S(2)}, u32[]{:S(2)}) collective-permute-start(bf16[128,512]{1,0:T(8,128)(2,1)S(1)} %collective-permute-done.8.refs_2_), channel_id=1, source_target_pairs={{0,112},{16,0},{32,16},{48,32},{64,48},{80,64},{96,80},{112,96},{1... | collective-permute-start | bytes 393224 | tf_op jit(solution)/shard_map/ppermute | solution.py:34
  112.5 11.5 %collective-permute-start.11 = (bf16[128,512]{1,0:T(8,128)(2,1)S(1)}, bf16[128,512]{1,0:T(8,128)(2,1)S(1)}, u32[]{:S(2)}, u32[]{:S(2)}) collective-permute-start(bf16[128,512]{1,0:T(8,128)(2,1)S(1)} %collective-permute-done.9.refs_3_), channel_id=1, source_target_pairs={{0,16},{16,32},{32,48},{48,64},{64,80},{80,96},{96,112},{112,0},{1... | collective-permute-start | bytes 393224 | tf_op jit(solution)/shard_map/ppermute | solution.py:34
  117.4 8.7 %collective-permute-start.12 = (bf16[128,512]{1,0:T(8,128)(2,1)S(1)}, bf16[128,512]{1,0:T(8,128)(2,1)S(1)}, u32[]{:S(2)}, u32[]{:S(2)}) collective-permute-start(bf16[128,512]{1,0:T(8,128)(2,1)S(1)} %collective-permute-done.10.refs_4_), channel_id=1, source_target_pairs={{0,112},{16,0},{32,16},{48,32},{64,48},{80,64},{96,80},{112,96},{1... | collective-permute-start | bytes 393224 | tf_op jit(solution)/shard_map/ppermute | solution.py:34
  124.0 7.9 %collective-permute-start.13 = (bf16[128,512]{1,0:T(8,128)(2,1)S(1)}, bf16[128,512]{1,0:T(8,128)(2,1)S(1)}, u32[]{:S(2)}, u32[]{:S(2)}) collective-permute-start(bf16[128,512]{1,0:T(8,128)(2,1)S(1)} %collective-permute-done.11.refs_5_), channel_id=1, source_target_pairs={{0,16},{16,32},{32,48},{48,64},{64,80},{80,96},{96,112},{112,0},{1... | collective-permute-start | bytes 393224 | tf_op jit(solution)/shard_map/ppermute | solution.py:34
  132.7 14.1 %collective-permute-start.16 = (bf16[128,512]{1,0:T(8,128)(2,1)S(1)}, bf16[128,512]{1,0:T(8,128)(2,1)S(1)}, u32[]{:S(2)}, u32[]{:S(2)}) collective-permute-start(bf16[128,512]{1,0:T(8,128)(2,1)S(1)} %get-tuple-element.23), channel_id=1, source_target_pairs={{0,12},{4,8},{8,4},{12,0},{1,13},{5,9},{9,5},{13,1},{2,14},{6,10},... | collective-permute-start | bytes 393224 | tf_op jit(solution)/shard_map/ppermute | solution.py:39
  141.8 6.0 %collective-permute-start.15 = (bf16[128,512]{1,0:T(8,128)(2,1)S(1)}, bf16[128,512]{1,0:T(8,128)(2,1)S(1)}, u32[]{:S(2)}, u32[]{:S(2)}) collective-permute-start(bf16[128,512]{1,0:T(8,128)(2,1)S(1)} %get-tuple-element.22), channel_id=1, source_target_pairs={{0,8},{4,12},{8,0},{12,4},{1,9},{5,13},{9,1},{13,5},{2,10},{6,14},... | collective-permute-start | bytes 393224 | tf_op jit(solution)/shard_map/ppermute | solution.py:39
  143.8 4.0 %collective-permute-start.14 = (bf16[128,512]{1,0:T(8,128)(2,1)S(1)}, bf16[128,512]{1,0:T(8,128)(2,1)S(1)}, u32[]{:S(2)}, u32[]{:S(2)}) collective-permute-start(bf16[128,512]{1,0:T(8,128)(2,1)S(1)} %get-tuple-element.21), channel_id=1, source_target_pairs={{0,4},{4,0},{8,12},{12,8},{1,5},{5,1},{9,13},{13,9},{2,6},{6,2},{1... | collective-permute-start | bytes 393224 | tf_op jit(solution)/shard_map/ppermute | solution.py:39

commit v4 on v3

--- a/solution.py
+++ b/solution.py
@@ -1,3 +1,5 @@
+import functools
+
 import jax
 import jax.numpy as jnp
 from jax import lax
@@ -55,41 +57,36 @@
         copy.wait()
 
 
-def slice_kernel(own_ref, sliced_ref, sems):
-    count, _, lanes = sliced_ref.shape
-    copy_all(
-        [
-            pltpu.make_async_copy(
-                own_ref.at[:, pl.ds(at * lanes, lanes)], sliced_ref.at[at], sems.at[at]
-            )
-            for at in range(count)
-        ]
-    )
-
-
 def pack_kernel(keys_ref, values_ref, out_grad_ref, held_ref, base_ref, sems):
-    lanes = base_ref.shape[1]
-    at = pl.multiple_of(lax.axis_index("section") * lanes, lanes)
+    rows = base_ref.shape[0]
+    at = pl.multiple_of(lax.axis_index("section") * rows, rows)
     copy_all(
         [
             pltpu.make_async_copy(keys_ref.at[0], held_ref.at[0], sems.at[0]),
             pltpu.make_async_copy(values_ref.at[0], held_ref.at[1], sems.at[1]),
-            pltpu.make_async_copy(out_grad_ref.at[:, pl.ds(at, lanes)], base_ref, sems.at[2]),
+            pltpu.make_async_copy(out_grad_ref.at[pl.ds(at, rows), :], base_ref, sems.at[2]),
         ]
     )
 
 
 def suffix_kernel(base_ref, layers_ref, grads_ref):
-    count = layers_ref.shape[0]
-    quarters, _, rows, _ = grads_ref.shape
     base = base_ref[...].astype(F32)
     upper = None
-    for layer in range(count - 1, -1, -1):
+    for layer in range(layers_ref.shape[0] - 1, -1, -1):
         own = layers_ref[layer].astype(F32)
         upper = own if upper is None else upper + own
         grads = (base + 0.25 * upper).astype(BF16)
-        for quarter in range(quarters):
-            grads_ref[quarter, layer] = grads[quarter * rows : (quarter + 1) * rows]
+        for copy in range(grads_ref.shape[0]):
+            grads_ref[copy, layer] = grads
+
+
+def quarter_kernel(grad_ref, mine_ref):
+    blocks, rows, lanes = mine_ref.shape
+    each = blocks // grad_ref.shape[0]
+    at = pl.multiple_of(lax.axis_index("tensor") * rows, rows)
+    for block in range(blocks):
+        first = block % each * lanes
+        mine_ref[block] = grad_ref[block // each, pl.ds(at, rows), first : first + lanes]
 
 
 def prob_kernel(
@@ -134,51 +131,31 @@
 
 
 def grads_kernel(
-    mine_ref, left_ref, right_ref, across_ref,
-    weight_hbm, prob_ref, query_ref, own_ref, near_ref, far_ref, context_ref,
+    grad_ref, weight_hbm, prob_ref, query_ref, own_ref, near_ref, far_ref, context_ref,
     query_grad_ref, own_part_ref, near_part_ref, far_part_ref,
-    d_context_ref, weight_ref, sems,
+    weight_ref, sems,
 ):
-    pieces, quarter, lanes = mine_ref.shape
-    rows = query_ref.shape[0]
-    count = rows // quarter
-    held_rows = ((0, mine_ref), (1, right_ref), (count - 1, left_ref), (2, across_ref))[:count]
-    chunks = sems.shape[0]
-    step = pieces // chunks
-    depth = step * lanes
+    parts, rows, depth = grad_ref.shape
     copies = [
         pltpu.make_async_copy(
-            weight_hbm.at[0, pl.ds(chunk * depth, depth)],
-            weight_ref.at[pl.ds(chunk * depth, depth)],
-            sems.at[chunk],
-        )
-        for chunk in range(chunks)
+            weight_hbm.at[0, pl.ds(part * depth, depth)],
+            weight_ref.at[pl.ds(part * depth, depth)],
+            sems.at[part],
+        )
+        for part in range(parts)
     ]
     for copy in copies:
         copy.start()
     total = None
-    for chunk in range(chunks):
-        grad = jnp.concatenate(
-            [
-                jnp.concatenate(
-                    [ref[at] for at in range(chunk * step, (chunk + 1) * step)], axis=1
-                )
-                for _, ref in held_rows
-            ],
-            axis=0,
-        )
-        copies[chunk].wait()
+    for part in range(parts):
+        copies[part].wait()
         term = jnp.dot(
-            grad, weight_ref[chunk * depth : (chunk + 1) * depth, :], preferred_element_type=F32
+            grad_ref[part],
+            weight_ref[part * depth : (part + 1) * depth, :],
+            preferred_element_type=F32,
         )
         total = term if total is None else total + term
-    total = total.astype(BF16)
-    for index, (steps, _) in enumerate(held_rows):
-        at = lax.rem(lax.axis_index("tensor") + steps, count) * quarter
-        d_context_ref[pl.ds(pl.multiple_of(at, quarter), quarter), :] = total[
-            index * quarter : (index + 1) * quarter
-        ]
-    d_context = d_context_ref[...]
+    d_context = total.astype(BF16)
     blocks = ((far_ref, far_part_ref), (near_ref, near_part_ref), (own_ref, own_part_ref))
     for head in range(query_ref.shape[1] // HD):
         cols = slice(head * HD, (head + 1) * HD)
@@ -199,8 +176,8 @@
         query_grad_ref[:, cols] = query_grad.astype(BF16)
 
 
-def weight_kernel(grad_ref, *refs):
-    quarters, blocks, owners, rows, _ = grad_ref.shape
+def weight_kernel(masks, grad_ref, *refs):
+    quarters, blocks, _, rows, _ = grad_ref.shape
     context_refs, term_refs = refs[:blocks], refs[blocks:]
     here, me = lax.axis_index("zh"), lax.axis_index(GROUP)
     places = [lax.rem(here + steps, blocks) for steps in ring_steps(blocks)]
@@ -208,14 +185,14 @@
         jnp.concatenate([ref[quarter * rows : (quarter + 1) * rows] for ref in context_refs], axis=0)
         for quarter in range(quarters)
     ]
-    for mask in range(owners):
+    for mask, term_ref in zip(masks, term_refs):
         owner = jnp.bitwise_xor(me, mask)
         total = None
         for quarter in range(quarters):
             grad = jnp.concatenate([grad_ref[quarter, at, owner] for at in places], axis=0)
             term = contract(grad, contexts[quarter], 0, 0)
             total = term if total is None else total + term
-        term_refs[mask][...] = total.astype(term_refs[mask].dtype)
+        term_ref[...] = total.astype(term_ref.dtype)
 
 
 def ring_steps(count):
@@ -251,24 +228,15 @@
     owners = lax.axis_size(GROUP)
     heads = width // HD
     window = (REACH + 1) * rows
-    lanes = features // sections
     quarter = rows // tensors
-    pieces = sections * tensors
+    lanes = features * tensors // (chips * owners)
+    slab = (sections, rows // sections, features)
     shape = jax.ShapeDtypeStruct
 
-    (sliced,) = call(
-        slice_kernel,
-        [shape((sections, rows, lanes), BF16)],
-        (section_out[0],),
-        [RAW],
-        0,
-        4 * rows * features,
-        [pltpu.SemaphoreType.DMA((sections,))],
-    )
-    layers = exchanged(sliced, "section")
+    layers = exchanged(section_out.reshape(slab), "section")
     held, base = call(
         pack_kernel,
-        [shape((2, rows, width), BF16), shape((rows, lanes), BF16)],
+        [shape((2, rows, width), BF16), shape(slab[1:], BF16)],
         (key_heads, values, out_grad),
         [RAW] * 3,
         0,
@@ -284,13 +252,15 @@
     far = shifted(held, 2)
     (grads,) = call(
         suffix_kernel,
-        [shape((tensors, sections, quarter, lanes), BF16)],
+        [shape((tensors, *slab), BF16)],
         (base, layers),
         [WHOLE] * 2,
         layers.size * 3,
         layers.size * 4,
     )
-    mine = exchanged(grads.reshape(pieces, quarter, lanes), ("tensor", "section"))
+    grad_full = exchanged(
+        grads.reshape(tensors * sections, *slab[1:]), ("tensor", "section")
+    ).reshape(tensors, rows, features)
     (prob,) = call(
         prob_kernel,
         [shape((heads, rows, window), F32)],
@@ -304,10 +274,15 @@
             pltpu.SemaphoreType.DMA((2,)),
         ],
     )
+    (mine,) = call(
+        quarter_kernel,
+        [shape((chips * owners, quarter, lanes), BF16)],
+        (grad_full,),
+        [WHOLE],
+        0,
+        4 * rows * features,
+    )
     columns = exchanged(mine.reshape(chips, owners, quarter, lanes), "zh")
-    from_left = turned(mine, "tensor", 1)
-    from_right = turned(mine, "tensor", -1)
-    across = turned(from_left, "tensor", 1)
     columns_all = spread(columns, "tensor")
 
     query_grad, own_part, near_part, far_part = call(
@@ -318,33 +293,34 @@
             shape((2, rows, width), BF16),
             shape((2, rows, width), BF16),
         ],
-        (
-            mine, from_left, from_right, across,
-            o_weight, prob, queries[0], held, near, far, context[0],
-        ),
-        [WHOLE] * 4 + [RAW] + [WHOLE] * 6,
+        (grad_full, o_weight, prob, queries[0], held, near, far, context[0]),
+        [WHOLE, RAW] + [WHOLE] * 6,
         2 * rows * features * tensors * width + 8 * rows * window * width,
         2 * features * tensors * width,
         [
-            pltpu.VMEM((rows, width), BF16),
             pltpu.VMEM(o_weight.shape[1:], BF16),
-            pltpu.SemaphoreType.DMA((4,)),
+            pltpu.SemaphoreType.DMA((tensors,)),
         ],
     )
     near_back = shifted(near_part, -1)
     far_back = shifted(far_part, -2)
     sums = (own_part + near_back.astype(F32) + far_back.astype(F32)).astype(BF16)
 
-    weight_grad, *terms = call(
-        weight_kernel,
-        [shape((lanes, width), F32)] + [shape((lanes, width), BF16)] * (owners - 1),
-        (columns_all, *blocks),
-        [WHOLE] * (1 + chips),
-        2 * columns_all.size * width,
-        2 * (columns_all.size + chips * context.size),
-    )
-    for mask in range(1, owners):
-        other = swapped(terms[mask - 1], mask)
+    def terms_for(masks, types):
+        return call(
+            functools.partial(weight_kernel, masks),
+            [shape((lanes, width), dtype) for dtype in types],
+            (columns_all, *blocks),
+            [WHOLE] * (1 + chips),
+            len(masks) * columns_all.size * width // 2,
+            2 * (columns_all.size + chips * context.size),
+        )
+
+    sent = range(owners - 1, 0, -1)
+    far_terms = terms_for(sent[:2], [BF16] * 2)
+    *near_terms, weight_grad = terms_for((*sent[2:], 0), [BF16] * len(sent[2:]) + [F32])
+    for mask, term in zip(sent, (*far_terms, *near_terms)):
+        other = swapped(term, mask)
         weight_grad = weight_grad + other.astype(F32)
     return query_grad[None], sums[:1], sums[1:], weight_grad[None]
 

time: 150 us -> 166 us (1.11)
  blocking collectives: 16.3 us -> 25.8 us
  waiting for transfers between devices: 23.1 us -> 30.7 us
  Pallas kernels: 11.4 us -> 9.73 us
    ppermute x10 -> x7, starting transfers between devices: 35 us -> 23.7 us  [turned(): lax.ppermute(value, axis, [(i, (i + steps) % count) for i in range(count)])]
    all_to_all x1, blocking collectives: 16.3 us -> 25.8 us  [exchanged(): return lax.all_to_all(value, axis, 0, 0, tiled=True)]
    ppermute x4, starting transfers between devices: 15.6 us -> 22.5 us  [shifted(): lax.ppermute(value, DP, [(i, (i + steps) % count) for i in range(count)])]
    all_to_all x3, waiting for transfers between devices: 8.34 us -> 14.6 us  [exchanged(): return lax.all_to_all(value, axis, 0, 0, tiled=True)]
    all_to_all x3, starting transfers between devices: 30.1 us -> 35.7 us  [exchanged(): return lax.all_to_all(value, axis, 0, 0, tiled=True)]
    ppermute x3, waiting for transfers between devices: 1.02 us -> 4.65 us  [swapped(): return lax.ppermute(value, GROUP, [(i, i ^ mask) for i in range(count)])]
    ppermute x10 -> x7, waiting for transfers between devices: 13.8 us -> 11.5 us  [turned(): lax.ppermute(value, axis, [(i, (i + steps) % count) for i in range(count)])]
    pallas_call x6 -> x7, Pallas kernels: 11.4 us -> 9.73 us  [call(): pl.pallas_call(kernel, out_shape=outs, in_specs=specs, out_specs=[WHOLE]...]
  transfers between devices with their start and end apart: 20 -> 17, of which waited for: 6 -> 8; matrix products, arithmetic and copies ran while one was open for 1% -> 1% of each run, Pallas kernels for 6% -> 5%
where the time goes in v4:
time: 166 us; the launch traced here: 164 us
  starting transfers between devices  93.6 us (56%)
  waiting for transfers between devices  30.7 us (18%)
  blocking collectives  25.8 us (16%)
  Pallas kernels  9.73 us (6%)
  local copies, waits for them, and re-layouts  1.99 us (1%)
    all_to_all x3, starting transfers between devices, exchanged(): return lax.all_to_all(value, axis, 0, 0, tiled=True)  35.7 us
    all_to_all x1, blocking collectives, exchanged(): return lax.all_to_all(value, axis, 0, 0, tiled=True)  25.8 us
    ppermute x7, starting transfers between devices, turned(): lax.ppermute(value, axis, [(i, (i + steps) % count) for i in range(count)])  23.7 us
    ppermute x4, starting transfers between devices, shifted(): lax.ppermute(value, DP, [(i, (i + steps) % count) for i in range(count)])  22.5 us
    all_to_all x3, waiting for transfers between devices, exchanged(): return lax.all_to_all(value, axis, 0, 0, tiled=True)  14.6 us
    ppermute x3, starting transfers between devices, swapped(): return lax.ppermute(value, GROUP, [(i, i ^ mask) for i in range(count)])  11.7 us
    ppermute x7, waiting for transfers between devices, turned(): lax.ppermute(value, axis, [(i, (i + steps) % count) for i in range(count)])  11.5 us
    pallas_call x7, Pallas kernels, call(): pl.pallas_call(kernel, out_shape=outs, in_specs=specs, out_specs=[WHOLE]...  9.73 us
  transfers between devices with their start and end apart: 17, of which 8 were waited for; matrix products, arithmetic and copies ran while one was open for 1% of the time, Pallas kernels for 5%

profile of v4, /device:TPU:1, one launch (start us, length us, event | category | flops | bytes accessed | tf_op | source)
XLA Modules:
  0.0 163.6 jit_solution(18114525943902130905)
XLA Ops:
  0.6 7.7 %all-to-all-start = ((bf16[8,16,1024]{2,1,0:T(8,128)(2,1)}), bf16[8,16,1024]{2,1,0:T(8,128)(2,1)S(1)}, u32[]{:S(2)}, u32[]{:S(2)}) async-start(bf16[8,16,1024]{2,1,0:T(8,128)(2,1)} %bitcast.18), calls=%async_computation | async-start | bytes 524288 | tf_op jit(solution)/shard_map/all_to_all | solution.py:45
  8.3 1.0 shard_map.111
  9.3 8.3 %all-to-all-done.layers_ref = bf16[8,16,1024]{2,1,0:T(8,128)(2,1)S(1)} async-done(((bf16[8,16,1024]{2,1,0:T(8,128)(2,1)}), bf16[8,16,1024]{2,1,0:T(8,128)(2,1)S(1)}, u32[]{:S(2)}, u32[]{:S(2)}) %all-to-all-start) | async-done | bytes 262176 | tf_op jit(solution)/shard_map/all_to_all | solution.py:45
  17.7 25.8 %all_to_all.20 = bf16[32,16,1024]{2,1,0:T(8,128)(2,1)S(1)} all-to-all(bf16[32,16,1024]{2,1,0:T(8,128)(2,1)S(1)} %bitcast.11), channel_id=1, replica_groups=mesh['section'=8,'zh'=8,'zl'=2,'core'=2,'tensor'=4] {'tensor','section'}, dimensions={0} | all-to-all | bytes 2097152 | tf_op jit(solution)/shard_map/all_to_all | solution.py:45
  43.5 0.7 shard_map.115
  44.3 24.5 %all-to-all-start.2 = ((bf16[8,4,32,128]{3,2,1,0:T(8,128)(2,1)}), bf16[8,4,32,128]{3,2,1,0:T(8,128)(2,1)S(1)}, u32[]{:S(2)}, u32[]{:S(2)}) async-start(bf16[8,4,32,128]{3,2,1,0:T(8,128)(2,1)} %bitcast.6), calls=%async_computation.2 | async-start | bytes 524288 | tf_op jit(solution)/shard_map/all_to_all | solution.py:45
  68.7 5.9 %collective-permute-start = (bf16[2,128,512]{2,1,0:T(8,128)(2,1)S(1)}, bf16[2,128,512]{2,1,0:T(8,128)(2,1)S(1)}, u32[]{:S(2)}, u32[]{:S(2)}) collective-permute-start(bf16[2,128,512]{2,1,0:T(8,128)(2,1)S(1)} %get-tuple-element.15.own_ref), channel_id=1, source_target_pairs={{0,4},{4,8},{8,12},{12,16},{16,20},{20,24},{24,28},{28,32},{32,36}... | collective-permute-start | bytes 786440 | tf_op jit(solution)/shard_map/ppermute | solution.py:31
  74.7 3.6 %collective-permute-start.1 = (bf16[2,128,512]{2,1,0:T(8,128)(2,1)S(1)}, bf16[2,128,512]{2,1,0:T(8,128)(2,1)S(1)}, u32[]{:S(2)}, u32[]{:S(2)}) collective-permute-start(bf16[2,128,512]{2,1,0:T(8,128)(2,1)S(1)} %get-tuple-element.15.own_ref), channel_id=1, source_target_pairs={{0,8},{4,12},{8,16},{12,20},{16,24},{20,28},{24,32},{28,36},{32,40... | collective-permute-start | bytes 786440 | tf_op jit(solution)/shard_map/ppermute | solution.py:31
  78.3 6.2 %all-to-all-done.2 = bf16[8,4,32,128]{3,2,1,0:T(8,128)(2,1)S(1)} async-done(((bf16[8,4,32,128]{3,2,1,0:T(8,128)(2,1)}), bf16[8,4,32,128]{3,2,1,0:T(8,128)(2,1)S(1)}, u32[]{:S(2)}, u32[]{:S(2)}) %all-to-all-start.2) | async-done | bytes 262176 | tf_op jit(solution)/shard_map/all_to_all | solution.py:45
  84.5 1.3 broadcast_in_dim.13
  85.8 3.5 %all-to-all-start.3 = ((bf16[4,8,4,32,128]{4,3,2,1,0:T(8,128)(2,1)}), bf16[4,8,4,32,128]{4,3,2,1,0:T(8,128)(2,1)S(1)}, u32[]{:S(2)}, u32[]{:S(2)}) async-start(bf16[4,8,4,32,128]{4,3,2,1,0:T(8,128)(2,1)} %broadcast_in_dim.13), calls=%async_computation.3 | async-start | bytes 2097152 | tf_op jit(solution)/shard_map/all_to_all | solution.py:45
  89.3 3.0 %collective-permute-start.4 = (bf16[128,512]{1,0:T(8,128)(2,1)S(1)}, bf16[128,512]{1,0:T(8,128)(2,1)S(1)}, u32[]{:S(2)}, u32[]{:S(2)}) collective-permute-start(bf16[128,512]{1,0:T(8,128)(2,1)S(1)} %bitcast.12), channel_id=1, source_target_pairs={{0,16},{16,32},{32,48},{48,64},{64,80},{80,96},{96,112},{112,0},{1... | collective-permute-start | bytes 393224 | tf_op jit(solution)/shard_map/ppermute | solution.py:36
  92.3 4.4 %collective-permute-start.5 = (bf16[128,512]{1,0:T(8,128)(2,1)S(1)}, bf16[128,512]{1,0:T(8,128)(2,1)S(1)}, u32[]{:S(2)}, u32[]{:S(2)}) collective-permute-start(bf16[128,512]{1,0:T(8,128)(2,1)S(1)} %bitcast.13), channel_id=1, source_target_pairs={{0,112},{16,0},{32,16},{48,32},{64,48},{80,64},{96,80},{112,96},{1... | collective-permute-start | bytes 393224 | tf_op jit(solution)/shard_map/ppermute | solution.py:36
  96.7 1.8 %collective-permute-done.4.refs_1_ = bf16[128,512]{1,0:T(8,128)(2,1)S(1)} collective-permute-done((bf16[128,512]{1,0:T(8,128)(2,1)S(1)}, bf16[128,512]{1,0:T(8,128)(2,1)S(1)}, u32[]{:S(2)}, u32[]{:S(2)}) %collective-permute-start.4) | collective-permute-done | bytes 131104 | tf_op jit(solution)/shard_map/ppermute | solution.py:36
  98.5 1.9 %collective-permute-start.6 = (bf16[128,512]{1,0:T(8,128)(2,1)S(1)}, bf16[128,512]{1,0:T(8,128)(2,1)S(1)}, u32[]{:S(2)}, u32[]{:S(2)}) collective-permute-start(bf16[128,512]{1,0:T(8,128)(2,1)S(1)} %collective-permute-done.4.refs_1_), channel_id=1, source_target_pairs={{0,16},{16,32},{32,48},{48,64},{64,80},{80,96},{96,112},{112,0},{1... | collective-permute-start | bytes 393224 | tf_op jit(solution)/shard_map/ppermute | solution.py:36
  100.5 1.7 %shard_map.113.prob_ref = f32[4,128,384]{2,1,0:T(8,128)S(1)} custom-call(s32[32]{0:T(128)} %lengths_hbm.1, bf16[1,128,512]{2,1,0:T(8,128)(2,1)} %query_hbm.1, bf16[2,128,512]{2,1,0:T(8,128)(2,1)S(1)} %get-tuple-element.15.own_ref, bf16[2,128,512]{2,1,0:T(8,128)(2,1)S(1)} %collective-permute-done.near_ref, bf16[2,128,512]{2,1,0:T(8,128)(2,1)S(1)} %collective-permute-done.1.far_ref), custom_call_target="tpu_custom_call" | custom-call | flops 52297728 | bytes 1572864 | tf_op jit(solution)/shard_map/pallas_call | solution.py:208
  102.2 5.2 %shard_map.114 = (bf16[128,512]{1,0:T(8,128)(2,1)}, f32[2,128,512]{2,1,0:T(8,128)S(1)}, bf16[2,128,512]{2,1,0:T(8,128)(2,1)S(1)}, bf16[2,128,512]{2,1,0:T(8,128)(2,1)S(1)}) custom-call(bf16[4,128,1024]{2,1,0:T(8,128)(2,1)S(1)} %bitcast.10, bf16[1,4096,512]{2,1,0:T(8,128)(2,1)} %weight_hbm.1, f32[4,128,384]{2,1,0:T(8,128)S(1)} %shard_map.113.prob_ref, ...), custom_call_target="tpu_custom_call" | custom-call | flops 738197504 | bytes 4194304 | tf_op jit(solution)/shard_map/pallas_call | solution.py:208
  107.4 3.4 %collective-permute-start.3 = (bf16[2,128,512]{2,1,0:T(8,128)(2,1)S(1)}, bf16[2,128,512]{2,1,0:T(8,128)(2,1)S(1)}, u32[]{:S(2)}, u32[]{:S(2)}) collective-permute-start(bf16[2,128,512]{2,1,0:T(8,128)(2,1)S(1)} %get-tuple-element.19), channel_id=1, source_target_pairs={{0,120},{4,124},{8,0},{12,4},{16,8},{20,12},{24,16},{28,20},{32,24... | collective-permute-start | bytes 786440 | tf_op jit(solution)/shard_map/ppermute | solution.py:31
  110.8 9.6 %collective-permute-start.2 = (bf16[2,128,512]{2,1,0:T(8,128)(2,1)S(1)}, bf16[2,128,512]{2,1,0:T(8,128)(2,1)S(1)}, u32[]{:S(2)}, u32[]{:S(2)}) collective-permute-start(bf16[2,128,512]{2,1,0:T(8,128)(2,1)S(1)} %get-tuple-element.18), channel_id=1, source_target_pairs={{0,124},{4,0},{8,4},{12,8},{16,12},{20,16},{24,20},{28,24},{32,28}... | collective-permute-start | bytes 786440 | tf_op jit(solution)/shard_map/ppermute | solution.py:31
  120.4 4.6 %collective-permute-start.7 = (bf16[128,512]{1,0:T(8,128)(2,1)S(1)}, bf16[128,512]{1,0:T(8,128)(2,1)S(1)}, u32[]{:S(2)}, u32[]{:S(2)}) collective-permute-start(bf16[128,512]{1,0:T(8,128)(2,1)S(1)} %collective-permute-done.5.refs_2_), channel_id=1, source_target_pairs={{0,112},{16,0},{32,16},{48,32},{64,48},{80,64},{96,80},{112,96},{1... | collective-permute-start | bytes 393224 | tf_op jit(solution)/shard_map/ppermute | solution.py:36
  125.0 1.9 %collective-permute-start.8 = (bf16[128,512]{1,0:T(8,128)(2,1)S(1)}, bf16[128,512]{1,0:T(8,128)(2,1)S(1)}, u32[]{:S(2)}, u32[]{:S(2)}) collective-permute-start(bf16[128,512]{1,0:T(8,128)(2,1)S(1)} %collective-permute-done.6.refs_3_), channel_id=1, source_target_pairs={{0,16},{16,32},{32,48},{48,64},{64,80},{80,96},{96,112},{112,0},{1... | collective-permute-start | bytes 393224 | tf_op jit(solution)/shard_map/ppermute | solution.py:36
  127.0 2.4 %collective-permute-done.7.refs_4_ = bf16[128,512]{1,0:T(8,128)(2,1)S(1)} collective-permute-done((bf16[128,512]{1,0:T(8,128)(2,1)S(1)}, bf16[128,512]{1,0:T(8,128)(2,1)S(1)}, u32[]{:S(2)}, u32[]{:S(2)}) %collective-permute-start.7) | collective-permute-done | bytes 131104 | tf_op jit(solution)/shard_map/ppermute | solution.py:36
  129.3 6.0 %collective-permute-start.9 = (bf16[128,512]{1,0:T(8,128)(2,1)S(1)}, bf16[128,512]{1,0:T(8,128)(2,1)S(1)}, u32[]{:S(2)}, u32[]{:S(2)}) collective-permute-start(bf16[128,512]{1,0:T(8,128)(2,1)S(1)} %collective-permute-done.7.refs_4_), channel_id=1, source_target_pairs={{0,112},{16,0},{32,16},{48,32},{64,48},{80,64},{96,80},{112,96},{1... | collective-permute-start | bytes 393224 | tf_op jit(solution)/shard_map/ppermute | solution.py:36
  135.3 1.5 collective-permute-done.8.refs_5_
  136.8 1.9 %collective-permute-start.10 = (bf16[128,512]{1,0:T(8,128)(2,1)S(1)}, bf16[128,512]{1,0:T(8,128)(2,1)S(1)}, u32[]{:S(2)}, u32[]{:S(2)}) collective-permute-start(bf16[128,512]{1,0:T(8,128)(2,1)S(1)} %collective-permute-done.8.refs_5_), channel_id=1, source_target_pairs={{0,16},{16,32},{32,48},{48,64},{64,80},{80,96},{96,112},{112,0},{1... | collective-permute-start | bytes 393224 | tf_op jit(solution)/shard_map/ppermute | solution.py:36
  138.9 5.8 %collective-permute-done.10.refs_7_ = bf16[128,512]{1,0:T(8,128)(2,1)S(1)} collective-permute-done((bf16[128,512]{1,0:T(8,128)(2,1)S(1)}, bf16[128,512]{1,0:T(8,128)(2,1)S(1)}, u32[]{:S(2)}, u32[]{:S(2)}) %collective-permute-start.10) | collective-permute-done | bytes 131104 | tf_op jit(solution)/shard_map/ppermute | solution.py:36
  145.2 4.0 %collective-permute-start.13 = (bf16[128,512]{1,0:T(8,128)(2,1)S(1)}, bf16[128,512]{1,0:T(8,128)(2,1)S(1)}, u32[]{:S(2)}, u32[]{:S(2)}) collective-permute-start(bf16[128,512]{1,0:T(8,128)(2,1)S(1)} %get-tuple-element.23), channel_id=1, source_target_pairs={{0,4},{4,0},{8,12},{12,8},{1,5},{5,1},{9,13},{13,9},{2,6},{6,2},{1... | collective-permute-start | bytes 393224 | tf_op jit(solution)/shard_map/ppermute | solution.py:41
  149.8 5.8 %collective-permute-start.12 = (bf16[128,512]{1,0:T(8,128)(2,1)S(1)}, bf16[128,512]{1,0:T(8,128)(2,1)S(1)}, u32[]{:S(2)}, u32[]{:S(2)}) collective-permute-start(bf16[128,512]{1,0:T(8,128)(2,1)S(1)} %get-tuple-element.22), channel_id=1, source_target_pairs={{0,8},{4,12},{8,0},{12,4},{1,9},{5,13},{9,1},{13,5},{2,10},{6,14},... | collective-permute-start | bytes 393224 | tf_op jit(solution)/shard_map/ppermute | solution.py:41
  155.5 1.9 %collective-permute-start.11 = (bf16[128,512]{1,0:T(8,128)(2,1)S(1)}, bf16[128,512]{1,0:T(8,128)(2,1)S(1)}, u32[]{:S(2)}, u32[]{:S(2)}) collective-permute-start(bf16[128,512]{1,0:T(8,128)(2,1)S(1)} %get-tuple-element.21), channel_id=1, source_target_pairs={{0,12},{4,8},{8,4},{12,0},{1,13},{5,9},{9,5},{13,1},{2,14},{6,10},... | collective-permute-start | bytes 393224 | tf_op jit(solution)/shard_map/ppermute | solution.py:41
  158.2 1.2 collective-permute-done.12
  159.4 3.4 %collective-permute-done.11 = bf16[128,512]{1,0:T(8,128)(2,1)S(1)} collective-permute-done((bf16[128,512]{1,0:T(8,128)(2,1)S(1)}, bf16[128,512]{1,0:T(8,128)(2,1)S(1)}, u32[]{:S(2)}, u32[]{:S(2)}) %collective-permute-start.11) | collective-permute-done | bytes 131104 | tf_op jit(solution)/shard_map/ppermute | solution.py:41
  162.8 0.8 add_bitcast_fusion
  (18 shorter events, 1.9 us)
Async XLA Ops:
  0.6 17.0 %all-to-all-start = ((bf16[8,16,1024]{2,1,0:T(8,128)(2,1)}), bf16[8,16,1024]{2,1,0:T(8,128)(2,1)S(1)}, u32[]{:S(2)}, u32[]{:S(2)}) async-start(bf16[8,16,1024]{2,1,0:T(8,128)(2,1)} %bitcast.18), calls=%async_computation | async-start | bytes 524288 | tf_op jit(solution)/shard_map/all_to_all | solution.py:45
  17.6 71.7 %copy-start = (bf16[1,128,512]{2,1,0:T(8,128)(2,1)S(1)}, bf16[1,128,512]{2,1,0:T(8,128)(2,1)}, u32[]{:S(2)}) copy-start(bf16[1,128,512]{2,1,0:T(8,128)(2,1)} %param.10) | copy-start | bytes 393220
  17.7 84.5 %copy-start.1 = (bf16[1,128,512]{2,1,0:T(8,128)(2,1)S(1)}, bf16[1,128,512]{2,1,0:T(8,128)(2,1)}, u32[]{:S(2)}) copy-start(bf16[1,128,512]{2,1,0:T(8,128)(2,1)} %query_hbm.1) | copy-start | bytes 393220
  44.3 40.3 %all-to-all-start.2 = ((bf16[8,4,32,128]{3,2,1,0:T(8,128)(2,1)}), bf16[8,4,32,128]{3,2,1,0:T(8,128)(2,1)S(1)}, u32[]{:S(2)}, u32[]{:S(2)}) async-start(bf16[8,4,32,128]{3,2,1,0:T(8,128)(2,1)} %bitcast.6), calls=%async_computation.2 | async-start | bytes 524288 | tf_op jit(solution)/shard_map/all_to_all | solution.py:45
  68.7 31.7 %collective-permute-start = (bf16[2,128,512]{2,1,0:T(8,128)(2,1)S(1)}, bf16[2,128,512]{2,1,0:T(8,128)(2,1)S(1)}, u32[]{:S(2)}, u32[]{:S(2)}) collective-permute-start(bf16[2,128,512]{2,1,0:T(8,128)(2,1)S(1)} %get-tuple-element.15.own_ref), channel_id=1, source_target_pairs={{0,4},{4,8},{8,12},{12,16},{16,20},{20,24},{24,28},{28,32},{32,36}... | collective-permute-start | bytes 786440 | tf_op jit(solution)/shard_map/ppermute | solution.py:31
  74.7 25.8 %collective-permute-start.1 = (bf16[2,128,512]{2,1,0:T(8,128)(2,1)S(1)}, bf16[2,128,512]{2,1,0:T(8,128)(2,1)S(1)}, u32[]{:S(2)}, u32[]{:S(2)}) collective-permute-start(bf16[2,128,512]{2,1,0:T(8,128)(2,1)S(1)} %get-tuple-element.15.own_ref), channel_id=1, source_target_pairs={{0,8},{4,12},{8,16},{12,20},{16,24},{20,28},{24,32},{28,36},{32,40... | collective-permute-start | bytes 786440 | tf_op jit(solution)/shard_map/ppermute | solution.py:31
  85.8 59.0 %all-to-all-start.3 = ((bf16[4,8,4,32,128]{4,3,2,1,0:T(8,128)(2,1)}), bf16[4,8,4,32,128]{4,3,2,1,0:T(8,128)(2,1)S(1)}, u32[]{:S(2)}, u32[]{:S(2)}) async-start(bf16[4,8,4,32,128]{4,3,2,1,0:T(8,128)(2,1)} %broadcast_in_dim.13), calls=%async_computation.3 | async-start | bytes 2097152 | tf_op jit(solution)/shard_map/all_to_all | solution.py:45
  89.3 9.2 %collective-permute-start.4 = (bf16[128,512]{1,0:T(8,128)(2,1)S(1)}, bf16[128,512]{1,0:T(8,128)(2,1)S(1)}, u32[]{:S(2)}, u32[]{:S(2)}) collective-permute-start(bf16[128,512]{1,0:T(8,128)(2,1)S(1)} %bitcast.12), channel_id=1, source_target_pairs={{0,16},{16,32},{32,48},{48,64},{64,80},{80,96},{96,112},{112,0},{1... | collective-permute-start | bytes 393224 | tf_op jit(solution)/shard_map/ppermute | solution.py:36
  92.3 28.1 %collective-permute-start.5 = (bf16[128,512]{1,0:T(8,128)(2,1)S(1)}, bf16[128,512]{1,0:T(8,128)(2,1)S(1)}, u32[]{:S(2)}, u32[]{:S(2)}) collective-permute-start(bf16[128,512]{1,0:T(8,128)(2,1)S(1)} %bitcast.13), channel_id=1, source_target_pairs={{0,112},{16,0},{32,16},{48,32},{64,48},{80,64},{96,80},{112,96},{1... | collective-permute-start | bytes 393224 | tf_op jit(solution)/shard_map/ppermute | solution.py:36
  98.5 26.5 %collective-permute-start.6 = (bf16[128,512]{1,0:T(8,128)(2,1)S(1)}, bf16[128,512]{1,0:T(8,128)(2,1)S(1)}, u32[]{:S(2)}, u32[]{:S(2)}) collective-permute-start(bf16[128,512]{1,0:T(8,128)(2,1)S(1)} %collective-permute-done.4.refs_1_), channel_id=1, source_target_pairs={{0,16},{16,32},{32,48},{48,64},{64,80},{80,96},{96,112},{112,0},{1... | collective-permute-start | bytes 393224 | tf_op jit(solution)/shard_map/ppermute | solution.py:36
  107.4 31.3 %collective-permute-start.3 = (bf16[2,128,512]{2,1,0:T(8,128)(2,1)S(1)}, bf16[2,128,512]{2,1,0:T(8,128)(2,1)S(1)}, u32[]{:S(2)}, u32[]{:S(2)}) collective-permute-start(bf16[2,128,512]{2,1,0:T(8,128)(2,1)S(1)} %get-tuple-element.19), channel_id=1, source_target_pairs={{0,120},{4,124},{8,0},{12,4},{16,8},{20,12},{24,16},{28,20},{32,24... | collective-permute-start | bytes 786440 | tf_op jit(solution)/shard_map/ppermute | solution.py:31
  110.8 27.9 %collective-permute-start.2 = (bf16[2,128,512]{2,1,0:T(8,128)(2,1)S(1)}, bf16[2,128,512]{2,1,0:T(8,128)(2,1)S(1)}, u32[]{:S(2)}, u32[]{:S(2)}) collective-permute-start(bf16[2,128,512]{2,1,0:T(8,128)(2,1)S(1)} %get-tuple-element.18), channel_id=1, source_target_pairs={{0,124},{4,0},{8,4},{12,8},{16,12},{20,16},{24,20},{28,24},{32,28}... | collective-permute-start | bytes 786440 | tf_op jit(solution)/shard_map/ppermute | solution.py:31
  120.4 8.9 %collective-permute-start.7 = (bf16[128,512]{1,0:T(8,128)(2,1)S(1)}, bf16[128,512]{1,0:T(8,128)(2,1)S(1)}, u32[]{:S(2)}, u32[]{:S(2)}) collective-permute-start(bf16[128,512]{1,0:T(8,128)(2,1)S(1)} %collective-permute-done.5.refs_2_), channel_id=1, source_target_pairs={{0,112},{16,0},{32,16},{48,32},{64,48},{80,64},{96,80},{112,96},{1... | collective-permute-start | bytes 393224 | tf_op jit(solution)/shard_map/ppermute | solution.py:36
  125.0 11.8 %collective-permute-start.8 = (bf16[128,512]{1,0:T(8,128)(2,1)S(1)}, bf16[128,512]{1,0:T(8,128)(2,1)S(1)}, u32[]{:S(2)}, u32[]{:S(2)}) collective-permute-start(bf16[128,512]{1,0:T(8,128)(2,1)S(1)} %collective-permute-done.6.refs_3_), channel_id=1, source_target_pairs={{0,16},{16,32},{32,48},{48,64},{64,80},{80,96},{96,112},{112,0},{1... | collective-permute-start | bytes 393224 | tf_op jit(solution)/shard_map/ppermute | solution.py:36
  129.3 9.5 %collective-permute-start.9 = (bf16[128,512]{1,0:T(8,128)(2,1)S(1)}, bf16[128,512]{1,0:T(8,128)(2,1)S(1)}, u32[]{:S(2)}, u32[]{:S(2)}) collective-permute-start(bf16[128,512]{1,0:T(8,128)(2,1)S(1)} %collective-permute-done.7.refs_4_), channel_id=1, source_target_pairs={{0,112},{16,0},{32,16},{48,32},{64,48},{80,64},{96,80},{112,96},{1... | collective-permute-start | bytes 393224 | tf_op jit(solution)/shard_map/ppermute | solution.py:36
  136.8 7.9 %collective-permute-start.10 = (bf16[128,512]{1,0:T(8,128)(2,1)S(1)}, bf16[128,512]{1,0:T(8,128)(2,1)S(1)}, u32[]{:S(2)}, u32[]{:S(2)}) collective-permute-start(bf16[128,512]{1,0:T(8,128)(2,1)S(1)} %collective-permute-done.8.refs_5_), channel_id=1, source_target_pairs={{0,16},{16,32},{32,48},{48,64},{64,80},{80,96},{96,112},{112,0},{1... | collective-permute-start | bytes 393224 | tf_op jit(solution)/shard_map/ppermute | solution.py:36
  145.2 13.0 %collective-permute-start.13 = (bf16[128,512]{1,0:T(8,128)(2,1)S(1)}, bf16[128,512]{1,0:T(8,128)(2,1)S(1)}, u32[]{:S(2)}, u32[]{:S(2)}) collective-permute-start(bf16[128,512]{1,0:T(8,128)(2,1)S(1)} %get-tuple-element.23), channel_id=1, source_target_pairs={{0,4},{4,0},{8,12},{12,8},{1,5},{5,1},{9,13},{13,9},{2,6},{6,2},{1... | collective-permute-start | bytes 393224 | tf_op jit(solution)/shard_map/ppermute | solution.py:41
  149.8 9.6 %collective-permute-start.12 = (bf16[128,512]{1,0:T(8,128)(2,1)S(1)}, bf16[128,512]{1,0:T(8,128)(2,1)S(1)}, u32[]{:S(2)}, u32[]{:S(2)}) collective-permute-start(bf16[128,512]{1,0:T(8,128)(2,1)S(1)} %get-tuple-element.22), channel_id=1, source_target_pairs={{0,8},{4,12},{8,0},{12,4},{1,9},{5,13},{9,1},{13,5},{2,10},{6,14},... | collective-permute-start | bytes 393224 | tf_op jit(solution)/shard_map/ppermute | solution.py:41
  155.5 7.3 %collective-permute-start.11 = (bf16[128,512]{1,0:T(8,128)(2,1)S(1)}, bf16[128,512]{1,0:T(8,128)(2,1)S(1)}, u32[]{:S(2)}, u32[]{:S(2)}) collective-permute-start(bf16[128,512]{1,0:T(8,128)(2,1)S(1)} %get-tuple-element.21), channel_id=1, source_target_pairs={{0,12},{4,8},{8,4},{12,0},{1,13},{5,9},{9,5},{13,1},{2,14},{6,10},... | collective-permute-start | bytes 393224 | tf_op jit(solution)/shard_map/ppermute | solution.py:41

commit v5 on v4

--- a/solution.py
+++ b/solution.py
@@ -45,11 +45,6 @@
     return lax.all_to_all(value, axis, 0, 0, tiled=True)
 
 
-def spread(value, axis):
-    copies = lax.axis_size(axis)
-    return exchanged(jnp.broadcast_to(value[None], (copies, *value.shape)), axis)
-
-
 def copy_all(copies):
     for copy in copies:
         copy.start()
@@ -87,6 +82,16 @@
     for block in range(blocks):
         first = block % each * lanes
         mine_ref[block] = grad_ref[block // each, pl.ds(at, rows), first : first + lanes]
+
+
+def repeat_kernel(value_ref, repeated_ref, held_ref, sems):
+    copy_all([pltpu.make_async_copy(value_ref, held_ref, sems.at[0])])
+    copy_all(
+        [
+            pltpu.make_async_copy(held_ref, repeated_ref.at[at], sems.at[1 + at])
+            for at in range(repeated_ref.shape[0])
+        ]
+    )
 
 
 def prob_kernel(
@@ -204,12 +209,12 @@
     return steps
 
 
-def call(kernel, outs, inputs, specs, flops, nbytes, scratch=()):
+def call(kernel, outs, inputs, specs, flops, nbytes, scratch=(), out_spec=WHOLE):
     return pl.pallas_call(
         kernel,
         out_shape=outs,
         in_specs=specs,
-        out_specs=[WHOLE] * len(outs),
+        out_specs=[out_spec] * len(outs),
         scratch_shapes=list(scratch),
         compiler_params=pltpu.CompilerParams(vmem_limit_bytes=24 * 2**20),
         cost_estimate=pl.CostEstimate(flops=flops, bytes_accessed=nbytes, transcendentals=0),
@@ -283,7 +288,17 @@
         4 * rows * features,
     )
     columns = exchanged(mine.reshape(chips, owners, quarter, lanes), "zh")
-    columns_all = spread(columns, "tensor")
+    (repeated,) = call(
+        repeat_kernel,
+        [shape((tensors, *columns.shape), BF16)],
+        (columns,),
+        [RAW],
+        0,
+        2 * (tensors + 1) * columns.size,
+        [pltpu.VMEM(columns.shape, BF16), pltpu.SemaphoreType.DMA((1 + tensors,))],
+        RAW,
+    )
+    columns_all = exchanged(repeated, "tensor")
 
     query_grad, own_part, near_part, far_part = call(
         grads_kernel,
@@ -317,9 +332,8 @@
         )
 
     sent = range(owners - 1, 0, -1)
-    far_terms = terms_for(sent[:2], [BF16] * 2)
-    *near_terms, weight_grad = terms_for((*sent[2:], 0), [BF16] * len(sent[2:]) + [F32])
-    for mask, term in zip(sent, (*far_terms, *near_terms)):
+    *sent_terms, weight_grad = terms_for((*sent, 0), [BF16] * len(sent) + [F32])
+    for mask, term in zip(sent, sent_terms):
         other = swapped(term, mask)
         weight_grad = weight_grad + other.astype(F32)
     return query_grad[None], sums[:1], sums[1:], weight_grad[None]

time: 166 us -> 167 us (level)
  the two profiles are of different devices: /device:TPU:1 before, /device:TPU:11 now
where the time goes in v5:
time: 167 us
  starting transfers between devices  91.9 us (55%)
  waiting for transfers between devices  31.9 us (19%)
  blocking collectives  28.1 us (17%)
  Pallas kernels  11.5 us (7%)
    all_to_all x3, starting transfers between devices, exchanged(): return lax.all_to_all(value, axis, 0, 0, tiled=True)  34.4 us
    all_to_all x1, blocking collectives, exchanged(): return lax.all_to_all(value, axis, 0, 0, tiled=True)  28.1 us
    ppermute x7, starting transfers between devices, turned(): lax.ppermute(value, axis, [(i, (i + steps) % count) for i in range(count)])  26.8 us
    ppermute x4, starting transfers between devices, shifted(): lax.ppermute(value, DP, [(i, (i + steps) % count) for i in range(count)])  20.6 us
    all_to_all x3, waiting for transfers between devices, exchanged(): return lax.all_to_all(value, axis, 0, 0, tiled=True)  16 us
    pallas_call x7, Pallas kernels, call(): pl.pallas_call(kernel, out_shape=outs, in_specs=specs, out_specs=[out_spe...  11.5 us
    ppermute x7, waiting for transfers between devices, turned(): lax.ppermute(value, axis, [(i, (i + steps) % count) for i in range(count)])  11.3 us
    ppermute x3, starting transfers between devices, swapped(): return lax.ppermute(value, GROUP, [(i, i ^ mask) for i in range(count)])  10.1 us
  transfers between devices with their start and end apart: 17, of which 9 were waited for; matrix products, arithmetic and copies ran while one was open for 0% of the time, Pallas kernels for 6%

profile of v5, /device:TPU:11, one launch (start us, length us, event | category | flops | bytes accessed | tf_op | source)
XLA Modules:
  0.0 166.5 jit_solution(3065901485517582910)
XLA Ops:
  0.6 7.0 %all-to-all-start = ((bf16[8,16,1024]{2,1,0:T(8,128)(2,1)}), bf16[8,16,1024]{2,1,0:T(8,128)(2,1)S(1)}, u32[]{:S(2)}, u32[]{:S(2)}) async-start(bf16[8,16,1024]{2,1,0:T(8,128)(2,1)} %bitcast.17), calls=%async_computation | async-start | bytes 524288 | tf_op jit(solution)/shard_map/all_to_all | solution.py:45
  7.6 1.0 shard_map.111
  8.6 7.5 %all-to-all-done.layers_ref = bf16[8,16,1024]{2,1,0:T(8,128)(2,1)S(1)} async-done(((bf16[8,16,1024]{2,1,0:T(8,128)(2,1)}), bf16[8,16,1024]{2,1,0:T(8,128)(2,1)S(1)}, u32[]{:S(2)}, u32[]{:S(2)}) %all-to-all-start) | async-done | bytes 262176 | tf_op jit(solution)/shard_map/all_to_all | solution.py:45
  16.2 28.1 %all_to_all.20 = bf16[32,16,1024]{2,1,0:T(8,128)(2,1)S(1)} all-to-all(bf16[32,16,1024]{2,1,0:T(8,128)(2,1)S(1)} %bitcast.11), channel_id=1, replica_groups=mesh['section'=8,'zh'=8,'zl'=2,'core'=2,'tensor'=4] {'tensor','section'}, dimensions={0} | all-to-all | bytes 2097152 | tf_op jit(solution)/shard_map/all_to_all | solution.py:45
  45.0 23.7 %all-to-all-start.2 = ((bf16[8,4,32,128]{3,2,1,0:T(8,128)(2,1)}), bf16[8,4,32,128]{3,2,1,0:T(8,128)(2,1)S(1)}, u32[]{:S(2)}, u32[]{:S(2)}) async-start(bf16[8,4,32,128]{3,2,1,0:T(8,128)(2,1)} %bitcast.6), calls=%async_computation.2 | async-start | bytes 524288 | tf_op jit(solution)/shard_map/all_to_all | solution.py:45
  68.7 4.2 %collective-permute-start = (bf16[2,128,512]{2,1,0:T(8,128)(2,1)S(1)}, bf16[2,128,512]{2,1,0:T(8,128)(2,1)S(1)}, u32[]{:S(2)}, u32[]{:S(2)}) collective-permute-start(bf16[2,128,512]{2,1,0:T(8,128)(2,1)S(1)} %get-tuple-element.15.own_ref), channel_id=1, source_target_pairs={{0,4},{4,8},{8,12},{12,16},{16,20},{20,24},{24,28},{28,32},{32,36}... | collective-permute-start | bytes 786440 | tf_op jit(solution)/shard_map/ppermute | solution.py:31
  73.0 3.6 %collective-permute-start.1 = (bf16[2,128,512]{2,1,0:T(8,128)(2,1)S(1)}, bf16[2,128,512]{2,1,0:T(8,128)(2,1)S(1)}, u32[]{:S(2)}, u32[]{:S(2)}) collective-permute-start(bf16[2,128,512]{2,1,0:T(8,128)(2,1)S(1)} %get-tuple-element.15.own_ref), channel_id=1, source_target_pairs={{0,8},{4,12},{8,16},{12,20},{16,24},{20,28},{24,32},{28,36},{32,40... | collective-permute-start | bytes 786440 | tf_op jit(solution)/shard_map/ppermute | solution.py:31
  76.6 8.5 %all-to-all-done.2.value_ref = bf16[8,4,32,128]{3,2,1,0:T(8,128)(2,1)S(1)} async-done(((bf16[8,4,32,128]{3,2,1,0:T(8,128)(2,1)}), bf16[8,4,32,128]{3,2,1,0:T(8,128)(2,1)S(1)}, u32[]{:S(2)}, u32[]{:S(2)}) %all-to-all-start.2) | async-done | bytes 262176 | tf_op jit(solution)/shard_map/all_to_all | solution.py:45
  85.8 2.0 %shard_map.116 = bf16[4,8,4,32,128]{4,3,2,1,0:T(8,128)(2,1)} custom-call(bf16[8,4,32,128]{3,2,1,0:T(8,128)(2,1)} %copy-done.2), custom_call_target="tpu_custom_call" | custom-call | bytes 1310720 | tf_op jit(solution)/shard_map/pallas_call | solution.py:213
  87.8 3.7 %all-to-all-start.3 = ((bf16[4,8,4,32,128]{4,3,2,1,0:T(8,128)(2,1)}), bf16[4,8,4,32,128]{4,3,2,1,0:T(8,128)(2,1)S(1)}, u32[]{:S(2)}, u32[]{:S(2)}) async-start(bf16[4,8,4,32,128]{4,3,2,1,0:T(8,128)(2,1)} %shard_map.116), calls=%async_computation.3 | async-start | bytes 2097152 | tf_op jit(solution)/shard_map/all_to_all | solution.py:45
  91.5 3.3 %collective-permute-start.4 = (bf16[128,512]{1,0:T(8,128)(2,1)S(1)}, bf16[128,512]{1,0:T(8,128)(2,1)S(1)}, u32[]{:S(2)}, u32[]{:S(2)}) collective-permute-start(bf16[128,512]{1,0:T(8,128)(2,1)S(1)} %bitcast.13), channel_id=1, source_target_pairs={{0,16},{16,32},{32,48},{48,64},{64,80},{80,96},{96,112},{112,0},{1... | collective-permute-start | bytes 393224 | tf_op jit(solution)/shard_map/ppermute | solution.py:36
  94.9 4.7 %collective-permute-start.5 = (bf16[128,512]{1,0:T(8,128)(2,1)S(1)}, bf16[128,512]{1,0:T(8,128)(2,1)S(1)}, u32[]{:S(2)}, u32[]{:S(2)}) collective-permute-start(bf16[128,512]{1,0:T(8,128)(2,1)S(1)} %bitcast.14), channel_id=1, source_target_pairs={{0,112},{16,0},{32,16},{48,32},{64,48},{80,64},{96,80},{112,96},{1... | collective-permute-start | bytes 393224 | tf_op jit(solution)/shard_map/ppermute | solution.py:36
  100.0 2.9 %collective-permute-start.6 = (bf16[128,512]{1,0:T(8,128)(2,1)S(1)}, bf16[128,512]{1,0:T(8,128)(2,1)S(1)}, u32[]{:S(2)}, u32[]{:S(2)}) collective-permute-start(bf16[128,512]{1,0:T(8,128)(2,1)S(1)} %collective-permute-done.4.refs_1_), channel_id=1, source_target_pairs={{0,16},{16,32},{32,48},{48,64},{64,80},{80,96},{96,112},{112,0},{1... | collective-permute-start | bytes 393224 | tf_op jit(solution)/shard_map/ppermute | solution.py:36
  102.9 1.7 %shard_map.113.prob_ref = f32[4,128,384]{2,1,0:T(8,128)S(1)} custom-call(s32[32]{0:T(128)} %lengths_hbm.1, bf16[1,128,512]{2,1,0:T(8,128)(2,1)} %query_hbm.1, bf16[2,128,512]{2,1,0:T(8,128)(2,1)S(1)} %get-tuple-element.15.own_ref, bf16[2,128,512]{2,1,0:T(8,128)(2,1)S(1)} %collective-permute-done.near_ref, bf16[2,128,512]{2,1,0:T(8,128)(2,1)S(1)} %collective-permute-done.1.far_ref), custom_call_target="tpu_custom_call" | custom-call | flops 52297728 | bytes 1572864 | tf_op jit(solution)/shard_map/pallas_call | solution.py:213
  104.6 5.2 %shard_map.114 = (bf16[128,512]{1,0:T(8,128)(2,1)}, f32[2,128,512]{2,1,0:T(8,128)S(1)}, bf16[2,128,512]{2,1,0:T(8,128)(2,1)S(1)}, bf16[2,128,512]{2,1,0:T(8,128)(2,1)S(1)}) custom-call(bf16[4,128,1024]{2,1,0:T(8,128)(2,1)S(1)} %bitcast.10, bf16[1,4096,512]{2,1,0:T(8,128)(2,1)} %weight_hbm.1, f32[4,128,384]{2,1,0:T(8,128)S(1)} %shard_map.113.prob_ref, ...), custom_call_target="tpu_custom_call" | custom-call | flops 738197504 | bytes 4194304 | tf_op jit(solution)/shard_map/pallas_call | solution.py:213
  109.8 3.1 %collective-permute-start.3 = (bf16[2,128,512]{2,1,0:T(8,128)(2,1)S(1)}, bf16[2,128,512]{2,1,0:T(8,128)(2,1)S(1)}, u32[]{:S(2)}, u32[]{:S(2)}) collective-permute-start(bf16[2,128,512]{2,1,0:T(8,128)(2,1)S(1)} %get-tuple-element.19), channel_id=1, source_target_pairs={{0,120},{4,124},{8,0},{12,4},{16,8},{20,12},{24,16},{28,20},{32,24... | collective-permute-start | bytes 786440 | tf_op jit(solution)/shard_map/ppermute | solution.py:31
  112.9 9.6 %collective-permute-start.2 = (bf16[2,128,512]{2,1,0:T(8,128)(2,1)S(1)}, bf16[2,128,512]{2,1,0:T(8,128)(2,1)S(1)}, u32[]{:S(2)}, u32[]{:S(2)}) collective-permute-start(bf16[2,128,512]{2,1,0:T(8,128)(2,1)S(1)} %get-tuple-element.18), channel_id=1, source_target_pairs={{0,124},{4,0},{8,4},{12,8},{16,12},{20,16},{24,20},{28,24},{32,28}... | collective-permute-start | bytes 786440 | tf_op jit(solution)/shard_map/ppermute | solution.py:31
  122.5 5.4 %collective-permute-start.7 = (bf16[128,512]{1,0:T(8,128)(2,1)S(1)}, bf16[128,512]{1,0:T(8,128)(2,1)S(1)}, u32[]{:S(2)}, u32[]{:S(2)}) collective-permute-start(bf16[128,512]{1,0:T(8,128)(2,1)S(1)} %collective-permute-done.5.refs_2_), channel_id=1, source_target_pairs={{0,112},{16,0},{32,16},{48,32},{64,48},{80,64},{96,80},{112,96},{1... | collective-permute-start | bytes 393224 | tf_op jit(solution)/shard_map/ppermute | solution.py:36
  127.9 1.9 %collective-permute-start.8 = (bf16[128,512]{1,0:T(8,128)(2,1)S(1)}, bf16[128,512]{1,0:T(8,128)(2,1)S(1)}, u32[]{:S(2)}, u32[]{:S(2)}) collective-permute-start(bf16[128,512]{1,0:T(8,128)(2,1)S(1)} %collective-permute-done.6.refs_3_), channel_id=1, source_target_pairs={{0,16},{16,32},{32,48},{48,64},{64,80},{80,96},{96,112},{112,0},{1... | collective-permute-start | bytes 393224 | tf_op jit(solution)/shard_map/ppermute | solution.py:36
  129.8 1.9 %collective-permute-done.7.refs_4_ = bf16[128,512]{1,0:T(8,128)(2,1)S(1)} collective-permute-done((bf16[128,512]{1,0:T(8,128)(2,1)S(1)}, bf16[128,512]{1,0:T(8,128)(2,1)S(1)}, u32[]{:S(2)}, u32[]{:S(2)}) %collective-permute-start.7) | collective-permute-done | bytes 131104 | tf_op jit(solution)/shard_map/ppermute | solution.py:36
  131.7 6.7 %collective-permute-start.9 = (bf16[128,512]{1,0:T(8,128)(2,1)S(1)}, bf16[128,512]{1,0:T(8,128)(2,1)S(1)}, u32[]{:S(2)}, u32[]{:S(2)}) collective-permute-start(bf16[128,512]{1,0:T(8,128)(2,1)S(1)} %collective-permute-done.7.refs_4_), channel_id=1, source_target_pairs={{0,112},{16,0},{32,16},{48,32},{64,48},{80,64},{96,80},{112,96},{1... | collective-permute-start | bytes 393224 | tf_op jit(solution)/shard_map/ppermute | solution.py:36
  138.4 0.9 collective-permute-done.8.refs_5_
  139.3 1.9 %collective-permute-start.10 = (bf16[128,512]{1,0:T(8,128)(2,1)S(1)}, bf16[128,512]{1,0:T(8,128)(2,1)S(1)}, u32[]{:S(2)}, u32[]{:S(2)}) collective-permute-start(bf16[128,512]{1,0:T(8,128)(2,1)S(1)} %collective-permute-done.8.refs_5_), channel_id=1, source_target_pairs={{0,16},{16,32},{32,48},{48,64},{64,80},{80,96},{96,112},{112,0},{1... | collective-permute-start | bytes 393224 | tf_op jit(solution)/shard_map/ppermute | solution.py:36
  141.3 1.2 collective-permute-done.9.refs_6_
  142.5 7.0 %collective-permute-done.10.refs_7_ = bf16[128,512]{1,0:T(8,128)(2,1)S(1)} collective-permute-done((bf16[128,512]{1,0:T(8,128)(2,1)S(1)}, bf16[128,512]{1,0:T(8,128)(2,1)S(1)}, u32[]{:S(2)}, u32[]{:S(2)}) %collective-permute-start.10) | collective-permute-done | bytes 131104 | tf_op jit(solution)/shard_map/ppermute | solution.py:36
  149.5 0.8 shard_map.117
  150.2 2.6 %collective-permute-start.13 = (bf16[128,512]{1,0:T(8,128)(2,1)S(1)}, bf16[128,512]{1,0:T(8,128)(2,1)S(1)}, u32[]{:S(2)}, u32[]{:S(2)}) collective-permute-start(bf16[128,512]{1,0:T(8,128)(2,1)S(1)} %get-tuple-element.23), channel_id=1, source_target_pairs={{0,4},{4,0},{8,12},{12,8},{1,5},{5,1},{9,13},{13,9},{2,6},{6,2},{1... | collective-permute-start | bytes 393224 | tf_op jit(solution)/shard_map/ppermute | solution.py:41
  152.8 5.6 %collective-permute-start.12 = (bf16[128,512]{1,0:T(8,128)(2,1)S(1)}, bf16[128,512]{1,0:T(8,128)(2,1)S(1)}, u32[]{:S(2)}, u32[]{:S(2)}) collective-permute-start(bf16[128,512]{1,0:T(8,128)(2,1)S(1)} %get-tuple-element.22), channel_id=1, source_target_pairs={{0,8},{4,12},{8,0},{12,4},{1,9},{5,13},{9,1},{13,5},{2,10},{6,14},... | collective-permute-start | bytes 393224 | tf_op jit(solution)/shard_map/ppermute | solution.py:41
  158.4 1.9 %collective-permute-start.11 = (bf16[128,512]{1,0:T(8,128)(2,1)S(1)}, bf16[128,512]{1,0:T(8,128)(2,1)S(1)}, u32[]{:S(2)}, u32[]{:S(2)}) collective-permute-start(bf16[128,512]{1,0:T(8,128)(2,1)S(1)} %get-tuple-element.21), channel_id=1, source_target_pairs={{0,12},{4,8},{8,4},{12,0},{1,13},{5,9},{9,5},{13,1},{2,14},{6,10},... | collective-permute-start | bytes 393224 | tf_op jit(solution)/shard_map/ppermute | solution.py:41
  161.1 1.2 collective-permute-done.12
  162.3 3.4 %collective-permute-done.11 = bf16[128,512]{1,0:T(8,128)(2,1)S(1)} collective-permute-done((bf16[128,512]{1,0:T(8,128)(2,1)S(1)}, bf16[128,512]{1,0:T(8,128)(2,1)S(1)}, u32[]{:S(2)}, u32[]{:S(2)}) %collective-permute-start.11) | collective-permute-done | bytes 131104 | tf_op jit(solution)/shard_map/ppermute | solution.py:41
  165.7 0.8 add_bitcast_fusion
  (19 shorter events, 2.8 us)
Async XLA Ops:
  0.6 15.5 %all-to-all-start = ((bf16[8,16,1024]{2,1,0:T(8,128)(2,1)}), bf16[8,16,1024]{2,1,0:T(8,128)(2,1)S(1)}, u32[]{:S(2)}, u32[]{:S(2)}) async-start(bf16[8,16,1024]{2,1,0:T(8,128)(2,1)} %bitcast.17), calls=%async_computation | async-start | bytes 524288 | tf_op jit(solution)/shard_map/all_to_all | solution.py:45
  16.1 75.4 %copy-start.1 = (bf16[1,128,512]{2,1,0:T(8,128)(2,1)S(1)}, bf16[1,128,512]{2,1,0:T(8,128)(2,1)}, u32[]{:S(2)}) copy-start(bf16[1,128,512]{2,1,0:T(8,128)(2,1)} %param.10) | copy-start | bytes 393220
  16.2 88.4 %copy-start = (bf16[1,128,512]{2,1,0:T(8,128)(2,1)S(1)}, bf16[1,128,512]{2,1,0:T(8,128)(2,1)}, u32[]{:S(2)}) copy-start(bf16[1,128,512]{2,1,0:T(8,128)(2,1)} %query_hbm.1) | copy-start | bytes 393220
  45.0 40.1 %all-to-all-start.2 = ((bf16[8,4,32,128]{3,2,1,0:T(8,128)(2,1)}), bf16[8,4,32,128]{3,2,1,0:T(8,128)(2,1)S(1)}, u32[]{:S(2)}, u32[]{:S(2)}) async-start(bf16[8,4,32,128]{3,2,1,0:T(8,128)(2,1)} %bitcast.6), calls=%async_computation.2 | async-start | bytes 524288 | tf_op jit(solution)/shard_map/all_to_all | solution.py:45
  68.7 34.1 %collective-permute-start = (bf16[2,128,512]{2,1,0:T(8,128)(2,1)S(1)}, bf16[2,128,512]{2,1,0:T(8,128)(2,1)S(1)}, u32[]{:S(2)}, u32[]{:S(2)}) collective-permute-start(bf16[2,128,512]{2,1,0:T(8,128)(2,1)S(1)} %get-tuple-element.15.own_ref), channel_id=1, source_target_pairs={{0,4},{4,8},{8,12},{12,16},{16,20},{20,24},{24,28},{28,32},{32,36}... | collective-permute-start | bytes 786440 | tf_op jit(solution)/shard_map/ppermute | solution.py:31
  73.0 29.9 %collective-permute-start.1 = (bf16[2,128,512]{2,1,0:T(8,128)(2,1)S(1)}, bf16[2,128,512]{2,1,0:T(8,128)(2,1)S(1)}, u32[]{:S(2)}, u32[]{:S(2)}) collective-permute-start(bf16[2,128,512]{2,1,0:T(8,128)(2,1)S(1)} %get-tuple-element.15.own_ref), channel_id=1, source_target_pairs={{0,8},{4,12},{8,16},{12,20},{16,24},{20,28},{24,32},{28,36},{32,40... | collective-permute-start | bytes 786440 | tf_op jit(solution)/shard_map/ppermute | solution.py:31
  85.1 0.7 copy-start.2
  87.8 61.7 %all-to-all-start.3 = ((bf16[4,8,4,32,128]{4,3,2,1,0:T(8,128)(2,1)}), bf16[4,8,4,32,128]{4,3,2,1,0:T(8,128)(2,1)S(1)}, u32[]{:S(2)}, u32[]{:S(2)}) async-start(bf16[4,8,4,32,128]{4,3,2,1,0:T(8,128)(2,1)} %shard_map.116), calls=%async_computation.3 | async-start | bytes 2097152 | tf_op jit(solution)/shard_map/all_to_all | solution.py:45
  91.5 8.5 %collective-permute-start.4 = (bf16[128,512]{1,0:T(8,128)(2,1)S(1)}, bf16[128,512]{1,0:T(8,128)(2,1)S(1)}, u32[]{:S(2)}, u32[]{:S(2)}) collective-permute-start(bf16[128,512]{1,0:T(8,128)(2,1)S(1)} %bitcast.13), channel_id=1, source_target_pairs={{0,16},{16,32},{32,48},{48,64},{64,80},{80,96},{96,112},{112,0},{1... | collective-permute-start | bytes 393224 | tf_op jit(solution)/shard_map/ppermute | solution.py:36
  94.9 27.7 %collective-permute-start.5 = (bf16[128,512]{1,0:T(8,128)(2,1)S(1)}, bf16[128,512]{1,0:T(8,128)(2,1)S(1)}, u32[]{:S(2)}, u32[]{:S(2)}) collective-permute-start(bf16[128,512]{1,0:T(8,128)(2,1)S(1)} %bitcast.14), channel_id=1, source_target_pairs={{0,112},{16,0},{32,16},{48,32},{64,48},{80,64},{96,80},{112,96},{1... | collective-permute-start | bytes 393224 | tf_op jit(solution)/shard_map/ppermute | solution.py:36
  100.0 27.9 %collective-permute-start.6 = (bf16[128,512]{1,0:T(8,128)(2,1)S(1)}, bf16[128,512]{1,0:T(8,128)(2,1)S(1)}, u32[]{:S(2)}, u32[]{:S(2)}) collective-permute-start(bf16[128,512]{1,0:T(8,128)(2,1)S(1)} %collective-permute-done.4.refs_1_), channel_id=1, source_target_pairs={{0,16},{16,32},{32,48},{48,64},{64,80},{80,96},{96,112},{112,0},{1... | collective-permute-start | bytes 393224 | tf_op jit(solution)/shard_map/ppermute | solution.py:36
  109.8 31.4 %collective-permute-start.3 = (bf16[2,128,512]{2,1,0:T(8,128)(2,1)S(1)}, bf16[2,128,512]{2,1,0:T(8,128)(2,1)S(1)}, u32[]{:S(2)}, u32[]{:S(2)}) collective-permute-start(bf16[2,128,512]{2,1,0:T(8,128)(2,1)S(1)} %get-tuple-element.19), channel_id=1, source_target_pairs={{0,120},{4,124},{8,0},{12,4},{16,8},{20,12},{24,16},{28,20},{32,24... | collective-permute-start | bytes 786440 | tf_op jit(solution)/shard_map/ppermute | solution.py:31
  112.9 28.3 %collective-permute-start.2 = (bf16[2,128,512]{2,1,0:T(8,128)(2,1)S(1)}, bf16[2,128,512]{2,1,0:T(8,128)(2,1)S(1)}, u32[]{:S(2)}, u32[]{:S(2)}) collective-permute-start(bf16[2,128,512]{2,1,0:T(8,128)(2,1)S(1)} %get-tuple-element.18), channel_id=1, source_target_pairs={{0,124},{4,0},{8,4},{12,8},{16,12},{20,16},{24,20},{28,24},{32,28}... | collective-permute-start | bytes 786440 | tf_op jit(solution)/shard_map/ppermute | solution.py:31
  122.5 9.2 %collective-permute-start.7 = (bf16[128,512]{1,0:T(8,128)(2,1)S(1)}, bf16[128,512]{1,0:T(8,128)(2,1)S(1)}, u32[]{:S(2)}, u32[]{:S(2)}) collective-permute-start(bf16[128,512]{1,0:T(8,128)(2,1)S(1)} %collective-permute-done.5.refs_2_), channel_id=1, source_target_pairs={{0,112},{16,0},{32,16},{48,32},{64,48},{80,64},{96,80},{112,96},{1... | collective-permute-start | bytes 393224 | tf_op jit(solution)/shard_map/ppermute | solution.py:36
  127.9 11.4 %collective-permute-start.8 = (bf16[128,512]{1,0:T(8,128)(2,1)S(1)}, bf16[128,512]{1,0:T(8,128)(2,1)S(1)}, u32[]{:S(2)}, u32[]{:S(2)}) collective-permute-start(bf16[128,512]{1,0:T(8,128)(2,1)S(1)} %collective-permute-done.6.refs_3_), channel_id=1, source_target_pairs={{0,16},{16,32},{32,48},{48,64},{64,80},{80,96},{96,112},{112,0},{1... | collective-permute-start | bytes 393224 | tf_op jit(solution)/shard_map/ppermute | solution.py:36
  131.7 10.8 %collective-permute-start.9 = (bf16[128,512]{1,0:T(8,128)(2,1)S(1)}, bf16[128,512]{1,0:T(8,128)(2,1)S(1)}, u32[]{:S(2)}, u32[]{:S(2)}) collective-permute-start(bf16[128,512]{1,0:T(8,128)(2,1)S(1)} %collective-permute-done.7.refs_4_), channel_id=1, source_target_pairs={{0,112},{16,0},{32,16},{48,32},{64,48},{80,64},{96,80},{112,96},{1... | collective-permute-start | bytes 393224 | tf_op jit(solution)/shard_map/ppermute | solution.py:36
  139.3 10.2 %collective-permute-start.10 = (bf16[128,512]{1,0:T(8,128)(2,1)S(1)}, bf16[128,512]{1,0:T(8,128)(2,1)S(1)}, u32[]{:S(2)}, u32[]{:S(2)}) collective-permute-start(bf16[128,512]{1,0:T(8,128)(2,1)S(1)} %collective-permute-done.8.refs_5_), channel_id=1, source_target_pairs={{0,16},{16,32},{32,48},{48,64},{64,80},{80,96},{96,112},{112,0},{1... | collective-permute-start | bytes 393224 | tf_op jit(solution)/shard_map/ppermute | solution.py:36
  150.2 10.9 %collective-permute-start.13 = (bf16[128,512]{1,0:T(8,128)(2,1)S(1)}, bf16[128,512]{1,0:T(8,128)(2,1)S(1)}, u32[]{:S(2)}, u32[]{:S(2)}) collective-permute-start(bf16[128,512]{1,0:T(8,128)(2,1)S(1)} %get-tuple-element.23), channel_id=1, source_target_pairs={{0,4},{4,0},{8,12},{12,8},{1,5},{5,1},{9,13},{13,9},{2,6},{6,2},{1... | collective-permute-start | bytes 393224 | tf_op jit(solution)/shard_map/ppermute | solution.py:41
  152.8 9.4 %collective-permute-start.12 = (bf16[128,512]{1,0:T(8,128)(2,1)S(1)}, bf16[128,512]{1,0:T(8,128)(2,1)S(1)}, u32[]{:S(2)}, u32[]{:S(2)}) collective-permute-start(bf16[128,512]{1,0:T(8,128)(2,1)S(1)} %get-tuple-element.22), channel_id=1, source_target_pairs={{0,8},{4,12},{8,0},{12,4},{1,9},{5,13},{9,1},{13,5},{2,10},{6,14},... | collective-permute-start | bytes 393224 | tf_op jit(solution)/shard_map/ppermute | solution.py:41
  158.4 7.3 %collective-permute-start.11 = (bf16[128,512]{1,0:T(8,128)(2,1)S(1)}, bf16[128,512]{1,0:T(8,128)(2,1)S(1)}, u32[]{:S(2)}, u32[]{:S(2)}) collective-permute-start(bf16[128,512]{1,0:T(8,128)(2,1)S(1)} %get-tuple-element.21), channel_id=1, source_target_pairs={{0,12},{4,8},{8,4},{12,0},{1,13},{5,9},{9,5},{13,1},{2,14},{6,10},... | collective-permute-start | bytes 393224 | tf_op jit(solution)/shard_map/ppermute | solution.py:41

commit v6 on v5

--- a/solution.py
+++ b/solution.py
@@ -71,17 +71,22 @@
         own = layers_ref[layer].astype(F32)
         upper = own if upper is None else upper + own
         grads = (base + 0.25 * upper).astype(BF16)
-        for copy in range(grads_ref.shape[0]):
-            grads_ref[copy, layer] = grads
+        for copy in range(grads_ref.shape[1]):
+            grads_ref[layer, copy] = grads
 
 
 def quarter_kernel(grad_ref, mine_ref):
+    _, tensors, slab_rows, _ = grad_ref.shape
     blocks, rows, lanes = mine_ref.shape
-    each = blocks // grad_ref.shape[0]
-    at = pl.multiple_of(lax.axis_index("tensor") * rows, rows)
+    each = blocks // tensors
+    slabs = rows // slab_rows
+    at = lax.axis_index("tensor") * slabs
     for block in range(blocks):
         first = block % each * lanes
-        mine_ref[block] = grad_ref[block // each, pl.ds(at, rows), first : first + lanes]
+        for slab in range(slabs):
+            mine_ref[block, slab * slab_rows : (slab + 1) * slab_rows] = grad_ref[
+                at + slab, block // each, :, first : first + lanes
+            ]
 
 
 def repeat_kernel(value_ref, repeated_ref, held_ref, sems):
@@ -140,7 +145,8 @@
     query_grad_ref, own_part_ref, near_part_ref, far_part_ref,
     weight_ref, sems,
 ):
-    parts, rows, depth = grad_ref.shape
+    slabs, parts, _, depth = grad_ref.shape
+    rows = query_ref.shape[0]
     copies = [
         pltpu.make_async_copy(
             weight_hbm.at[0, pl.ds(part * depth, depth)],
@@ -154,8 +160,9 @@
     total = None
     for part in range(parts):
         copies[part].wait()
+        grad = jnp.concatenate([grad_ref[slab, part] for slab in range(slabs)], axis=0)
         term = jnp.dot(
-            grad_ref[part],
+            grad,
             weight_ref[part * depth : (part + 1) * depth, :],
             preferred_element_type=F32,
         )
@@ -257,15 +264,15 @@
     far = shifted(held, 2)
     (grads,) = call(
         suffix_kernel,
-        [shape((tensors, *slab), BF16)],
+        [shape((sections, tensors, *slab[1:]), BF16)],
         (base, layers),
         [WHOLE] * 2,
         layers.size * 3,
         layers.size * 4,
     )
     grad_full = exchanged(
-        grads.reshape(tensors * sections, *slab[1:]), ("tensor", "section")
-    ).reshape(tensors, rows, features)
+        grads.reshape(sections * tensors, *slab[1:]), ("section", "tensor")
+    ).reshape(grads.shape)
     (prob,) = call(
         prob_kernel,
         [shape((heads, rows, window), F32)],

time: 167 us -> 168 us (level)
  the two profiles are of different devices: /device:TPU:11 before, /device:TPU:1 now
where the time goes in v6:
time: 168 us; the launch traced here: 167 us
  starting transfers between devices  93.4 us (56%)
  waiting for transfers between devices  31.7 us (19%)
  blocking collectives  27.1 us (16%)
  Pallas kernels  11.5 us (7%)
    all_to_all x3, starting transfers between devices, exchanged(): return lax.all_to_all(value, axis, 0, 0, tiled=True)  35.8 us
    all_to_all x1, blocking collectives, exchanged(): return lax.all_to_all(value, axis, 0, 0, tiled=True)  27.1 us
    ppermute x7, starting transfers between devices, turned(): lax.ppermute(value, axis, [(i, (i + steps) % count) for i in range(count)])  26.2 us
    ppermute x4, starting transfers between devices, shifted(): lax.ppermute(value, DP, [(i, (i + steps) % count) for i in range(count)])  20.6 us
    all_to_all x3, waiting for transfers between devices, exchanged(): return lax.all_to_all(value, axis, 0, 0, tiled=True)  16.8 us
    pallas_call x7, Pallas kernels, call(): pl.pallas_call(kernel, out_shape=outs, in_specs=specs, out_specs=[out_spe...  11.5 us
    ppermute x3, starting transfers between devices, swapped(): return lax.ppermute(value, GROUP, [(i, i ^ mask) for i in range(count)])  10.8 us
    ppermute x7, waiting for transfers between devices, turned(): lax.ppermute(value, axis, [(i, (i + steps) % count) for i in range(count)])  10.2 us
  transfers between devices with their start and end apart: 17, of which 9 were waited for; matrix products, arithmetic and copies ran while one was open for 0% of the time, Pallas kernels for 6%

profile of v6, /device:TPU:1, one launch (start us, length us, event | category | flops | bytes accessed | tf_op | source)
XLA Modules:
  0.0 166.9 jit_solution(9578418229829593846)
XLA Ops:
  0.6 7.7 %all-to-all-start = ((bf16[8,16,1024]{2,1,0:T(8,128)(2,1)}), bf16[8,16,1024]{2,1,0:T(8,128)(2,1)S(1)}, u32[]{:S(2)}, u32[]{:S(2)}) async-start(bf16[8,16,1024]{2,1,0:T(8,128)(2,1)} %bitcast.17), calls=%async_computation | async-start | bytes 524288 | tf_op jit(solution)/shard_map/all_to_all | solution.py:45
  8.3 1.0 shard_map.111
  9.3 8.3 %all-to-all-done.layers_ref = bf16[8,16,1024]{2,1,0:T(8,128)(2,1)S(1)} async-done(((bf16[8,16,1024]{2,1,0:T(8,128)(2,1)}), bf16[8,16,1024]{2,1,0:T(8,128)(2,1)S(1)}, u32[]{:S(2)}, u32[]{:S(2)}) %all-to-all-start) | async-done | bytes 262176 | tf_op jit(solution)/shard_map/all_to_all | solution.py:45
  17.7 27.1 %all_to_all.20 = bf16[32,16,1024]{2,1,0:T(8,128)(2,1)S(1)} all-to-all(bf16[32,16,1024]{2,1,0:T(8,128)(2,1)S(1)} %bitcast.11), channel_id=1, replica_groups=mesh['section'=8,'zh'=8,'zl'=2,'core'=2,'tensor'=4] {'section','tensor'}, dimensions={0} | all-to-all | bytes 2097152 | tf_op jit(solution)/shard_map/all_to_all | solution.py:45
  45.6 23.9 %all-to-all-start.2 = ((bf16[8,4,32,128]{3,2,1,0:T(8,128)(2,1)}), bf16[8,4,32,128]{3,2,1,0:T(8,128)(2,1)S(1)}, u32[]{:S(2)}, u32[]{:S(2)}) async-start(bf16[8,4,32,128]{3,2,1,0:T(8,128)(2,1)} %bitcast.6), calls=%async_computation.2 | async-start | bytes 524288 | tf_op jit(solution)/shard_map/all_to_all | solution.py:45
  69.5 4.5 %collective-permute-start = (bf16[2,128,512]{2,1,0:T(8,128)(2,1)S(1)}, bf16[2,128,512]{2,1,0:T(8,128)(2,1)S(1)}, u32[]{:S(2)}, u32[]{:S(2)}) collective-permute-start(bf16[2,128,512]{2,1,0:T(8,128)(2,1)S(1)} %get-tuple-element.15.own_ref), channel_id=1, source_target_pairs={{0,4},{4,8},{8,12},{12,16},{16,20},{20,24},{24,28},{28,32},{32,36}... | collective-permute-start | bytes 786440 | tf_op jit(solution)/shard_map/ppermute | solution.py:31
  73.9 3.6 %collective-permute-start.1 = (bf16[2,128,512]{2,1,0:T(8,128)(2,1)S(1)}, bf16[2,128,512]{2,1,0:T(8,128)(2,1)S(1)}, u32[]{:S(2)}, u32[]{:S(2)}) collective-permute-start(bf16[2,128,512]{2,1,0:T(8,128)(2,1)S(1)} %get-tuple-element.15.own_ref), channel_id=1, source_target_pairs={{0,8},{4,12},{8,16},{12,20},{16,24},{20,28},{24,32},{28,36},{32,40... | collective-permute-start | bytes 786440 | tf_op jit(solution)/shard_map/ppermute | solution.py:31
  77.6 8.5 %all-to-all-done.2.value_ref = bf16[8,4,32,128]{3,2,1,0:T(8,128)(2,1)S(1)} async-done(((bf16[8,4,32,128]{3,2,1,0:T(8,128)(2,1)}), bf16[8,4,32,128]{3,2,1,0:T(8,128)(2,1)S(1)}, u32[]{:S(2)}, u32[]{:S(2)}) %all-to-all-start.2) | async-done | bytes 262176 | tf_op jit(solution)/shard_map/all_to_all | solution.py:45
  86.8 2.0 %shard_map.116 = bf16[4,8,4,32,128]{4,3,2,1,0:T(8,128)(2,1)} custom-call(bf16[8,4,32,128]{3,2,1,0:T(8,128)(2,1)} %copy-done.2), custom_call_target="tpu_custom_call" | custom-call | bytes 1310720 | tf_op jit(solution)/shard_map/pallas_call | solution.py:220
  88.8 4.3 %all-to-all-start.3 = ((bf16[4,8,4,32,128]{4,3,2,1,0:T(8,128)(2,1)}), bf16[4,8,4,32,128]{4,3,2,1,0:T(8,128)(2,1)S(1)}, u32[]{:S(2)}, u32[]{:S(2)}) async-start(bf16[4,8,4,32,128]{4,3,2,1,0:T(8,128)(2,1)} %shard_map.116), calls=%async_computation.3 | async-start | bytes 2097152 | tf_op jit(solution)/shard_map/all_to_all | solution.py:45
  93.1 3.1 %collective-permute-start.4 = (bf16[128,512]{1,0:T(8,128)(2,1)S(1)}, bf16[128,512]{1,0:T(8,128)(2,1)S(1)}, u32[]{:S(2)}, u32[]{:S(2)}) collective-permute-start(bf16[128,512]{1,0:T(8,128)(2,1)S(1)} %bitcast.13), channel_id=1, source_target_pairs={{0,16},{16,32},{32,48},{48,64},{64,80},{80,96},{96,112},{112,0},{1... | collective-permute-start | bytes 393224 | tf_op jit(solution)/shard_map/ppermute | solution.py:36
  96.2 4.9 %collective-permute-start.5 = (bf16[128,512]{1,0:T(8,128)(2,1)S(1)}, bf16[128,512]{1,0:T(8,128)(2,1)S(1)}, u32[]{:S(2)}, u32[]{:S(2)}) collective-permute-start(bf16[128,512]{1,0:T(8,128)(2,1)S(1)} %bitcast.14), channel_id=1, source_target_pairs={{0,112},{16,0},{32,16},{48,32},{64,48},{80,64},{96,80},{112,96},{1... | collective-permute-start | bytes 393224 | tf_op jit(solution)/shard_map/ppermute | solution.py:36
  101.5 2.7 %collective-permute-start.6 = (bf16[128,512]{1,0:T(8,128)(2,1)S(1)}, bf16[128,512]{1,0:T(8,128)(2,1)S(1)}, u32[]{:S(2)}, u32[]{:S(2)}) collective-permute-start(bf16[128,512]{1,0:T(8,128)(2,1)S(1)} %collective-permute-done.4.refs_1_), channel_id=1, source_target_pairs={{0,16},{16,32},{32,48},{48,64},{64,80},{80,96},{96,112},{112,0},{1... | collective-permute-start | bytes 393224 | tf_op jit(solution)/shard_map/ppermute | solution.py:36
  104.2 1.7 %shard_map.113.prob_ref = f32[4,128,384]{2,1,0:T(8,128)S(1)} custom-call(s32[32]{0:T(128)} %lengths_hbm.1, bf16[1,128,512]{2,1,0:T(8,128)(2,1)} %query_hbm.1, bf16[2,128,512]{2,1,0:T(8,128)(2,1)S(1)} %get-tuple-element.15.own_ref, bf16[2,128,512]{2,1,0:T(8,128)(2,1)S(1)} %collective-permute-done.near_ref, bf16[2,128,512]{2,1,0:T(8,128)(2,1)S(1)} %collective-permute-done.1.far_ref), custom_call_target="tpu_custom_call" | custom-call | flops 52297728 | bytes 1572864 | tf_op jit(solution)/shard_map/pallas_call | solution.py:220
  106.0 5.2 %shard_map.114 = (bf16[128,512]{1,0:T(8,128)(2,1)}, f32[2,128,512]{2,1,0:T(8,128)S(1)}, bf16[2,128,512]{2,1,0:T(8,128)(2,1)S(1)}, bf16[2,128,512]{2,1,0:T(8,128)(2,1)S(1)}) custom-call(bf16[8,4,16,1024]{3,2,1,0:T(8,128)(2,1)S(1)} %bitcast.10, bf16[1,4096,512]{2,1,0:T(8,128)(2,1)} %weight_hbm.1, f32[4,128,384]{2,1,0:T(8,128)S(1)} %shard_map.113.prob_ref, ...), custom_call_target="tpu_custom_call" | custom-call | flops 738197504 | bytes 4194304 | tf_op jit(solution)/shard_map/pallas_call | solution.py:220
  111.2 3.1 %collective-permute-start.3 = (bf16[2,128,512]{2,1,0:T(8,128)(2,1)S(1)}, bf16[2,128,512]{2,1,0:T(8,128)(2,1)S(1)}, u32[]{:S(2)}, u32[]{:S(2)}) collective-permute-start(bf16[2,128,512]{2,1,0:T(8,128)(2,1)S(1)} %get-tuple-element.19), channel_id=1, source_target_pairs={{0,120},{4,124},{8,0},{12,4},{16,8},{20,12},{24,16},{28,20},{32,24... | collective-permute-start | bytes 786440 | tf_op jit(solution)/shard_map/ppermute | solution.py:31
  114.3 9.5 %collective-permute-start.2 = (bf16[2,128,512]{2,1,0:T(8,128)(2,1)S(1)}, bf16[2,128,512]{2,1,0:T(8,128)(2,1)S(1)}, u32[]{:S(2)}, u32[]{:S(2)}) collective-permute-start(bf16[2,128,512]{2,1,0:T(8,128)(2,1)S(1)} %get-tuple-element.18), channel_id=1, source_target_pairs={{0,124},{4,0},{8,4},{12,8},{16,12},{20,16},{24,20},{28,24},{32,28}... | collective-permute-start | bytes 786440 | tf_op jit(solution)/shard_map/ppermute | solution.py:31
  123.7 5.0 %collective-permute-start.7 = (bf16[128,512]{1,0:T(8,128)(2,1)S(1)}, bf16[128,512]{1,0:T(8,128)(2,1)S(1)}, u32[]{:S(2)}, u32[]{:S(2)}) collective-permute-start(bf16[128,512]{1,0:T(8,128)(2,1)S(1)} %collective-permute-done.5.refs_2_), channel_id=1, source_target_pairs={{0,112},{16,0},{32,16},{48,32},{64,48},{80,64},{96,80},{112,96},{1... | collective-permute-start | bytes 393224 | tf_op jit(solution)/shard_map/ppermute | solution.py:36
  128.8 1.9 %collective-permute-start.8 = (bf16[128,512]{1,0:T(8,128)(2,1)S(1)}, bf16[128,512]{1,0:T(8,128)(2,1)S(1)}, u32[]{:S(2)}, u32[]{:S(2)}) collective-permute-start(bf16[128,512]{1,0:T(8,128)(2,1)S(1)} %collective-permute-done.6.refs_3_), channel_id=1, source_target_pairs={{0,16},{16,32},{32,48},{48,64},{64,80},{80,96},{96,112},{112,0},{1... | collective-permute-start | bytes 393224 | tf_op jit(solution)/shard_map/ppermute | solution.py:36
  130.7 1.9 %collective-permute-done.7.refs_4_ = bf16[128,512]{1,0:T(8,128)(2,1)S(1)} collective-permute-done((bf16[128,512]{1,0:T(8,128)(2,1)S(1)}, bf16[128,512]{1,0:T(8,128)(2,1)S(1)}, u32[]{:S(2)}, u32[]{:S(2)}) %collective-permute-start.7) | collective-permute-done | bytes 131104 | tf_op jit(solution)/shard_map/ppermute | solution.py:36
  132.6 6.6 %collective-permute-start.9 = (bf16[128,512]{1,0:T(8,128)(2,1)S(1)}, bf16[128,512]{1,0:T(8,128)(2,1)S(1)}, u32[]{:S(2)}, u32[]{:S(2)}) collective-permute-start(bf16[128,512]{1,0:T(8,128)(2,1)S(1)} %collective-permute-done.7.refs_4_), channel_id=1, source_target_pairs={{0,112},{16,0},{32,16},{48,32},{64,48},{80,64},{96,80},{112,96},{1... | collective-permute-start | bytes 393224 | tf_op jit(solution)/shard_map/ppermute | solution.py:36
  139.2 0.9 collective-permute-done.8.refs_5_
  140.1 1.9 %collective-permute-start.10 = (bf16[128,512]{1,0:T(8,128)(2,1)S(1)}, bf16[128,512]{1,0:T(8,128)(2,1)S(1)}, u32[]{:S(2)}, u32[]{:S(2)}) collective-permute-start(bf16[128,512]{1,0:T(8,128)(2,1)S(1)} %collective-permute-done.8.refs_5_), channel_id=1, source_target_pairs={{0,16},{16,32},{32,48},{48,64},{64,80},{80,96},{96,112},{112,0},{1... | collective-permute-start | bytes 393224 | tf_op jit(solution)/shard_map/ppermute | solution.py:36
  142.2 0.8 collective-permute-done.9.refs_6_
  143.0 6.1 %collective-permute-done.10.refs_7_ = bf16[128,512]{1,0:T(8,128)(2,1)S(1)} collective-permute-done((bf16[128,512]{1,0:T(8,128)(2,1)S(1)}, bf16[128,512]{1,0:T(8,128)(2,1)S(1)}, u32[]{:S(2)}, u32[]{:S(2)}) %collective-permute-start.10) | collective-permute-done | bytes 131104 | tf_op jit(solution)/shard_map/ppermute | solution.py:36
  149.2 0.8 shard_map.117
  149.9 3.3 %collective-permute-start.13 = (bf16[128,512]{1,0:T(8,128)(2,1)S(1)}, bf16[128,512]{1,0:T(8,128)(2,1)S(1)}, u32[]{:S(2)}, u32[]{:S(2)}) collective-permute-start(bf16[128,512]{1,0:T(8,128)(2,1)S(1)} %get-tuple-element.23), channel_id=1, source_target_pairs={{0,4},{4,0},{8,12},{12,8},{1,5},{5,1},{9,13},{13,9},{2,6},{6,2},{1... | collective-permute-start | bytes 393224 | tf_op jit(solution)/shard_map/ppermute | solution.py:41
  153.3 5.6 %collective-permute-start.12 = (bf16[128,512]{1,0:T(8,128)(2,1)S(1)}, bf16[128,512]{1,0:T(8,128)(2,1)S(1)}, u32[]{:S(2)}, u32[]{:S(2)}) collective-permute-start(bf16[128,512]{1,0:T(8,128)(2,1)S(1)} %get-tuple-element.22), channel_id=1, source_target_pairs={{0,8},{4,12},{8,0},{12,4},{1,9},{5,13},{9,1},{13,5},{2,10},{6,14},... | collective-permute-start | bytes 393224 | tf_op jit(solution)/shard_map/ppermute | solution.py:41
  158.9 1.9 %collective-permute-start.11 = (bf16[128,512]{1,0:T(8,128)(2,1)S(1)}, bf16[128,512]{1,0:T(8,128)(2,1)S(1)}, u32[]{:S(2)}, u32[]{:S(2)}) collective-permute-start(bf16[128,512]{1,0:T(8,128)(2,1)S(1)} %get-tuple-element.21), channel_id=1, source_target_pairs={{0,12},{4,8},{8,4},{12,0},{1,13},{5,9},{9,5},{13,1},{2,14},{6,10},... | collective-permute-start | bytes 393224 | tf_op jit(solution)/shard_map/ppermute | solution.py:41
  161.5 1.2 collective-permute-done.12
  162.7 3.4 %collective-permute-done.11 = bf16[128,512]{1,0:T(8,128)(2,1)S(1)} collective-permute-done((bf16[128,512]{1,0:T(8,128)(2,1)S(1)}, bf16[128,512]{1,0:T(8,128)(2,1)S(1)}, u32[]{:S(2)}, u32[]{:S(2)}) %collective-permute-start.11) | collective-permute-done | bytes 131104 | tf_op jit(solution)/shard_map/ppermute | solution.py:41
  166.1 0.8 add_bitcast_fusion
  (19 shorter events, 2.8 us)
Async XLA Ops:
  0.6 17.0 %all-to-all-start = ((bf16[8,16,1024]{2,1,0:T(8,128)(2,1)}), bf16[8,16,1024]{2,1,0:T(8,128)(2,1)S(1)}, u32[]{:S(2)}, u32[]{:S(2)}) async-start(bf16[8,16,1024]{2,1,0:T(8,128)(2,1)} %bitcast.17), calls=%async_computation | async-start | bytes 524288 | tf_op jit(solution)/shard_map/all_to_all | solution.py:45
  17.6 75.5 %copy-start.1 = (bf16[1,128,512]{2,1,0:T(8,128)(2,1)S(1)}, bf16[1,128,512]{2,1,0:T(8,128)(2,1)}, u32[]{:S(2)}) copy-start(bf16[1,128,512]{2,1,0:T(8,128)(2,1)} %param.10) | copy-start | bytes 393220
  17.7 88.3 %copy-start = (bf16[1,128,512]{2,1,0:T(8,128)(2,1)S(1)}, bf16[1,128,512]{2,1,0:T(8,128)(2,1)}, u32[]{:S(2)}) copy-start(bf16[1,128,512]{2,1,0:T(8,128)(2,1)} %query_hbm.1) | copy-start | bytes 393220
  45.6 40.5 %all-to-all-start.2 = ((bf16[8,4,32,128]{3,2,1,0:T(8,128)(2,1)}), bf16[8,4,32,128]{3,2,1,0:T(8,128)(2,1)S(1)}, u32[]{:S(2)}, u32[]{:S(2)}) async-start(bf16[8,4,32,128]{3,2,1,0:T(8,128)(2,1)} %bitcast.6), calls=%async_computation.2 | async-start | bytes 524288 | tf_op jit(solution)/shard_map/all_to_all | solution.py:45
  69.5 34.8 %collective-permute-start = (bf16[2,128,512]{2,1,0:T(8,128)(2,1)S(1)}, bf16[2,128,512]{2,1,0:T(8,128)(2,1)S(1)}, u32[]{:S(2)}, u32[]{:S(2)}) collective-permute-start(bf16[2,128,512]{2,1,0:T(8,128)(2,1)S(1)} %get-tuple-element.15.own_ref), channel_id=1, source_target_pairs={{0,4},{4,8},{8,12},{12,16},{16,20},{20,24},{24,28},{28,32},{32,36}... | collective-permute-start | bytes 786440 | tf_op jit(solution)/shard_map/ppermute | solution.py:31
  73.9 30.3 %collective-permute-start.1 = (bf16[2,128,512]{2,1,0:T(8,128)(2,1)S(1)}, bf16[2,128,512]{2,1,0:T(8,128)(2,1)S(1)}, u32[]{:S(2)}, u32[]{:S(2)}) collective-permute-start(bf16[2,128,512]{2,1,0:T(8,128)(2,1)S(1)} %get-tuple-element.15.own_ref), channel_id=1, source_target_pairs={{0,8},{4,12},{8,16},{12,20},{16,24},{20,28},{24,32},{28,36},{32,40... | collective-permute-start | bytes 786440 | tf_op jit(solution)/shard_map/ppermute | solution.py:31
  86.1 0.7 copy-start.2
  88.8 60.4 %all-to-all-start.3 = ((bf16[4,8,4,32,128]{4,3,2,1,0:T(8,128)(2,1)}), bf16[4,8,4,32,128]{4,3,2,1,0:T(8,128)(2,1)S(1)}, u32[]{:S(2)}, u32[]{:S(2)}) async-start(bf16[4,8,4,32,128]{4,3,2,1,0:T(8,128)(2,1)} %shard_map.116), calls=%async_computation.3 | async-start | bytes 2097152 | tf_op jit(solution)/shard_map/all_to_all | solution.py:45
  93.1 8.4 %collective-permute-start.4 = (bf16[128,512]{1,0:T(8,128)(2,1)S(1)}, bf16[128,512]{1,0:T(8,128)(2,1)S(1)}, u32[]{:S(2)}, u32[]{:S(2)}) collective-permute-start(bf16[128,512]{1,0:T(8,128)(2,1)S(1)} %bitcast.13), channel_id=1, source_target_pairs={{0,16},{16,32},{32,48},{48,64},{64,80},{80,96},{96,112},{112,0},{1... | collective-permute-start | bytes 393224 | tf_op jit(solution)/shard_map/ppermute | solution.py:36
  96.2 27.5 %collective-permute-start.5 = (bf16[128,512]{1,0:T(8,128)(2,1)S(1)}, bf16[128,512]{1,0:T(8,128)(2,1)S(1)}, u32[]{:S(2)}, u32[]{:S(2)}) collective-permute-start(bf16[128,512]{1,0:T(8,128)(2,1)S(1)} %bitcast.14), channel_id=1, source_target_pairs={{0,112},{16,0},{32,16},{48,32},{64,48},{80,64},{96,80},{112,96},{1... | collective-permute-start | bytes 393224 | tf_op jit(solution)/shard_map/ppermute | solution.py:36
  101.5 27.3 %collective-permute-start.6 = (bf16[128,512]{1,0:T(8,128)(2,1)S(1)}, bf16[128,512]{1,0:T(8,128)(2,1)S(1)}, u32[]{:S(2)}, u32[]{:S(2)}) collective-permute-start(bf16[128,512]{1,0:T(8,128)(2,1)S(1)} %collective-permute-done.4.refs_1_), channel_id=1, source_target_pairs={{0,16},{16,32},{32,48},{48,64},{64,80},{80,96},{96,112},{112,0},{1... | collective-permute-start | bytes 393224 | tf_op jit(solution)/shard_map/ppermute | solution.py:36
  111.2 30.9 %collective-permute-start.3 = (bf16[2,128,512]{2,1,0:T(8,128)(2,1)S(1)}, bf16[2,128,512]{2,1,0:T(8,128)(2,1)S(1)}, u32[]{:S(2)}, u32[]{:S(2)}) collective-permute-start(bf16[2,128,512]{2,1,0:T(8,128)(2,1)S(1)} %get-tuple-element.19), channel_id=1, source_target_pairs={{0,120},{4,124},{8,0},{12,4},{16,8},{20,12},{24,16},{28,20},{32,24... | collective-permute-start | bytes 786440 | tf_op jit(solution)/shard_map/ppermute | solution.py:31
  114.3 27.8 %collective-permute-start.2 = (bf16[2,128,512]{2,1,0:T(8,128)(2,1)S(1)}, bf16[2,128,512]{2,1,0:T(8,128)(2,1)S(1)}, u32[]{:S(2)}, u32[]{:S(2)}) collective-permute-start(bf16[2,128,512]{2,1,0:T(8,128)(2,1)S(1)} %get-tuple-element.18), channel_id=1, source_target_pairs={{0,124},{4,0},{8,4},{12,8},{16,12},{20,16},{24,20},{28,24},{32,28}... | collective-permute-start | bytes 786440 | tf_op jit(solution)/shard_map/ppermute | solution.py:31
  123.7 8.9 %collective-permute-start.7 = (bf16[128,512]{1,0:T(8,128)(2,1)S(1)}, bf16[128,512]{1,0:T(8,128)(2,1)S(1)}, u32[]{:S(2)}, u32[]{:S(2)}) collective-permute-start(bf16[128,512]{1,0:T(8,128)(2,1)S(1)} %collective-permute-done.5.refs_2_), channel_id=1, source_target_pairs={{0,112},{16,0},{32,16},{48,32},{64,48},{80,64},{96,80},{112,96},{1... | collective-permute-start | bytes 393224 | tf_op jit(solution)/shard_map/ppermute | solution.py:36
  128.8 11.4 %collective-permute-start.8 = (bf16[128,512]{1,0:T(8,128)(2,1)S(1)}, bf16[128,512]{1,0:T(8,128)(2,1)S(1)}, u32[]{:S(2)}, u32[]{:S(2)}) collective-permute-start(bf16[128,512]{1,0:T(8,128)(2,1)S(1)} %collective-permute-done.6.refs_3_), channel_id=1, source_target_pairs={{0,16},{16,32},{32,48},{48,64},{64,80},{80,96},{96,112},{112,0},{1... | collective-permute-start | bytes 393224 | tf_op jit(solution)/shard_map/ppermute | solution.py:36
  132.6 10.4 %collective-permute-start.9 = (bf16[128,512]{1,0:T(8,128)(2,1)S(1)}, bf16[128,512]{1,0:T(8,128)(2,1)S(1)}, u32[]{:S(2)}, u32[]{:S(2)}) collective-permute-start(bf16[128,512]{1,0:T(8,128)(2,1)S(1)} %collective-permute-done.7.refs_4_), channel_id=1, source_target_pairs={{0,112},{16,0},{32,16},{48,32},{64,48},{80,64},{96,80},{112,96},{1... | collective-permute-start | bytes 393224 | tf_op jit(solution)/shard_map/ppermute | solution.py:36
  140.1 9.0 %collective-permute-start.10 = (bf16[128,512]{1,0:T(8,128)(2,1)S(1)}, bf16[128,512]{1,0:T(8,128)(2,1)S(1)}, u32[]{:S(2)}, u32[]{:S(2)}) collective-permute-start(bf16[128,512]{1,0:T(8,128)(2,1)S(1)} %collective-permute-done.8.refs_5_), channel_id=1, source_target_pairs={{0,16},{16,32},{32,48},{48,64},{64,80},{80,96},{96,112},{112,0},{1... | collective-permute-start | bytes 393224 | tf_op jit(solution)/shard_map/ppermute | solution.py:36
  149.9 11.6 %collective-permute-start.13 = (bf16[128,512]{1,0:T(8,128)(2,1)S(1)}, bf16[128,512]{1,0:T(8,128)(2,1)S(1)}, u32[]{:S(2)}, u32[]{:S(2)}) collective-permute-start(bf16[128,512]{1,0:T(8,128)(2,1)S(1)} %get-tuple-element.23), channel_id=1, source_target_pairs={{0,4},{4,0},{8,12},{12,8},{1,5},{5,1},{9,13},{13,9},{2,6},{6,2},{1... | collective-permute-start | bytes 393224 | tf_op jit(solution)/shard_map/ppermute | solution.py:41
  153.3 9.4 %collective-permute-start.12 = (bf16[128,512]{1,0:T(8,128)(2,1)S(1)}, bf16[128,512]{1,0:T(8,128)(2,1)S(1)}, u32[]{:S(2)}, u32[]{:S(2)}) collective-permute-start(bf16[128,512]{1,0:T(8,128)(2,1)S(1)} %get-tuple-element.22), channel_id=1, source_target_pairs={{0,8},{4,12},{8,0},{12,4},{1,9},{5,13},{9,1},{13,5},{2,10},{6,14},... | collective-permute-start | bytes 393224 | tf_op jit(solution)/shard_map/ppermute | solution.py:41
  158.9 7.3 %collective-permute-start.11 = (bf16[128,512]{1,0:T(8,128)(2,1)S(1)}, bf16[128,512]{1,0:T(8,128)(2,1)S(1)}, u32[]{:S(2)}, u32[]{:S(2)}) collective-permute-start(bf16[128,512]{1,0:T(8,128)(2,1)S(1)} %get-tuple-element.21), channel_id=1, source_target_pairs={{0,12},{4,8},{8,4},{12,0},{1,13},{5,9},{9,5},{13,1},{2,14},{6,10},... | collective-permute-start | bytes 393224 | tf_op jit(solution)/shard_map/ppermute | solution.py:41

commit v7 on v4

--- a/solution.py
+++ b/solution.py
@@ -1,5 +1,3 @@
-import functools
-
 import jax
 import jax.numpy as jnp
 from jax import lax
@@ -75,9 +73,7 @@
     for layer in range(layers_ref.shape[0] - 1, -1, -1):
         own = layers_ref[layer].astype(F32)
         upper = own if upper is None else upper + own
-        grads = (base + 0.25 * upper).astype(BF16)
-        for copy in range(grads_ref.shape[0]):
-            grads_ref[copy, layer] = grads
+        grads_ref[layer] = (base + 0.25 * upper).astype(BF16)
 
 
 def quarter_kernel(grad_ref, mine_ref):
@@ -176,8 +172,8 @@
         query_grad_ref[:, cols] = query_grad.astype(BF16)
 
 
-def weight_kernel(masks, grad_ref, *refs):
-    quarters, blocks, _, rows, _ = grad_ref.shape
+def weight_kernel(grad_ref, *refs):
+    quarters, blocks, owners, rows, _ = grad_ref.shape
     context_refs, term_refs = refs[:blocks], refs[blocks:]
     here, me = lax.axis_index("zh"), lax.axis_index(GROUP)
     places = [lax.rem(here + steps, blocks) for steps in ring_steps(blocks)]
@@ -185,14 +181,14 @@
         jnp.concatenate([ref[quarter * rows : (quarter + 1) * rows] for ref in context_refs], axis=0)
         for quarter in range(quarters)
     ]
-    for mask, term_ref in zip(masks, term_refs):
+    for mask in range(owners):
         owner = jnp.bitwise_xor(me, mask)
         total = None
         for quarter in range(quarters):
             grad = jnp.concatenate([grad_ref[quarter, at, owner] for at in places], axis=0)
             term = contract(grad, contexts[quarter], 0, 0)
             total = term if total is None else total + term
-        term_ref[...] = total.astype(term_ref.dtype)
+        term_refs[mask][...] = total.astype(term_refs[mask].dtype)
 
 
 def ring_steps(count):
@@ -252,15 +248,14 @@
     far = shifted(held, 2)
     (grads,) = call(
         suffix_kernel,
-        [shape((tensors, *slab), BF16)],
+        [shape(slab, BF16)],
         (base, layers),
         [WHOLE] * 2,
         layers.size * 3,
         layers.size * 4,
     )
-    grad_full = exchanged(
-        grads.reshape(tensors * sections, *slab[1:]), ("tensor", "section")
-    ).reshape(tensors, rows, features)
+    grad_local = exchanged(grads, "section").reshape(rows, features)
+    grad_full = spread(grad_local, "tensor")
     (prob,) = call(
         prob_kernel,
         [shape((heads, rows, window), F32)],
@@ -306,21 +301,16 @@
     far_back = shifted(far_part, -2)
     sums = (own_part + near_back.astype(F32) + far_back.astype(F32)).astype(BF16)
 
-    def terms_for(masks, types):
-        return call(
-            functools.partial(weight_kernel, masks),
-            [shape((lanes, width), dtype) for dtype in types],
-            (columns_all, *blocks),
-            [WHOLE] * (1 + chips),
-            len(masks) * columns_all.size * width // 2,
-            2 * (columns_all.size + chips * context.size),
-        )
-
-    sent = range(owners - 1, 0, -1)
-    far_terms = terms_for(sent[:2], [BF16] * 2)
-    *near_terms, weight_grad = terms_for((*sent[2:], 0), [BF16] * len(sent[2:]) + [F32])
-    for mask, term in zip(sent, (*far_terms, *near_terms)):
-        other = swapped(term, mask)
+    weight_grad, *terms = call(
+        weight_kernel,
+        [shape((lanes, width), F32)] + [shape((lanes, width), BF16)] * (owners - 1),
+        (columns_all, *blocks),
+        [WHOLE] * (1 + chips),
+        2 * columns_all.size * width,
+        2 * (columns_all.size + chips * context.size),
+    )
+    for mask in range(1, owners):
+        other = swapped(terms[mask - 1], mask)
         weight_grad = weight_grad + other.astype(F32)
     return query_grad[None], sums[:1], sums[1:], weight_grad[None]
 

time: 166 us -> 160 us (0.964)
  starting transfers between devices: 93.6 us -> 89.6 us
    all_to_all x3, starting transfers between devices: 35.7 us -> 31.2 us  [exchanged(): return lax.all_to_all(value, axis, 0, 0, tiled=True)]
    ppermute x3, waiting for transfers between devices: 4.65 us -> 2.2 us  [swapped(): return lax.ppermute(value, GROUP, [(i, i ^ mask) for i in range(count)])]
    all_to_all x1 -> x2, blocking collectives: 25.8 us -> 26.9 us  [exchanged(): return lax.all_to_all(value, axis, 0, 0, tiled=True)]
    pallas_call x7 -> x6, Pallas kernels: 9.73 us -> 9.49 us  [call(): pl.pallas_call(kernel, out_shape=outs, in_specs=specs, out_specs=[WHOLE]...]
where the time goes in v7:
time: 160 us; the launch traced here: 159 us
  starting transfers between devices  89.6 us (56%)
  waiting for transfers between devices  29.3 us (18%)
  blocking collectives  26.9 us (17%)
  Pallas kernels  9.49 us (6%)
  local copies, waits for them, and re-layouts  2.09 us (1%)
    all_to_all x3, starting transfers between devices, exchanged(): return lax.all_to_all(value, axis, 0, 0, tiled=True)  31.2 us
    all_to_all x2, blocking collectives, exchanged(): return lax.all_to_all(value, axis, 0, 0, tiled=True)  26.9 us
    ppermute x7, starting transfers between devices, turned(): lax.ppermute(value, axis, [(i, (i + steps) % count) for i in range(count)])  25.3 us
    ppermute x4, starting transfers between devices, shifted(): lax.ppermute(value, DP, [(i, (i + steps) % count) for i in range(count)])  22.7 us
    all_to_all x3, waiting for transfers between devices, exchanged(): return lax.all_to_all(value, axis, 0, 0, tiled=True)  14.5 us
    ppermute x7, waiting for transfers between devices, turned(): lax.ppermute(value, axis, [(i, (i + steps) % count) for i in range(count)])  12.6 us
    ppermute x3, starting transfers between devices, swapped(): return lax.ppermute(value, GROUP, [(i, i ^ mask) for i in range(count)])  10.3 us
    pallas_call x6, Pallas kernels, call(): pl.pallas_call(kernel, out_shape=outs, in_specs=specs, out_specs=[WHOLE]...  9.49 us
  transfers between devices with their start and end apart: 17, of which 8 were waited for; matrix products, arithmetic and copies ran while one was open for 1% of the time, Pallas kernels for 5%

profile of v7, /device:TPU:1, one launch (start us, length us, event | category | flops | bytes accessed | tf_op | source)
XLA Modules:
  0.0 159.1 jit_solution(1489024761796437658)
XLA Ops:
  0.6 7.7 %all-to-all-start = ((bf16[8,16,1024]{2,1,0:T(8,128)(2,1)}), bf16[8,16,1024]{2,1,0:T(8,128)(2,1)S(1)}, u32[]{:S(2)}, u32[]{:S(2)}) async-start(bf16[8,16,1024]{2,1,0:T(8,128)(2,1)} %bitcast.14), calls=%async_computation | async-start | bytes 524288 | tf_op jit(solution)/shard_map/all_to_all | solution.py:43
  8.3 1.0 shard_map.111
  9.3 8.3 %all-to-all-done.layers_ref = bf16[8,16,1024]{2,1,0:T(8,128)(2,1)S(1)} async-done(((bf16[8,16,1024]{2,1,0:T(8,128)(2,1)}), bf16[8,16,1024]{2,1,0:T(8,128)(2,1)S(1)}, u32[]{:S(2)}, u32[]{:S(2)}) %all-to-all-start) | async-done | bytes 262176 | tf_op jit(solution)/shard_map/all_to_all | solution.py:43
  17.7 13.0 %all_to_all.25 = bf16[8,16,1024]{2,1,0:T(8,128)(2,1)S(1)} all-to-all(bf16[8,16,1024]{2,1,0:T(8,128)(2,1)S(1)} %shard_map.112), channel_id=1, replica_groups=mesh['section'=8,'zh'=8,'zl'=2,'core'=2,'tensor'=4] {'section'}, dimensions={0} | all-to-all | bytes 524288 | tf_op jit(solution)/shard_map/all_to_all | solution.py:43
  30.8 13.9 %all_to_all.26.grad_ref = bf16[4,128,1024]{2,1,0:T(8,128)(2,1)S(1)} all-to-all(bf16[4,128,1024]{2,1,0:T(8,128)(2,1)S(1)} %broadcast_in_dim.20), channel_id=1, replica_groups=mesh['section'=8,'zh'=8,'zl'=2,'core'=2,'tensor'=4] {'tensor'}, dimensions={0} | all-to-all | bytes 2097152 | tf_op jit(solution)/shard_map/all_to_all | solution.py:43
  45.5 20.1 %all-to-all-start.3 = ((bf16[8,4,32,128]{3,2,1,0:T(8,128)(2,1)}), bf16[8,4,32,128]{3,2,1,0:T(8,128)(2,1)S(1)}, u32[]{:S(2)}, u32[]{:S(2)}) async-start(bf16[8,4,32,128]{3,2,1,0:T(8,128)(2,1)} %bitcast.5), calls=%async_computation.3 | async-start | bytes 524288 | tf_op jit(solution)/shard_map/all_to_all | solution.py:43
  65.5 6.1 %collective-permute-start = (bf16[2,128,512]{2,1,0:T(8,128)(2,1)S(1)}, bf16[2,128,512]{2,1,0:T(8,128)(2,1)S(1)}, u32[]{:S(2)}, u32[]{:S(2)}) collective-permute-start(bf16[2,128,512]{2,1,0:T(8,128)(2,1)S(1)} %get-tuple-element.15.own_ref), channel_id=1, source_target_pairs={{0,4},{4,8},{8,12},{12,16},{16,20},{20,24},{24,28},{28,32},{32,36}... | collective-permute-start | bytes 786440 | tf_op jit(solution)/shard_map/ppermute | solution.py:29
  71.6 3.6 %collective-permute-start.1 = (bf16[2,128,512]{2,1,0:T(8,128)(2,1)S(1)}, bf16[2,128,512]{2,1,0:T(8,128)(2,1)S(1)}, u32[]{:S(2)}, u32[]{:S(2)}) collective-permute-start(bf16[2,128,512]{2,1,0:T(8,128)(2,1)S(1)} %get-tuple-element.15.own_ref), channel_id=1, source_target_pairs={{0,8},{4,12},{8,16},{12,20},{16,24},{20,28},{24,32},{28,36},{32,40... | collective-permute-start | bytes 786440 | tf_op jit(solution)/shard_map/ppermute | solution.py:29
  75.3 6.2 %all-to-all-done.3 = bf16[8,4,32,128]{3,2,1,0:T(8,128)(2,1)S(1)} async-done(((bf16[8,4,32,128]{3,2,1,0:T(8,128)(2,1)}), bf16[8,4,32,128]{3,2,1,0:T(8,128)(2,1)S(1)}, u32[]{:S(2)}, u32[]{:S(2)}) %all-to-all-start.3) | async-done | bytes 262176 | tf_op jit(solution)/shard_map/all_to_all | solution.py:43
  81.4 1.2 broadcast_in_dim.22
  82.7 3.5 %all-to-all-start.4 = ((bf16[4,8,4,32,128]{4,3,2,1,0:T(8,128)(2,1)}), bf16[4,8,4,32,128]{4,3,2,1,0:T(8,128)(2,1)S(1)}, u32[]{:S(2)}, u32[]{:S(2)}) async-start(bf16[4,8,4,32,128]{4,3,2,1,0:T(8,128)(2,1)} %broadcast_in_dim.22), calls=%async_computation.4 | async-start | bytes 2097152 | tf_op jit(solution)/shard_map/all_to_all | solution.py:43
  86.2 2.9 %collective-permute-start.4 = (bf16[128,512]{1,0:T(8,128)(2,1)S(1)}, bf16[128,512]{1,0:T(8,128)(2,1)S(1)}, u32[]{:S(2)}, u32[]{:S(2)}) collective-permute-start(bf16[128,512]{1,0:T(8,128)(2,1)S(1)} %bitcast.9), channel_id=1, source_target_pairs={{0,16},{16,32},{32,48},{48,64},{64,80},{80,96},{96,112},{112,0},{1... | collective-permute-start | bytes 393224 | tf_op jit(solution)/shard_map/ppermute | solution.py:34
  89.1 4.5 %collective-permute-start.5 = (bf16[128,512]{1,0:T(8,128)(2,1)S(1)}, bf16[128,512]{1,0:T(8,128)(2,1)S(1)}, u32[]{:S(2)}, u32[]{:S(2)}) collective-permute-start(bf16[128,512]{1,0:T(8,128)(2,1)S(1)} %bitcast.10), channel_id=1, source_target_pairs={{0,112},{16,0},{32,16},{48,32},{64,48},{80,64},{96,80},{112,96},{1... | collective-permute-start | bytes 393224 | tf_op jit(solution)/shard_map/ppermute | solution.py:34
  93.6 1.8 %collective-permute-done.4.refs_1_ = bf16[128,512]{1,0:T(8,128)(2,1)S(1)} collective-permute-done((bf16[128,512]{1,0:T(8,128)(2,1)S(1)}, bf16[128,512]{1,0:T(8,128)(2,1)S(1)}, u32[]{:S(2)}, u32[]{:S(2)}) %collective-permute-start.4) | collective-permute-done | bytes 131104 | tf_op jit(solution)/shard_map/ppermute | solution.py:34
  95.4 1.9 %collective-permute-start.6 = (bf16[128,512]{1,0:T(8,128)(2,1)S(1)}, bf16[128,512]{1,0:T(8,128)(2,1)S(1)}, u32[]{:S(2)}, u32[]{:S(2)}) collective-permute-start(bf16[128,512]{1,0:T(8,128)(2,1)S(1)} %collective-permute-done.4.refs_1_), channel_id=1, source_target_pairs={{0,16},{16,32},{32,48},{48,64},{64,80},{80,96},{96,112},{112,0},{1... | collective-permute-start | bytes 393224 | tf_op jit(solution)/shard_map/ppermute | solution.py:34
  97.4 1.7 %shard_map.113.prob_ref = f32[4,128,384]{2,1,0:T(8,128)S(1)} custom-call(s32[32]{0:T(128)} %lengths_hbm.1, bf16[1,128,512]{2,1,0:T(8,128)(2,1)} %query_hbm.1, bf16[2,128,512]{2,1,0:T(8,128)(2,1)S(1)} %get-tuple-element.15.own_ref, bf16[2,128,512]{2,1,0:T(8,128)(2,1)S(1)} %collective-permute-done.near_ref, bf16[2,128,512]{2,1,0:T(8,128)(2,1)S(1)} %collective-permute-done.1.far_ref), custom_call_target="tpu_custom_call" | custom-call | flops 52297728 | bytes 1572864 | tf_op jit(solution)/shard_map/pallas_call | solution.py:204
  99.1 5.2 %shard_map.114 = (bf16[128,512]{1,0:T(8,128)(2,1)}, f32[2,128,512]{2,1,0:T(8,128)S(1)}, bf16[2,128,512]{2,1,0:T(8,128)(2,1)S(1)}, bf16[2,128,512]{2,1,0:T(8,128)(2,1)S(1)}) custom-call(bf16[4,128,1024]{2,1,0:T(8,128)(2,1)S(1)} %all_to_all.26.grad_ref, bf16[1,4096,512]{2,1,0:T(8,128)(2,1)} %weight_hbm.1, f32[4,128,384]{2,1,0:T(8,128)S(1)} %shard_map.113.prob_ref, ...), custom_call_target="tpu_custom_call" | custom-call | flops 738197504 | bytes 4194304 | tf_op jit(solution)/shard_map/pallas_call | solution.py:204
  104.3 3.2 %collective-permute-start.3 = (bf16[2,128,512]{2,1,0:T(8,128)(2,1)S(1)}, bf16[2,128,512]{2,1,0:T(8,128)(2,1)S(1)}, u32[]{:S(2)}, u32[]{:S(2)}) collective-permute-start(bf16[2,128,512]{2,1,0:T(8,128)(2,1)S(1)} %get-tuple-element.19), channel_id=1, source_target_pairs={{0,120},{4,124},{8,0},{12,4},{16,8},{20,12},{24,16},{28,20},{32,24... | collective-permute-start | bytes 786440 | tf_op jit(solution)/shard_map/ppermute | solution.py:29
  107.5 9.8 %collective-permute-start.2 = (bf16[2,128,512]{2,1,0:T(8,128)(2,1)S(1)}, bf16[2,128,512]{2,1,0:T(8,128)(2,1)S(1)}, u32[]{:S(2)}, u32[]{:S(2)}) collective-permute-start(bf16[2,128,512]{2,1,0:T(8,128)(2,1)S(1)} %get-tuple-element.18), channel_id=1, source_target_pairs={{0,124},{4,0},{8,4},{12,8},{16,12},{20,16},{24,20},{28,24},{32,28}... | collective-permute-start | bytes 786440 | tf_op jit(solution)/shard_map/ppermute | solution.py:29
  117.3 5.5 %collective-permute-start.7 = (bf16[128,512]{1,0:T(8,128)(2,1)S(1)}, bf16[128,512]{1,0:T(8,128)(2,1)S(1)}, u32[]{:S(2)}, u32[]{:S(2)}) collective-permute-start(bf16[128,512]{1,0:T(8,128)(2,1)S(1)} %collective-permute-done.5.refs_2_), channel_id=1, source_target_pairs={{0,112},{16,0},{32,16},{48,32},{64,48},{80,64},{96,80},{112,96},{1... | collective-permute-start | bytes 393224 | tf_op jit(solution)/shard_map/ppermute | solution.py:34
  122.8 1.9 %collective-permute-start.8 = (bf16[128,512]{1,0:T(8,128)(2,1)S(1)}, bf16[128,512]{1,0:T(8,128)(2,1)S(1)}, u32[]{:S(2)}, u32[]{:S(2)}) collective-permute-start(bf16[128,512]{1,0:T(8,128)(2,1)S(1)} %collective-permute-done.6.refs_3_), channel_id=1, source_target_pairs={{0,16},{16,32},{32,48},{48,64},{64,80},{80,96},{96,112},{112,0},{1... | collective-permute-start | bytes 393224 | tf_op jit(solution)/shard_map/ppermute | solution.py:34
  124.7 1.9 %collective-permute-done.7.refs_4_ = bf16[128,512]{1,0:T(8,128)(2,1)S(1)} collective-permute-done((bf16[128,512]{1,0:T(8,128)(2,1)S(1)}, bf16[128,512]{1,0:T(8,128)(2,1)S(1)}, u32[]{:S(2)}, u32[]{:S(2)}) %collective-permute-start.7) | collective-permute-done | bytes 131104 | tf_op jit(solution)/shard_map/ppermute | solution.py:34
  126.6 6.7 %collective-permute-start.9 = (bf16[128,512]{1,0:T(8,128)(2,1)S(1)}, bf16[128,512]{1,0:T(8,128)(2,1)S(1)}, u32[]{:S(2)}, u32[]{:S(2)}) collective-permute-start(bf16[128,512]{1,0:T(8,128)(2,1)S(1)} %collective-permute-done.7.refs_4_), channel_id=1, source_target_pairs={{0,112},{16,0},{32,16},{48,32},{64,48},{80,64},{96,80},{112,96},{1... | collective-permute-start | bytes 393224 | tf_op jit(solution)/shard_map/ppermute | solution.py:34
  133.6 1.9 %collective-permute-start.10 = (bf16[128,512]{1,0:T(8,128)(2,1)S(1)}, bf16[128,512]{1,0:T(8,128)(2,1)S(1)}, u32[]{:S(2)}, u32[]{:S(2)}) collective-permute-start(bf16[128,512]{1,0:T(8,128)(2,1)S(1)} %collective-permute-done.8.refs_5_), channel_id=1, source_target_pairs={{0,16},{16,32},{32,48},{48,64},{64,80},{80,96},{96,112},{112,0},{1... | collective-permute-start | bytes 393224 | tf_op jit(solution)/shard_map/ppermute | solution.py:34
  135.7 1.8 %collective-permute-done.9.refs_6_ = bf16[128,512]{1,0:T(8,128)(2,1)S(1)} collective-permute-done((bf16[128,512]{1,0:T(8,128)(2,1)S(1)}, bf16[128,512]{1,0:T(8,128)(2,1)S(1)}, u32[]{:S(2)}, u32[]{:S(2)}) %collective-permute-start.9) | collective-permute-done | bytes 131104 | tf_op jit(solution)/shard_map/ppermute | solution.py:34
  137.5 6.8 %collective-permute-done.10.refs_7_ = bf16[128,512]{1,0:T(8,128)(2,1)S(1)} collective-permute-done((bf16[128,512]{1,0:T(8,128)(2,1)S(1)}, bf16[128,512]{1,0:T(8,128)(2,1)S(1)}, u32[]{:S(2)}, u32[]{:S(2)}) %collective-permute-start.10) | collective-permute-done | bytes 131104 | tf_op jit(solution)/shard_map/ppermute | solution.py:34
  144.3 0.8 shard_map.116
  145.0 6.1 %collective-permute-start.13 = (bf16[128,512]{1,0:T(8,128)(2,1)S(1)}, bf16[128,512]{1,0:T(8,128)(2,1)S(1)}, u32[]{:S(2)}, u32[]{:S(2)}) collective-permute-start(bf16[128,512]{1,0:T(8,128)(2,1)S(1)} %get-tuple-element.23), channel_id=1, source_target_pairs={{0,12},{4,8},{8,4},{12,0},{1,13},{5,9},{9,5},{13,1},{2,14},{6,10},... | collective-permute-start | bytes 393224 | tf_op jit(solution)/shard_map/ppermute | solution.py:39
  151.2 1.9 %collective-permute-start.12 = (bf16[128,512]{1,0:T(8,128)(2,1)S(1)}, bf16[128,512]{1,0:T(8,128)(2,1)S(1)}, u32[]{:S(2)}, u32[]{:S(2)}) collective-permute-start(bf16[128,512]{1,0:T(8,128)(2,1)S(1)} %get-tuple-element.22), channel_id=1, source_target_pairs={{0,8},{4,12},{8,0},{12,4},{1,9},{5,13},{9,1},{13,5},{2,10},{6,14},... | collective-permute-start | bytes 393224 | tf_op jit(solution)/shard_map/ppermute | solution.py:39
  153.1 2.3 %collective-permute-start.11 = (bf16[128,512]{1,0:T(8,128)(2,1)S(1)}, bf16[128,512]{1,0:T(8,128)(2,1)S(1)}, u32[]{:S(2)}, u32[]{:S(2)}) collective-permute-start(bf16[128,512]{1,0:T(8,128)(2,1)S(1)} %get-tuple-element.21), channel_id=1, source_target_pairs={{0,4},{4,0},{8,12},{12,8},{1,5},{5,1},{9,13},{13,9},{2,6},{6,2},{1... | collective-permute-start | bytes 393224 | tf_op jit(solution)/shard_map/ppermute | solution.py:39
  156.1 2.2 %collective-permute-done.12 = bf16[128,512]{1,0:T(8,128)(2,1)S(1)} collective-permute-done((bf16[128,512]{1,0:T(8,128)(2,1)S(1)}, bf16[128,512]{1,0:T(8,128)(2,1)S(1)}, u32[]{:S(2)}, u32[]{:S(2)}) %collective-permute-start.12) | collective-permute-done | bytes 131104 | tf_op jit(solution)/shard_map/ppermute | solution.py:39
  158.3 0.8 add_bitcast_fusion
  (19 shorter events, 2.1 us)
Async XLA Ops:
  0.6 17.0 %all-to-all-start = ((bf16[8,16,1024]{2,1,0:T(8,128)(2,1)}), bf16[8,16,1024]{2,1,0:T(8,128)(2,1)S(1)}, u32[]{:S(2)}, u32[]{:S(2)}) async-start(bf16[8,16,1024]{2,1,0:T(8,128)(2,1)} %bitcast.14), calls=%async_computation | async-start | bytes 524288 | tf_op jit(solution)/shard_map/all_to_all | solution.py:43
  30.7 55.5 %copy-start.1 = (bf16[1,128,512]{2,1,0:T(8,128)(2,1)S(1)}, bf16[1,128,512]{2,1,0:T(8,128)(2,1)}, u32[]{:S(2)}) copy-start(bf16[1,128,512]{2,1,0:T(8,128)(2,1)} %param.10) | copy-start | bytes 393220
  30.8 68.3 %copy-start = (bf16[1,128,512]{2,1,0:T(8,128)(2,1)S(1)}, bf16[1,128,512]{2,1,0:T(8,128)(2,1)}, u32[]{:S(2)}) copy-start(bf16[1,128,512]{2,1,0:T(8,128)(2,1)} %query_hbm.1) | copy-start | bytes 393220
  45.5 35.9 %all-to-all-start.3 = ((bf16[8,4,32,128]{3,2,1,0:T(8,128)(2,1)}), bf16[8,4,32,128]{3,2,1,0:T(8,128)(2,1)S(1)}, u32[]{:S(2)}, u32[]{:S(2)}) async-start(bf16[8,4,32,128]{3,2,1,0:T(8,128)(2,1)} %bitcast.5), calls=%async_computation.3 | async-start | bytes 524288 | tf_op jit(solution)/shard_map/all_to_all | solution.py:43
  65.5 31.8 %collective-permute-start = (bf16[2,128,512]{2,1,0:T(8,128)(2,1)S(1)}, bf16[2,128,512]{2,1,0:T(8,128)(2,1)S(1)}, u32[]{:S(2)}, u32[]{:S(2)}) collective-permute-start(bf16[2,128,512]{2,1,0:T(8,128)(2,1)S(1)} %get-tuple-element.15.own_ref), channel_id=1, source_target_pairs={{0,4},{4,8},{8,12},{12,16},{16,20},{20,24},{24,28},{28,32},{32,36}... | collective-permute-start | bytes 786440 | tf_op jit(solution)/shard_map/ppermute | solution.py:29
  71.6 25.7 %collective-permute-start.1 = (bf16[2,128,512]{2,1,0:T(8,128)(2,1)S(1)}, bf16[2,128,512]{2,1,0:T(8,128)(2,1)S(1)}, u32[]{:S(2)}, u32[]{:S(2)}) collective-permute-start(bf16[2,128,512]{2,1,0:T(8,128)(2,1)S(1)} %get-tuple-element.15.own_ref), channel_id=1, source_target_pairs={{0,8},{4,12},{8,16},{12,20},{16,24},{20,28},{24,32},{28,36},{32,40... | collective-permute-start | bytes 786440 | tf_op jit(solution)/shard_map/ppermute | solution.py:29
  82.7 61.6 %all-to-all-start.4 = ((bf16[4,8,4,32,128]{4,3,2,1,0:T(8,128)(2,1)}), bf16[4,8,4,32,128]{4,3,2,1,0:T(8,128)(2,1)S(1)}, u32[]{:S(2)}, u32[]{:S(2)}) async-start(bf16[4,8,4,32,128]{4,3,2,1,0:T(8,128)(2,1)} %broadcast_in_dim.22), calls=%async_computation.4 | async-start | bytes 2097152 | tf_op jit(solution)/shard_map/all_to_all | solution.py:43
  86.2 9.2 %collective-permute-start.4 = (bf16[128,512]{1,0:T(8,128)(2,1)S(1)}, bf16[128,512]{1,0:T(8,128)(2,1)S(1)}, u32[]{:S(2)}, u32[]{:S(2)}) collective-permute-start(bf16[128,512]{1,0:T(8,128)(2,1)S(1)} %bitcast.9), channel_id=1, source_target_pairs={{0,16},{16,32},{32,48},{48,64},{64,80},{80,96},{96,112},{112,0},{1... | collective-permute-start | bytes 393224 | tf_op jit(solution)/shard_map/ppermute | solution.py:34
  89.1 28.2 %collective-permute-start.5 = (bf16[128,512]{1,0:T(8,128)(2,1)S(1)}, bf16[128,512]{1,0:T(8,128)(2,1)S(1)}, u32[]{:S(2)}, u32[]{:S(2)}) collective-permute-start(bf16[128,512]{1,0:T(8,128)(2,1)S(1)} %bitcast.10), channel_id=1, source_target_pairs={{0,112},{16,0},{32,16},{48,32},{64,48},{80,64},{96,80},{112,96},{1... | collective-permute-start | bytes 393224 | tf_op jit(solution)/shard_map/ppermute | solution.py:34
  95.4 27.3 %collective-permute-start.6 = (bf16[128,512]{1,0:T(8,128)(2,1)S(1)}, bf16[128,512]{1,0:T(8,128)(2,1)S(1)}, u32[]{:S(2)}, u32[]{:S(2)}) collective-permute-start(bf16[128,512]{1,0:T(8,128)(2,1)S(1)} %collective-permute-done.4.refs_1_), channel_id=1, source_target_pairs={{0,16},{16,32},{32,48},{48,64},{64,80},{80,96},{96,112},{112,0},{1... | collective-permute-start | bytes 393224 | tf_op jit(solution)/shard_map/ppermute | solution.py:34
  104.3 31.2 %collective-permute-start.3 = (bf16[2,128,512]{2,1,0:T(8,128)(2,1)S(1)}, bf16[2,128,512]{2,1,0:T(8,128)(2,1)S(1)}, u32[]{:S(2)}, u32[]{:S(2)}) collective-permute-start(bf16[2,128,512]{2,1,0:T(8,128)(2,1)S(1)} %get-tuple-element.19), channel_id=1, source_target_pairs={{0,120},{4,124},{8,0},{12,4},{16,8},{20,12},{24,16},{28,20},{32,24... | collective-permute-start | bytes 786440 | tf_op jit(solution)/shard_map/ppermute | solution.py:29
  107.5 28.0 %collective-permute-start.2 = (bf16[2,128,512]{2,1,0:T(8,128)(2,1)S(1)}, bf16[2,128,512]{2,1,0:T(8,128)(2,1)S(1)}, u32[]{:S(2)}, u32[]{:S(2)}) collective-permute-start(bf16[2,128,512]{2,1,0:T(8,128)(2,1)S(1)} %get-tuple-element.18), channel_id=1, source_target_pairs={{0,124},{4,0},{8,4},{12,8},{16,12},{20,16},{24,20},{28,24},{32,28}... | collective-permute-start | bytes 786440 | tf_op jit(solution)/shard_map/ppermute | solution.py:29
  117.3 9.3 %collective-permute-start.7 = (bf16[128,512]{1,0:T(8,128)(2,1)S(1)}, bf16[128,512]{1,0:T(8,128)(2,1)S(1)}, u32[]{:S(2)}, u32[]{:S(2)}) collective-permute-start(bf16[128,512]{1,0:T(8,128)(2,1)S(1)} %collective-permute-done.5.refs_2_), channel_id=1, source_target_pairs={{0,112},{16,0},{32,16},{48,32},{64,48},{80,64},{96,80},{112,96},{1... | collective-permute-start | bytes 393224 | tf_op jit(solution)/shard_map/ppermute | solution.py:34
  122.8 10.8 %collective-permute-start.8 = (bf16[128,512]{1,0:T(8,128)(2,1)S(1)}, bf16[128,512]{1,0:T(8,128)(2,1)S(1)}, u32[]{:S(2)}, u32[]{:S(2)}) collective-permute-start(bf16[128,512]{1,0:T(8,128)(2,1)S(1)} %collective-permute-done.6.refs_3_), channel_id=1, source_target_pairs={{0,16},{16,32},{32,48},{48,64},{64,80},{80,96},{96,112},{112,0},{1... | collective-permute-start | bytes 393224 | tf_op jit(solution)/shard_map/ppermute | solution.py:34
  126.6 10.9 %collective-permute-start.9 = (bf16[128,512]{1,0:T(8,128)(2,1)S(1)}, bf16[128,512]{1,0:T(8,128)(2,1)S(1)}, u32[]{:S(2)}, u32[]{:S(2)}) collective-permute-start(bf16[128,512]{1,0:T(8,128)(2,1)S(1)} %collective-permute-done.7.refs_4_), channel_id=1, source_target_pairs={{0,112},{16,0},{32,16},{48,32},{64,48},{80,64},{96,80},{112,96},{1... | collective-permute-start | bytes 393224 | tf_op jit(solution)/shard_map/ppermute | solution.py:34
  133.6 10.6 %collective-permute-start.10 = (bf16[128,512]{1,0:T(8,128)(2,1)S(1)}, bf16[128,512]{1,0:T(8,128)(2,1)S(1)}, u32[]{:S(2)}, u32[]{:S(2)}) collective-permute-start(bf16[128,512]{1,0:T(8,128)(2,1)S(1)} %collective-permute-done.8.refs_5_), channel_id=1, source_target_pairs={{0,16},{16,32},{32,48},{48,64},{64,80},{80,96},{96,112},{112,0},{1... | collective-permute-start | bytes 393224 | tf_op jit(solution)/shard_map/ppermute | solution.py:34
  145.0 11.1 %collective-permute-start.13 = (bf16[128,512]{1,0:T(8,128)(2,1)S(1)}, bf16[128,512]{1,0:T(8,128)(2,1)S(1)}, u32[]{:S(2)}, u32[]{:S(2)}) collective-permute-start(bf16[128,512]{1,0:T(8,128)(2,1)S(1)} %get-tuple-element.23), channel_id=1, source_target_pairs={{0,12},{4,8},{8,4},{12,0},{1,13},{5,9},{9,5},{13,1},{2,14},{6,10},... | collective-permute-start | bytes 393224 | tf_op jit(solution)/shard_map/ppermute | solution.py:39
  151.2 7.2 %collective-permute-start.12 = (bf16[128,512]{1,0:T(8,128)(2,1)S(1)}, bf16[128,512]{1,0:T(8,128)(2,1)S(1)}, u32[]{:S(2)}, u32[]{:S(2)}) collective-permute-start(bf16[128,512]{1,0:T(8,128)(2,1)S(1)} %get-tuple-element.22), channel_id=1, source_target_pairs={{0,8},{4,12},{8,0},{12,4},{1,9},{5,13},{9,1},{13,5},{2,10},{6,14},... | collective-permute-start | bytes 393224 | tf_op jit(solution)/shard_map/ppermute | solution.py:39
  153.1 5.2 %collective-permute-start.11 = (bf16[128,512]{1,0:T(8,128)(2,1)S(1)}, bf16[128,512]{1,0:T(8,128)(2,1)S(1)}, u32[]{:S(2)}, u32[]{:S(2)}) collective-permute-start(bf16[128,512]{1,0:T(8,128)(2,1)S(1)} %get-tuple-element.21), channel_id=1, source_target_pairs={{0,4},{4,0},{8,12},{12,8},{1,5},{5,1},{9,13},{13,9},{2,6},{6,2},{1... | collective-permute-start | bytes 393224 | tf_op jit(solution)/shard_map/ppermute | solution.py:39
